TPU v7x, 32 devices: a whole 2x2x4 slice. The times are simulated.
32 devices in a mesh: grp: 4 (over z), seq: 8 (over y, x, core).
Axes of the slice: x: 2, y: 2, z: 4, core: 2. Of those that a mesh axis runs over, the one named last changes fastest.
Arguments:
- mixer_input: bfloat16 [8192, 1024], P(('grp', 'seq')), may hold values from -6 to 6
- write_proj: bfloat16 [8192, 128], P(('grp', 'seq')), may hold values from -0.29882812 to 0.29882812
- read_proj: bfloat16 [8192, 128], P(('grp', 'seq')), may hold values from -0.29882812 to 0.29882812
- log_decay: float32 [8192, 16], P(('grp', 'seq')), may hold values from -2 to 0
- resid: bfloat16 [8192, 1024], P(('grp', 'seq')), may hold values from -134 to 134
- out_grad: bfloat16 [8192, 1024], P(('grp', 'seq')), may hold values from -6 to 6
- gate_probs: float32 [8192, 2], P(('grp', 'seq')), may hold values from 0.1 to 0.9
- expert_ids: int32 [8192, 2], P(('grp', 'seq')), may hold values from 0 to 31, as said below
- expert_up: bfloat16 [32, 1024, 1024], P(('grp', 'seq')), may hold values from -0.1875 to 0.1875
- expert_down: bfloat16 [32, 1024, 1024], P(('grp', 'seq')), may hold values from -0.1875 to 0.1875
Outputs:
- input_grad: bfloat16 [8192, 1024], P(('grp', 'seq'))
- write_grad: float32 [8192, 128], P(('grp', 'seq'))
- read_grad: float32 [8192, 128], P(('grp', 'seq'))
- decay_grad: float32 [8192, 16], P(('grp', 'seq'))
- resid_grad: bfloat16 [8192, 1024], P(('grp', 'seq'))
- gate_grad: bfloat16 [8192, 2], P(('grp', 'seq'))
- up_grad: bfloat16 [32, 1024, 1024], P(('grp', 'seq'))
- down_grad: bfloat16 [32, 1024, 1024], P(('grp', 'seq'))
Inputs may be any that keep to these rules, and one draw needn't show every extreme that they name: `expert_ids`: each row names two different experts; among the 256 rows of one device no expert is named more than 32 times.
All inputs are finite; a program needn't handle non-finite values.
Results may differ from a plain program's by a relative error of at most 0.0072.
Values may be sent and summed in bfloat16 or wider, within the bound.
No kernel may reach another device: no remote copies, remote signals or barrier semaphores. Data moves between devices by JAX's collectives and lax.ppermute only.
A program may use at most 192 MiB of HBM per device.

v0:
```python
import functools

import jax
import jax.numpy as jnp
from jax import lax
from jax.experimental import pallas as pl
from jax.experimental.pallas import tpu as pltpu
from jax.sharding import PartitionSpec as P

EPSILON = 1e-06
HIGHEST = lax.Precision.HIGHEST
F32 = jnp.float32
BF16 = jnp.bfloat16
VMEM_LIMIT = 60 * 1024 * 1024


def iota(shape, axis):
    return lax.broadcasted_iota(jnp.int32, shape, axis)


def dot(a, b, ca, cb, precision=None):
    return lax.dot_general(
        a, b, (((ca,), (cb,)), ((), ())), precision=precision, preferred_element_type=F32
    )


def call(kernel, outs, *args, grid=None, in_specs=None, out_specs=None, scratch=(), cost=None):
    whole = pl.BlockSpec(memory_space=pltpu.VMEM)
    many = isinstance(outs, (tuple, list))
    kwargs = {}
    if grid is not None:
        kwargs["grid"] = grid
    return pl.pallas_call(
        kernel,
        out_shape=outs,
        in_specs=in_specs if in_specs is not None else [whole] * len(args),
        out_specs=out_specs
        if out_specs is not None
        else (tuple([whole] * len(outs)) if many else whole),
        scratch_shapes=list(scratch),
        compiler_params=pltpu.CompilerParams(vmem_limit_bytes=VMEM_LIMIT),
        cost_estimate=cost,
        **kwargs,
    )(*args)


def shape(dims, dtype):
    return jax.ShapeDtypeStruct(dims, dtype)


def one_hot(targets, slots):
    slot = iota((slots, targets.shape[1]), 0)
    first = slot == targets[0:1, :]
    second = slot == targets[1:2, :]
    return first, second


def rows_kernel(experts, cap, resid_ref, ids_ref, rows_ref, targets_ref):
    resid = resid_ref[...].astype(F32)
    inverse = lax.rsqrt(jnp.mean(resid * resid, axis=1, keepdims=True) + EPSILON)
    normed_b = (resid * inverse).astype(BF16)
    ids = ids_ref[...]
    tokens = ids.shape[1]
    number = iota((experts, tokens), 0)
    first = (number == ids[0:1, :]).astype(F32)
    second = (number == ids[1:2, :]).astype(F32)
    earlier = (iota((tokens, tokens), 0) < iota((tokens, tokens), 1)).astype(BF16)
    before = dot((first + second).astype(BF16), earlier, 1, 0)
    rank0 = jnp.sum(before * first, axis=0, keepdims=True).astype(jnp.int32)
    rank1 = jnp.sum(before * second, axis=0, keepdims=True).astype(jnp.int32)
    targets = jnp.concatenate([ids[0:1, :] * cap + rank0, ids[1:2, :] * cap + rank1], axis=0)
    targets_ref[...] = targets
    hit0, hit1 = one_hot(targets, experts * cap)
    select = jnp.where(hit0 | hit1, 1.0, 0.0).astype(BF16)
    rows_ref[...] = dot(select, normed_b, 1, 0).astype(BF16)


def grads_kernel(out_grad_ref, gates_ref, targets_ref, rows_ref):
    slots = rows_ref.shape[0]
    hit0, hit1 = one_hot(targets_ref[...], slots)
    gates = gates_ref[...].astype(BF16).astype(F32)
    select = jnp.where(hit0, gates[0:1, :], 0.0) + jnp.where(hit1, gates[1:2, :], 0.0)
    rows_ref[...] = dot(select.astype(BF16), out_grad_ref[...], 1, 0).astype(BF16)


def expert_kernel(scaled_ref, act_ref, slope_ref, up_ref, down_ref, pre_ref, row_ref, term_ref):
    act_grad = dot(scaled_ref[...], down_ref[...], 1, 1)
    pre = (act_grad * slope_ref[...]).astype(BF16)
    pre_ref[...] = pre
    row_ref[...] = dot(pre, up_ref[...], 1, 1).astype(BF16)
    prod = act_grad * act_ref[...].astype(F32)
    high = prod.astype(BF16)
    low = (prod - high.astype(F32)).astype(BF16)
    ones = jnp.ones((8, prod.shape[1]), BF16)
    term_ref[...] = (dot(ones, high, 1, 1) + dot(ones, low, 1, 1))[None]


def expert_stage(scaled, act, slope, up, down):
    rows, width = scaled.shape
    hidden = act.shape[1]
    tile = min(256, rows)
    steps = rows // tile
    by_rows = lambda w: pl.BlockSpec((tile, w), lambda i: (i, 0))
    whole = pl.BlockSpec(memory_space=pltpu.VMEM)
    pre, row_grad, term = call(
        expert_kernel,
        (shape((rows, hidden), BF16), shape((rows, width), BF16), shape((steps, 8, tile), F32)),
        scaled,
        act,
        slope,
        up,
        down,
        grid=(steps,),
        in_specs=[by_rows(width), by_rows(hidden), by_rows(hidden), whole, whole],
        out_specs=(by_rows(hidden), by_rows(width), pl.BlockSpec((1, 8, tile), lambda i: (i, 0, 0))),
        cost=pl.CostEstimate(
            flops=4 * rows * width * hidden, bytes_accessed=20 * rows * width, transcendentals=0
        ),
    )
    return pre, row_grad, term[:, 0, :].reshape(-1)


def gate_kernel(terms_ref, targets_ref, gates_ref, out_ref):
    slots = terms_ref.shape[1]
    hit0, hit1 = one_hot(targets_ref[...], slots)
    terms = terms_ref[...]
    gates = gates_ref[...].astype(BF16).astype(F32)
    first = dot(terms, jnp.where(hit0, 1.0, 0.0).astype(BF16), 1, 0)
    second = dot(terms, jnp.where(hit1, 1.0, 0.0).astype(BF16), 1, 0)
    out_ref[...] = jnp.concatenate([first[0:1, :], second[0:1, :]], axis=0) / gates


def spread(heads, width):
    return (iota((heads, width), 1) // (width // heads) == iota((heads, width), 0)).astype(F32)


def ends_kernel(inputs_ref, writes_ref, decays_ref, cum_ref, cumt_ref, send_ref):
    decays = decays_ref[...]
    tokens, heads = decays.shape
    parts, padded, width = send_ref.shape
    upto = (iota((tokens, tokens), 0) >= iota((tokens, tokens), 1)).astype(F32)
    cum = dot(upto, decays, 1, 0, HIGHEST)
    cum_ref[...] = cum
    cumt_ref[...] = dot(decays, upto, 0, 1, HIGHEST)
    total = cum[tokens - 1 : tokens, :]
    wide = spread(heads, width)
    remaining = dot(jnp.exp(total - cum), wide, 1, 0, HIGHEST)
    scaled = (inputs_ref[...].astype(F32) * remaining).astype(BF16)
    ends = dot(writes_ref[...], scaled, 0, 0)
    kept = dot(jnp.exp(jnp.broadcast_to(total, (8, heads))), wide, 1, 0, HIGHEST)[0:1, :]
    high = kept.astype(BF16)
    low = (kept - high.astype(F32)).astype(BF16)
    rows = ends.shape[0] // parts
    for part in range(parts):
        send_ref[part, 0:rows, :] = ends[part * rows : (part + 1) * rows, :].astype(BF16)
        send_ref[part, rows : rows + 1, :] = high
        send_ref[part, rows + 1 : rows + 2, :] = low
        send_ref[part, rows + 2 :, :] = jnp.zeros((padded - rows - 2, width), BF16)


def scan_kernel(reverse, ends_ref, kept_ref, out_ref):
    parts, rows, _ = out_ref.shape
    state = jnp.zeros(out_ref.shape[1:], F32)
    for step in range(parts):
        at = parts - 1 - step if reverse else step
        out_ref[at] = state.astype(BF16)
        kept = kept_ref[at, rows : rows + 1, :].astype(F32) + kept_ref[
            at, rows + 1 : rows + 2, :
        ].astype(F32)
        state = state * kept + ends_ref[at, 0:rows, :].astype(F32)


def home_kernel(
    back_ref, targets_ref, resid_ref, out_grad_ref, reads_ref, cum_ref, grad_ref, adjoint_ref
):
    slots, width = back_ref.shape
    heads = cum_ref.shape[1]
    hit0, hit1 = one_hot(targets_ref[...], slots)
    select = jnp.where(hit0 | hit1, 1.0, 0.0).astype(BF16)
    d_normed = dot(select, back_ref[...], 0, 0)
    resid = resid_ref[...].astype(F32)
    inverse = lax.rsqrt(jnp.mean(resid * resid, axis=1, keepdims=True) + EPSILON)
    normed = resid * inverse
    mean = jnp.mean(d_normed * normed, axis=1, keepdims=True)
    grad = (out_grad_ref[...].astype(F32) + inverse * (d_normed - normed * mean)).astype(BF16)
    grad_ref[...] = grad
    grown = dot(jnp.exp(cum_ref[...]), spread(heads, width), 1, 0, HIGHEST)
    scaled = (grad.astype(F32) * grown).astype(BF16)
    adjoint_ref[...] = dot(reads_ref[...], scaled, 0, 0).astype(BF16)


def inside_kernel(
    inputs_ref,
    grads_ref,
    writes_ref,
    reads_ref,
    state_ref,
    cum_ref,
    cumt_ref,
    dx_ref,
    dwrite_ref,
    dread_ref,
    dcum_ref,
    dcumt_ref,
    score_ref,
    total_ref,
):
    step = pl.program_id(0)
    steps = pl.num_programs(0)
    tokens, lanes = inputs_ref.shape
    each = cumt_ref.shape[0]
    size = lanes // each

    @pl.when(step == 0)
    def _():
        score_ref[...] = dot(reads_ref[...], writes_ref[...], 1, 1)
        total_ref[...] = jnp.zeros_like(total_ref)
        dread_ref[...] = jnp.zeros_like(dread_ref)
        dcum_ref[...] = jnp.zeros_like(dcum_ref)

    inputs = inputs_ref[...]
    grads = grads_ref[...]
    cum = cum_ref[...]
    scores = score_ref[...]
    causal = iota((tokens, tokens), 0) >= iota((tokens, tokens), 1)
    column = iota(cum.shape, 1)
    lane = iota((tokens, lanes), 1) // size
    dx = jnp.zeros((tokens, lanes), F32)
    sums = jnp.zeros(cum.shape, F32)
    grown = jnp.zeros((tokens, lanes), F32)
    state = state_ref[...]
    read_state = dot(reads_ref[...], state, 1, 0)
    inter = grads.astype(F32) * read_state
    total = jnp.zeros((tokens, tokens), F32)
    for k in range(each):
        head = step * each + k
        at_t = jnp.sum(jnp.where(column == head, cum, 0.0), axis=1, keepdims=True)
        at_s = cumt_ref[k]
        decay = jnp.exp(jnp.where(causal, at_t - at_s, -1e30))
        mine = lane == k
        grads_k = jnp.where(mine, grads, jnp.zeros_like(grads))
        weights = dot(grads_k, inputs, 1, 1) * decay
        total = total + weights
        dx = dx + dot((decay * scores).astype(BF16), grads_k, 0, 0)
        both = weights * scores
        grow = jnp.exp(at_t)
        row = jnp.sum(both, axis=1, keepdims=True) + grow * jnp.sum(
            jnp.where(mine, inter, 0.0), axis=1, keepdims=True
        )
        sums = sums + jnp.where(column == head, row, 0.0)
        dcumt_ref[k] = jnp.sum(both, axis=0, keepdims=True)
        grown = grown + jnp.where(mine, grow, 0.0)
    total_ref[...] += total
    dcum_ref[...] += sums
    dx_ref[...] = dx
    dread_ref[...] += dot((grown * grads.astype(F32)).astype(BF16), state, 1, 1)

    @pl.when(step == steps - 1)
    def _():
        total_b = total_ref[...].astype(BF16)
        dread_ref[...] += dot(total_b, writes_ref[...], 1, 0)
        dwrite_ref[...] = dot(total_b, reads_ref[...], 0, 0)


def inside_stage(inputs, grads, writes, reads, state, cum, cumt):
    tokens, width = inputs.shape
    heads = cum.shape[1]
    n = writes.shape[1]
    lanes = max(128, width // heads)
    steps = width // lanes
    each = heads // steps
    part = pl.BlockSpec((tokens, lanes), lambda i: (0, i))
    whole = pl.BlockSpec(memory_space=pltpu.VMEM)
    fixed = lambda dims: pl.BlockSpec(dims, lambda i: (0,) * len(dims))
    return call(
        inside_kernel,
        (
            shape((tokens, width), F32),
            shape((tokens, n), F32),
            shape((tokens, n), F32),
            shape((tokens, heads), F32),
            shape((heads, 1, tokens), F32),
        ),
        inputs,
        grads,
        writes,
        reads,
        state,
        cum,
        cumt.reshape(heads, 1, tokens),
        grid=(steps,),
        in_specs=[
            part,
            part,
            whole,
            whole,
            pl.BlockSpec((n, lanes), lambda i: (0, i)),
            whole,
            pl.BlockSpec((each, 1, tokens), lambda i: (i, 0, 0)),
        ],
        out_specs=(
            part,
            fixed((tokens, n)),
            fixed((tokens, n)),
            fixed((tokens, heads)),
            pl.BlockSpec((each, 1, tokens), lambda i: (i, 0, 0)),
        ),
        scratch=[pltpu.VMEM((tokens, tokens), F32), pltpu.VMEM((tokens, tokens), F32)],
        cost=pl.CostEstimate(
            flops=8 * heads * tokens * tokens * 64, bytes_accessed=8 * tokens * width, transcendentals=heads * tokens * tokens
        ),
    )


def last_kernel(
    inputs_ref,
    writes_ref,
    state_ref,
    adjoint_ref,
    cum_ref,
    dx_ref,
    dwrite_in_ref,
    dcum_ref,
    dcumt_ref,
    input_grad_ref,
    dwrite_ref,
    decay_ref,
):
    tokens, width = inputs_ref.shape
    heads = cum_ref.shape[1]
    cum = cum_ref[...]
    total = cum[tokens - 1 : tokens, :]
    wide = spread(heads, width)
    remaining = dot(jnp.exp(total - cum), wide, 1, 0, HIGHEST)
    adjoint = adjoint_ref[...]
    inputs = inputs_ref[...].astype(F32)
    moved = remaining * dot(writes_ref[...], adjoint, 1, 0)
    input_grad_ref[...] = (dx_ref[...] + moved).astype(BF16)
    dwrite_ref[...] = dwrite_in_ref[...] + dot((remaining * inputs).astype(BF16), adjoint, 1, 1)
    shares = dot(moved * inputs, wide, 1, 1, HIGHEST)
    kept = state_ref[...].astype(F32) * adjoint.astype(F32)
    kept = jnp.broadcast_to(jnp.sum(kept, axis=0, keepdims=True), (8, width))
    tail = dot(kept, wide, 1, 1, HIGHEST)[0:1, :] * jnp.exp(total)
    after = (iota((tokens, tokens), 1) >= iota((tokens, tokens), 0)).astype(F32)
    before = (iota((tokens, tokens), 1) < iota((tokens, tokens), 0)).astype(F32)
    decay_ref[...] = (
        dot(after, dcum_ref[...], 1, 0, HIGHEST)
        - dot(after, dcumt_ref[...], 1, 1, HIGHEST)
        + dot(before, shares, 1, 0, HIGHEST)
        + tail
    )


def shards(
    mixer_input,
    write_proj,
    read_proj,
    log_decay,
    resid,
    out_grad,
    gate_probs,
    expert_ids,
    expert_up,
    expert_down,
):
    tokens, width = resid.shape
    heads = log_decay.shape[1]
    n = write_proj.shape[1]
    shard_count = lax.axis_size("seq")
    experts = lax.axis_size("grp") * shard_count
    cap = 4 * tokens // experts
    slots = experts * cap
    everyone = ("grp", "seq")
    up, down = expert_up[0], expert_down[0]
    ids = expert_ids.T
    gates = gate_probs.T

    def swap(x, axes):
        return lax.all_to_all(x, axes, split_axis=0, concat_axis=0, tiled=True)

    send_rows, targets = call(
        functools.partial(rows_kernel, experts, cap),
        (shape((slots, width), BF16), shape((2, tokens), jnp.int32)),
        resid,
        ids,
    )
    rows = swap(send_rows, everyone)
    send_scaled = call(grads_kernel, shape((slots, width), BF16), out_grad, gates, targets)
    scaled = swap(send_scaled, everyone)

    state_rows = n // shard_count
    padded = -(-(state_rows + 2) // 16) * 16
    cum, cumt, send_ends = call(
        ends_kernel,
        (
            shape((tokens, heads), F32),
            shape((heads, tokens), F32),
            shape((shard_count, padded, width), BF16),
        ),
        mixer_input,
        write_proj,
        log_decay,
    )
    ends = swap(send_ends, "seq")
    parts = shape((shard_count, state_rows, width), BF16)
    starts = call(functools.partial(scan_kernel, False), parts, ends, ends)
    state = swap(starts, "seq").reshape(n, width)

    hidden = jnp.dot(rows, up, preferred_element_type=F32)
    sigmoid = jax.nn.sigmoid(hidden)
    act = (hidden * sigmoid).astype(BF16)
    slope = sigmoid * (1.0 + hidden * (1.0 - sigmoid))
    pre_grad, row_grad, term = expert_stage(scaled, act, slope, up, down)
    back = swap(row_grad, everyone)
    terms = swap(term.astype(BF16).reshape(experts, cap), everyone)
    down_grad = dot(act, scaled, 0, 0).astype(BF16)
    up_grad = dot(rows, pre_grad, 0, 0).astype(BF16)

    resid_grad, send_adjoint = call(
        home_kernel,
        (shape((tokens, width), BF16), shape((n, width), BF16)),
        back,
        targets,
        resid,
        out_grad,
        read_proj,
        cum,
    )
    adjoints = swap(send_adjoint.reshape(shard_count, state_rows, width), "seq")
    later = call(functools.partial(scan_kernel, True), parts, adjoints, ends)
    adjoint = swap(later, "seq").reshape(n, width)

    gate_grad = call(
        gate_kernel,
        shape((2, tokens), F32),
        jnp.broadcast_to(terms.reshape(1, slots), (8, slots)),
        targets,
        gates,
    )
    gate_grad = gate_grad.T.astype(BF16)

    dx, dwrite, read_grad, dcum, dcumt = inside_stage(
        mixer_input, resid_grad, write_proj, read_proj, state, cum, cumt
    )
    input_grad, write_grad, decay_grad = call(
        last_kernel,
        (shape((tokens, width), BF16), shape((tokens, n), F32), shape((tokens, heads), F32)),
        mixer_input,
        write_proj,
        state,
        adjoint,
        cum,
        dx,
        dwrite,
        dcum,
        dcumt.reshape(heads, tokens),
    )
    return (
        input_grad,
        write_grad,
        read_grad,
        decay_grad,
        resid_grad,
        gate_grad,
        up_grad[None],
        down_grad[None],
    )


def solution(mesh):
    flat = P(("grp", "seq"), None)
    cube = P(("grp", "seq"), None, None)
    return jax.shard_map(
        shards,
        mesh=mesh,
        in_specs=(flat,) * 8 + (cube,) * 2,
        out_specs=(flat,) * 6 + (cube,) * 2,
        check_vma=False,
    )
```

profile of v0, /device:TPU:1, one launch (start us, length us, event | category | flops | bytes accessed | tf_op | source)
XLA Modules:
  0.0 249.5 jit_solution(4476205882531320749)
XLA Ops:
  0.6 3.3 %shard_map.163 = (bf16[1024,1024]{1,0:T(8,128)(2,1)}, s32[2,256]{1,0:T(2,128)}) custom-call(bf16[256,1024]{1,0:T(8,128)(2,1)} %resid_ref.3, s32[2,256]{1,0:T(2,128)} %bitcast.46), custom_call_target="tpu_custom_call" | custom-call | tf_op jit(solution)/shard_map/pallas_call | solution.py:33
  3.9 3.1 %shard_map.164 = bf16[1024,1024]{1,0:T(8,128)(2,1)} custom-call(bf16[256,1024]{1,0:T(8,128)(2,1)} %out_grad_ref.3, f32[2,256]{1,0:T(2,128)} %bitcast.44, s32[2,256]{1,0:T(2,128)} %get-tuple-element.27.targets_ref), custom_call_target="tpu_custom_call" | custom-call | tf_op jit(solution)/shard_map/pallas_call | solution.py:33
  7.0 54.9 %all_to_all.60 = bf16[32,32,1024]{2,1,0:T(8,128)(2,1)} all-to-all(bf16[32,32,1024]{2,1,0:T(8,128)(2,1)} %bitcast.31), channel_id=1, replica_groups=mesh['grp'=4,'seq'=8] {'grp','seq'}, dimensions={0} | all-to-all | bytes 4194304 | tf_op jit(solution)/shard_map/all_to_all | solution.py:379
  61.9 4.7 %all-to-all-start.3 = ((bf16[32,32,1024]{2,1,0:T(8,128)(2,1)}), bf16[32,32,1024]{2,1,0:T(8,128)(2,1)S(1)}, u32[]{:S(2)}, u32[]{:S(2)}) async-start(bf16[32,32,1024]{2,1,0:T(8,128)(2,1)} %bitcast.38), calls=%async_computation.3 | async-start | bytes 4194304 | tf_op jit(solution)/shard_map/all_to_all | solution.py:379
  66.6 0.0 copy-done.7
  66.6 0.8 copy.25.decays_ref
  67.3 3.7 %shard_map.161 = (f32[256,16]{1,0:T(8,128)}, f32[16,256]{1,0:T(8,128)}, bf16[8,32,1024]{2,1,0:T(8,128)(2,1)}) custom-call(bf16[256,1024]{1,0:T(8,128)(2,1)} %inputs_ref.5, bf16[256,128]{1,0:T(8,128)(2,1)} %writes_ref.5, f32[256,16]{1,0:T(8,128)} %copy.25.decays_ref), custom_call_target="tpu_custom_call" | custom-call | tf_op jit(solution)/shard_map/pallas_call | solution.py:33
  71.0 43.6 %all-to-all-done.3 = bf16[32,32,1024]{2,1,0:T(8,128)(2,1)S(1)} async-done(((bf16[32,32,1024]{2,1,0:T(8,128)(2,1)}), bf16[32,32,1024]{2,1,0:T(8,128)(2,1)S(1)}, u32[]{:S(2)}, u32[]{:S(2)}) %all-to-all-start.3) | async-done | bytes 2097184 | tf_op jit(solution)/shard_map/all_to_all | solution.py:379
  114.6 4.7 %all-to-all-start = ((bf16[8,32,1024]{2,1,0:T(8,128)(2,1)}), bf16[8,32,1024]{2,1,0:T(8,128)(2,1)S(1)}, u32[]{:S(2)}, u32[]{:S(2)}) async-start(bf16[8,32,1024]{2,1,0:T(8,128)(2,1)} %get-tuple-element.26), calls=%async_computation | async-start | bytes 1048576 | tf_op jit(solution)/shard_map/all_to_all | solution.py:379
  119.3 7.7 %add_multiply_fusion = (f32[1024,1024]{1,0:T(8,128)}, bf16[1024,1024]{1,0:T(8,128)(2,1)}) fusion(bf16[1024,1024]{1,0:T(8,128)(2,1)S(1)} %bitcast.33, bf16[1,1024,1024]{2,1,0:T(8,128)(2,1)} %param.18), kind=kOutput, calls=%fused_computation | convolution fusion | flops 2156920832 | bytes 10485760 | tf_op jit(solution)/shard_map/dot_general | solution.py:409
  127.0 0.0 copy-done.2
  127.0 10.9 %shard_map.165 = (bf16[1024,1024]{1,0:T(8,128)(2,1)}, bf16[1024,1024]{1,0:T(8,128)(2,1)}, f32[4,8,256]{2,1,0:T(8,128)}) custom-call(bf16[1024,1024]{1,0:T(8,128)(2,1)} %bitcast.35, bf16[1024,1024]{1,0:T(8,128)(2,1)} %get-tuple-element.77.act_ref, f32[1024,1024]{1,0:T(8,128)} %get-tuple-element.76.slope_ref, bf16[1024,1024]{1,0:T(8,128)(2,1)} %bitcast.47, ...), custom_call_target="tpu_custom_call" | custom-call | flops 4294967296 | bytes 20971520 | tf_op jit(solution)/shard_map/pallas_call | solution.py:33
  137.9 0.0 all-to-all-done.ends_ref.kept_ref
  137.9 0.0 copy-start.8
  137.9 0.8 copy-done.1
  138.7 4.3 %all-to-all-start.4 = ((bf16[32,32,1024]{2,1,0:T(8,128)(2,1)}), bf16[32,32,1024]{2,1,0:T(8,128)(2,1)S(1)}, u32[]{:S(2)}, u32[]{:S(2)}) async-start(bf16[32,32,1024]{2,1,0:T(8,128)(2,1)} %bitcast.37), calls=%async_computation.4 | async-start | bytes 4194304 | tf_op jit(solution)/shard_map/all_to_all | solution.py:379
  143.0 0.8 fusion
  143.8 0.7 convert_element_type.33
  144.5 46.5 %all-to-all-done.4 = bf16[32,32,1024]{2,1,0:T(8,128)(2,1)S(1)} async-done(((bf16[32,32,1024]{2,1,0:T(8,128)(2,1)}), bf16[32,32,1024]{2,1,0:T(8,128)(2,1)S(1)}, u32[]{:S(2)}, u32[]{:S(2)}) %all-to-all-start.4) | async-done | bytes 2097184 | tf_op jit(solution)/shard_map/all_to_all | solution.py:379
  191.0 4.8 %all-to-all-start.7 = ((bf16[32,1,32]{2,1,0:T(2,128)(2,1)}), bf16[32,1,32]{2,1,0:T(2,128)(2,1)S(1)}, u32[]{:S(2)}, u32[]{:S(2)}) async-start(bf16[32,1,32]{2,1,0:T(2,128)(2,1)} %convert_element_type.33), calls=%async_computation.7 | async-start | bytes 32768 | tf_op jit(solution)/shard_map/all_to_all | solution.py:379
  195.8 0.0 copy-done.8
  195.9 0.6 reshape.58.cumt_ref
  196.5 2.1 shard_map.162
  198.6 0.0 copy-done
  198.6 4.4 %shard_map.166 = (bf16[256,1024]{1,0:T(8,128)(2,1)}, bf16[128,1024]{1,0:T(8,128)(2,1)}) custom-call(bf16[1024,1024]{1,0:T(8,128)(2,1)} %bitcast.32, s32[2,256]{1,0:T(2,128)} %get-tuple-element.27.targets_ref, bf16[256,1024]{1,0:T(8,128)(2,1)} %resid_ref.3, bf16[256,1024]{1,0:T(8,128)(2,1)} %out_grad_ref.3, bf16[256,128]{1,0:T(8,128)(2,1)} %reads_ref.3, ...), custom_call_target="tpu_custom_call" | custom-call | tf_op jit(solution)/shard_map/pallas_call | solution.py:33
  203.0 0.0 all-to-all-done.7
  203.0 4.2 %all-to-all-start.5 = ((bf16[8,16,1024]{2,1,0:T(8,128)(2,1)}), bf16[8,16,1024]{2,1,0:T(8,128)(2,1)S(1)}, u32[]{:S(2)}, u32[]{:S(2)}) async-start(bf16[8,16,1024]{2,1,0:T(8,128)(2,1)} %bitcast.42), calls=%async_computation.5 | async-start | bytes 524288 | tf_op jit(solution)/shard_map/all_to_all | solution.py:379
  207.2 6.1 %convert_bitcast_fusion = bf16[1,1024,1024]{2,1,0:T(8,128)(2,1)} fusion(bf16[1024,1024]{1,0:T(8,128)(2,1)} %get-tuple-element.77.act_ref, bf16[1024,1024]{1,0:T(8,128)(2,1)} %bitcast.36), kind=kOutput, calls=%fused_computation.3 | convolution fusion | flops 2148532224 | bytes 6291456 | tf_op jit(solution)/shard_map/dot_general | solution.py:22
  213.2 0.0 all-to-all-done.5.ends_ref
  213.2 4.2 %all-to-all-start.1 = ((bf16[8,16,1024]{2,1,0:T(8,128)(2,1)}), bf16[8,16,1024]{2,1,0:T(8,128)(2,1)S(1)}, u32[]{:S(2)}, u32[]{:S(2)}) async-start(bf16[8,16,1024]{2,1,0:T(8,128)(2,1)} %shard_map.162), calls=%async_computation.1 | async-start | bytes 524288 | tf_op jit(solution)/shard_map/all_to_all | solution.py:379
  217.4 0.0 copy-done.3
  217.4 5.3 %convert_bitcast_fusion.1 = bf16[1,1024,1024]{2,1,0:T(8,128)(2,1)} fusion(bf16[1024,1024]{1,0:T(8,128)(2,1)S(1)} %bitcast.34, bf16[1024,1024]{1,0:T(8,128)(2,1)} %get-tuple-element.43), kind=kOutput, calls=%fused_computation.4 | convolution fusion | flops 2148532224 | bytes 6291456 | tf_op jit(solution)/shard_map/dot_general | solution.py:22
  222.7 0.0 copy-done.6
  222.7 0.1 reduce.1
  222.8 0.1 broadcast_in_dim.13
  222.9 0.6 broadcast_in_dim.14.terms_ref
  223.5 1.6 shard_map.170
  225.1 1.9 shard_map.167
  227.0 0.0 all-to-all-done.1
  227.0 4.2 %all-to-all-start.6 = ((bf16[8,16,1024]{2,1,0:T(8,128)(2,1)}), bf16[8,16,1024]{2,1,0:T(8,128)(2,1)S(1)}, u32[]{:S(2)}, u32[]{:S(2)}) async-start(bf16[8,16,1024]{2,1,0:T(8,128)(2,1)} %shard_map.167), calls=%async_computation.6 | async-start | bytes 524288 | tf_op jit(solution)/shard_map/all_to_all | solution.py:379
  231.2 1.2 convert_bitcast_fusion.2
  232.4 0.0 copy-done.4
  232.4 7.8 %shard_map.168 = (f32[256,1024]{1,0:T(8,128)}, f32[256,128]{1,0:T(8,128)}, f32[256,128]{1,0:T(8,128)}, f32[256,16]{1,0:T(8,128)}, f32[16,1,256]{2,1,0:T(1,128)}) custom-call(bf16[256,1024]{1,0:T(8,128)(2,1)} %inputs_ref.5, bf16[256,1024]{1,0:T(8,128)(2,1)} %get-tuple-element.72.grads_ref, bf16[256,128]{1,0:T(8,128)(2,1)} %writes_ref.5, ...), custom_call_target="tpu_custom_call" | custom-call | flops 536870912 | bytes 2097152 | tf_op jit(solution)/shard_map/pallas_call | solution.py:33
  240.3 1.3 copy.30
  241.6 0.0 all-to-all-done.6
  241.6 0.7 copy-done.5
  242.3 5.6 %shard_map.169 = (bf16[256,1024]{1,0:T(8,128)(2,1)}, f32[256,128]{1,0:T(8,128)}, f32[256,16]{1,0:T(8,128)}) custom-call(bf16[256,1024]{1,0:T(8,128)(2,1)} %inputs_ref.5, bf16[256,128]{1,0:T(8,128)(2,1)} %writes_ref.5, bf16[128,1024]{1,0:T(8,128)(2,1)} %bitcast.40, bf16[128,1024]{1,0:T(8,128)(2,1)} %bitcast.41, f32[256,16]{1,0:T(8,128)} %get-tuple-element.30.cum_ref, ...), custom_call_target="tpu_custom_call" | custom-call | tf_op jit(solution)/shard_map/pallas_call | solution.py:33
  247.9 1.6 copy.27
  (8 shorter events, 0.0 us)
Async XLA Ops:
  61.9 4.7 %copy-start.7 = (f32[256,16]{0,1:T(8,128)S(1)}, f32[256,16]{0,1:T(8,128)}, u32[]{:S(2)}) copy-start(f32[256,16]{0,1:T(8,128)} %param.13) | copy-start | bytes 49156
  61.9 52.7 %all-to-all-start.3 = ((bf16[32,32,1024]{2,1,0:T(8,128)(2,1)}), bf16[32,32,1024]{2,1,0:T(8,128)(2,1)S(1)}, u32[]{:S(2)}, u32[]{:S(2)}) async-start(bf16[32,32,1024]{2,1,0:T(8,128)(2,1)} %bitcast.38), calls=%async_computation.3 | async-start | bytes 4194304 | tf_op jit(solution)/shard_map/all_to_all | solution.py:379
  114.6 12.4 %copy-start.2 = (bf16[32,32,1024]{2,1,0:T(8,128)(2,1)}, bf16[32,32,1024]{2,1,0:T(8,128)(2,1)S(1)}, u32[]{:S(2)}) copy-start(bf16[32,32,1024]{2,1,0:T(8,128)(2,1)S(1)} %all-to-all-done.3) | copy-start | bytes 6291460
  114.6 23.3 %all-to-all-start = ((bf16[8,32,1024]{2,1,0:T(8,128)(2,1)}), bf16[8,32,1024]{2,1,0:T(8,128)(2,1)S(1)}, u32[]{:S(2)}, u32[]{:S(2)}) async-start(bf16[8,32,1024]{2,1,0:T(8,128)(2,1)} %get-tuple-element.26), calls=%async_computation | async-start | bytes 1048576 | tf_op jit(solution)/shard_map/all_to_all | solution.py:379
  137.9 0.8 copy-start.1
  137.9 58.0 %copy-start.8 = (f32[16,256]{1,0:T(8,128)S(1)}, f32[16,256]{1,0:T(8,128)}, u32[]{:S(2)}) copy-start(f32[16,256]{1,0:T(8,128)} %get-tuple-element.33) | copy-start | bytes 49156
  138.7 52.4 %all-to-all-start.4 = ((bf16[32,32,1024]{2,1,0:T(8,128)(2,1)}), bf16[32,32,1024]{2,1,0:T(8,128)(2,1)S(1)}, u32[]{:S(2)}, u32[]{:S(2)}) async-start(bf16[32,32,1024]{2,1,0:T(8,128)(2,1)} %bitcast.37), calls=%async_computation.4 | async-start | bytes 4194304 | tf_op jit(solution)/shard_map/all_to_all | solution.py:379
  191.0 7.5 %copy-start = (bf16[32,32,1024]{2,1,0:T(8,128)(2,1)}, bf16[32,32,1024]{2,1,0:T(8,128)(2,1)S(1)}, u32[]{:S(2)}) copy-start(bf16[32,32,1024]{2,1,0:T(8,128)(2,1)S(1)} %all-to-all-done.4) | copy-start | bytes 6291460
  191.0 11.9 %all-to-all-start.7 = ((bf16[32,1,32]{2,1,0:T(2,128)(2,1)}), bf16[32,1,32]{2,1,0:T(2,128)(2,1)S(1)}, u32[]{:S(2)}, u32[]{:S(2)}) async-start(bf16[32,1,32]{2,1,0:T(2,128)(2,1)} %convert_element_type.33), calls=%async_computation.7 | async-start | bytes 32768 | tf_op jit(solution)/shard_map/all_to_all | solution.py:379
  203.0 10.3 %all-to-all-start.5 = ((bf16[8,16,1024]{2,1,0:T(8,128)(2,1)}), bf16[8,16,1024]{2,1,0:T(8,128)(2,1)S(1)}, u32[]{:S(2)}, u32[]{:S(2)}) async-start(bf16[8,16,1024]{2,1,0:T(8,128)(2,1)} %bitcast.42), calls=%async_computation.5 | async-start | bytes 524288 | tf_op jit(solution)/shard_map/all_to_all | solution.py:379
  207.2 10.3 %copy-start.3 = (bf16[32,32,1024]{2,1,0:T(8,128)(2,1)S(1)}, bf16[32,32,1024]{2,1,0:T(8,128)(2,1)}, u32[]{:S(2)}) copy-start(bf16[32,32,1024]{2,1,0:T(8,128)(2,1)} %copy-done.2) | copy-start | bytes 6291460
  213.2 9.5 %copy-start.6 = (bf16[8,16,1024]{2,1,0:T(8,128)(2,1)}, bf16[8,16,1024]{2,1,0:T(8,128)(2,1)S(1)}, u32[]{:S(2)}) copy-start(bf16[8,16,1024]{2,1,0:T(8,128)(2,1)S(1)} %all-to-all-done.5.ends_ref) | copy-start | bytes 786436
  213.2 13.7 %all-to-all-start.1 = ((bf16[8,16,1024]{2,1,0:T(8,128)(2,1)}), bf16[8,16,1024]{2,1,0:T(8,128)(2,1)S(1)}, u32[]{:S(2)}, u32[]{:S(2)}) async-start(bf16[8,16,1024]{2,1,0:T(8,128)(2,1)} %shard_map.162), calls=%async_computation.1 | async-start | bytes 524288 | tf_op jit(solution)/shard_map/all_to_all | solution.py:379
  227.0 5.4 %copy-start.4 = (bf16[8,16,1024]{2,1,0:T(8,128)(2,1)}, bf16[8,16,1024]{2,1,0:T(8,128)(2,1)S(1)}, u32[]{:S(2)}) copy-start(bf16[8,16,1024]{2,1,0:T(8,128)(2,1)S(1)} %all-to-all-done.1) | copy-start | bytes 786436
  227.0 14.6 %all-to-all-start.6 = ((bf16[8,16,1024]{2,1,0:T(8,128)(2,1)}), bf16[8,16,1024]{2,1,0:T(8,128)(2,1)S(1)}, u32[]{:S(2)}, u32[]{:S(2)}) async-start(bf16[8,16,1024]{2,1,0:T(8,128)(2,1)} %shard_map.167), calls=%async_computation.6 | async-start | bytes 524288 | tf_op jit(solution)/shard_map/all_to_all | solution.py:379
  241.6 0.7 copy-start.5
where the time goes:
time: 251 us; the launch traced here: 249 us
  waiting for transfers between devices  90.1 us (36%)
  blocking collectives  54.9 us (22%)
  Pallas kernels  44.4 us (18%)
  starting transfers between devices  31.1 us (12%)
  matrix products  19.1 us (8%)
  local copies, waits for them, and re-layouts  7.95 us (3%)
    all_to_all x7, waiting for transfers between devices, swap(): return lax.all_to_all(x, axes, split_axis=0, concat_axis=0, tiled=True)  90.1 us
    all_to_all x1, blocking collectives, swap(): return lax.all_to_all(x, axes, split_axis=0, concat_axis=0, tiled=True)  54.9 us
    pallas_call x10, Pallas kernels, call(): pl.pallas_call(kernel, out_shape=outs, in_specs=in_specs if in_specs is n...  44.4 us
    all_to_all x7, starting transfers between devices, swap(): return lax.all_to_all(x, axes, split_axis=0, concat_axis=0, tiled=True)  31.1 us
    dot_general x2, matrix products, dot(): lax.dot_general(a, b, (((ca,), (cb,)), ((), ())), precision=precision, pr...  11.4 us
    dot_general x1, matrix products, shards(): hidden = jnp.dot(rows, up, preferred_element_type=F32)  7.7 us
    unnamed x21, local copies, waits for them, and re-layouts  5.16 us
  transfers between devices with their start and end apart: 7, of which 2 were waited for; matrix products, arithmetic and copies ran while one was open for 10% of the time, Pallas kernels for 13%

commit v1 on v0

--- a/solution.py
+++ b/solution.py
@@ -7,11 +7,12 @@
 from jax.experimental.pallas import tpu as pltpu
 from jax.sharding import PartitionSpec as P
 
+
 EPSILON = 1e-06
 HIGHEST = lax.Precision.HIGHEST
 F32 = jnp.float32
 BF16 = jnp.bfloat16
-VMEM_LIMIT = 60 * 1024 * 1024
+VMEM_LIMIT = 20 * 1024 * 1024
 
 
 def iota(shape, axis):
@@ -130,18 +131,351 @@
     out_ref[...] = jnp.concatenate([first[0:1, :], second[0:1, :]], axis=0) / gates
 
 
+def message_kernel(planes, shard_count, cap, resid_ref, ids_ref, gates_ref, message_ref, targets_ref):
+    tokens, width = resid_ref.shape
+    experts = planes * shard_count
+    resid = resid_ref[...].astype(F32)
+    inverse = lax.rsqrt(jnp.mean(resid * resid, axis=1, keepdims=True) + EPSILON)
+    message_ref[0:tokens, :] = (resid * inverse).astype(BF16)
+    ids = ids_ref[...]
+    number = iota((experts, tokens), 0)
+    first = (number == ids[0:1, :]).astype(F32)
+    second = (number == ids[1:2, :]).astype(F32)
+    earlier = (iota((tokens, tokens), 0) < iota((tokens, tokens), 1)).astype(BF16)
+    before = dot((first + second).astype(BF16), earlier, 1, 0)
+    ranks = jnp.concatenate(
+        [
+            jnp.sum(before * first, axis=0, keepdims=True),
+            jnp.sum(before * second, axis=0, keepdims=True),
+        ],
+        axis=0,
+    )
+    targets_ref[...] = ids * cap + ranks.astype(jnp.int32)
+    named = ids.astype(F32)
+    plane = jnp.floor((named + 0.5) * (1.0 / shard_count))
+    shard = named - plane * shard_count
+    facts = jnp.concatenate(
+        [plane, shard, ranks, gates_ref[...], jnp.zeros((8, tokens), F32)], axis=0
+    )
+    message_ref[tokens:, 0:tokens] = facts.astype(BF16)
+    if width > tokens:
+        message_ref[tokens:, tokens:] = jnp.zeros((16, width - tokens), BF16)
+
+
+def named_rows(me_ref, message, slots, cap):
+    tokens = message.shape[0] - 16
+    facts = message[tokens:, 0:tokens].astype(F32)
+    places = (facts[2:4, :].astype(jnp.int32) ^ me_ref[1]) * cap
+    places = places + facts[4:6, :].astype(jnp.int32)
+    places = jnp.where(facts[0:2, :] == me_ref[0].astype(F32), places, -1)
+    hit0, hit1 = one_hot(places, slots)
+    select = jnp.where(hit0 | hit1, 1.0, 0.0).astype(BF16)
+    rows = dot(select, message[0:tokens, :], 1, 0).astype(BF16)
+    keys = jnp.concatenate(
+        [places.astype(F32), facts[6:8, :], jnp.zeros((4, tokens), F32)], axis=0
+    )
+    return keys, rows
+
+
+def pick_rows_kernel(blocks, cap, me_ref, *refs):
+    messages, outs, keys_ref = refs[:blocks], refs[blocks:-1], refs[-1]
+    for m, message in enumerate(messages):
+        keys_ref[m], rows = named_rows(me_ref, message, len(outs) * cap, cap)
+        for x, out in enumerate(outs):
+            out[m * cap : (m + 1) * cap, :] = rows[x * cap : (x + 1) * cap, :]
+
+
+def scaled_rows(keys, grads, slots):
+    hit0, hit1 = one_hot(keys[0:2, :].astype(jnp.int32), slots)
+    select = jnp.where(hit0, keys[2:3, :], 0.0) + jnp.where(hit1, keys[3:4, :], 0.0)
+    return dot(select.astype(BF16), grads, 1, 0).astype(BF16)
+
+
+def pick_grads_kernel(blocks, cap, keys_ref, *refs):
+    grads, outs = refs[:blocks], refs[blocks:]
+    for m, grad in enumerate(grads):
+        rows = scaled_rows(keys_ref[m], grad[...], len(outs) * cap)
+        for x, out in enumerate(outs):
+            out[m * cap : (m + 1) * cap, :] = rows[x * cap : (x + 1) * cap, :]
+
+
+def pick_both_kernel(cap, me_ref, message_ref, grads_ref, *outs):
+    slots = len(outs) * cap
+    keys, rows = named_rows(me_ref, message_ref, slots, cap)
+    scaled = scaled_rows(keys, grads_ref[...], slots)
+    for x, out in enumerate(outs):
+        out[0:cap, :] = rows[x * cap : (x + 1) * cap, :]
+        out[cap:, :] = scaled[x * cap : (x + 1) * cap, :]
+
+
+def gather_group(me_ref, parts, group_ref):
+    cap = parts[0].shape[0]
+    for x, part in enumerate(parts):
+        at = pl.multiple_of((me_ref[1] ^ x) * cap, cap)
+        group_ref[pl.ds(at, cap), :] = part[...]
+    return group_ref[...]
+
+
+def forward_group(rows, up_ref):
+    hidden = dot(rows, up_ref[...], 1, 0)
+    sigmoid = jax.nn.sigmoid(hidden)
+    return (hidden * sigmoid).astype(BF16), sigmoid * (1.0 + hidden * (1.0 - sigmoid))
+
+
+def hidden_kernel(count, me_ref, *refs):
+    parts, (up_ref, rows_ref, act_ref, slope_ref) = refs[:count], refs[count:]
+    act_ref[...], slope_ref[...] = forward_group(gather_group(me_ref, parts, rows_ref), up_ref)
+
+
+def backward_group(scaled, act, slope, up_ref, down_ref, pre_ref, row_ref, term_ref):
+    act_grad = dot(scaled, down_ref[...], 1, 1)
+    pre = (act_grad * slope).astype(BF16)
+    pre_ref[...] = pre
+    row_ref[0] = dot(pre, up_ref[...], 1, 1).astype(BF16)
+    prod = act_grad * act.astype(F32)
+    high = prod.astype(BF16)
+    low = (prod - high.astype(F32)).astype(BF16)
+    ones = jnp.ones((8, prod.shape[1]), BF16)
+    term_ref[0] = dot(ones, high, 1, 1) + dot(ones, low, 1, 1)
+
+
+def routed_kernel(count, me_ref, *refs):
+    parts = refs[:count]
+    act_ref, slope_ref, up_ref, down_ref, scaled_ref, pre_ref, row_ref, term_ref = refs[count:]
+    scaled = gather_group(me_ref, parts, scaled_ref)
+    backward_group(
+        scaled, act_ref[...], slope_ref[...], up_ref, down_ref, pre_ref, row_ref, term_ref
+    )
+
+
+def far_kernel(count, me_ref, *refs):
+    cap = refs[0].shape[0] // 2
+    up_ref, down_ref = refs[count : count + 2]
+    rows_ref, act_ref, scaled_ref, pre_ref, row_ref, term_ref = refs[-6:]
+    rows = gather_group(me_ref, [part.at[0:cap, :] for part in refs[:count]], rows_ref)
+    act, slope = forward_group(rows, up_ref)
+    act_ref[...] = act
+    scaled = gather_group(me_ref, [part.at[cap:, :] for part in refs[:count]], scaled_ref)
+    backward_group(scaled, act, slope, up_ref, down_ref, pre_ref, row_ref, term_ref)
+
+
+def grouped(kernel, me, parts, each, extras, extra_specs, outs, out_specs, steps, aliases, flops):
+    width = parts[0].shape[1]
+    return pl.pallas_call(
+        functools.partial(kernel, len(parts)),
+        out_shape=outs,
+        grid_spec=pltpu.PrefetchScalarGridSpec(
+            num_scalar_prefetch=1,
+            grid=(steps,),
+            in_specs=[pl.BlockSpec((each, width), lambda i, me: (i, 0))] * len(parts) + extra_specs,
+            out_specs=out_specs,
+        ),
+        input_output_aliases=aliases,
+        compiler_params=pltpu.CompilerParams(vmem_limit_bytes=VMEM_LIMIT),
+        cost_estimate=pl.CostEstimate(
+            flops=flops, bytes_accessed=6 * width * width, transcendentals=0
+        ),
+    )(me, *parts, *extras)
+
+
+def outer_kernel(a1_ref, b1_ref, a2_ref, b2_ref, out_ref):
+    out_ref[...] = (
+        dot(a1_ref[...], b1_ref[...], 0, 0) + dot(a2_ref[...], b2_ref[...], 0, 0)
+    ).astype(BF16)
+
+
+def outer_stage(a1, b1, a2, b2):
+    left, right = a1.shape[1], b1.shape[1]
+    tile = min(256, right)
+    whole = pl.BlockSpec(memory_space=pltpu.VMEM)
+    column = lambda b: pl.BlockSpec((b.shape[0], tile), lambda i: (0, i))
+    rows = a1.shape[0] + a2.shape[0]
+    return call(
+        outer_kernel,
+        shape((left, right), BF16),
+        a1,
+        b1,
+        a2,
+        b2,
+        grid=(right // tile,),
+        in_specs=[whole, column(b1), whole, column(b2)],
+        out_specs=pl.BlockSpec((left, tile), lambda i: (0, i)),
+        cost=pl.CostEstimate(
+            flops=2 * rows * left * right, bytes_accessed=6 * left * right, transcendentals=0
+        ),
+    )
+
+
+def routed_experts(resid, out_grad, ids, gates, up, down, cap, shard_count, planes, early):
+    tokens, width = resid.shape
+    hidden = up.shape[1]
+    group = shard_count * cap
+    plane, shard = lax.axis_index("grp"), lax.axis_index("seq")
+    me = jnp.stack([plane, shard]).astype(jnp.int32)
+    smem = pl.BlockSpec(memory_space=pltpu.SMEM)
+    vmem = pl.BlockSpec(memory_space=pltpu.VMEM)
+
+    def across(x, bit):
+        return lax.ppermute(x, "grp", [(i, i ^ bit) for i in range(planes)])
+
+    def spread_out(parts):
+        moved = [
+            lax.ppermute(part, "seq", [(i, i ^ x) for i in range(shard_count)])
+            for x, part in enumerate(parts)
+            if x
+        ]
+        return [parts[0]] + moved
+
+    def pick_rows(messages):
+        count = len(messages)
+        outs = [shape((count * cap, width), BF16)] * shard_count
+        *parts, keys = call(
+            functools.partial(pick_rows_kernel, count, cap),
+            tuple(outs + [shape((count, 8, tokens), F32)]),
+            me,
+            *messages,
+            in_specs=[smem] + [vmem] * count,
+        )
+        return parts, keys
+
+    def pick_grads(keys, grads):
+        count = len(grads)
+        outs = [shape((count * cap, width), BF16)] * shard_count
+        return call(functools.partial(pick_grads_kernel, count, cap), tuple(outs), keys, *grads)
+
+    def block(width):
+        return pl.BlockSpec((group, width), lambda i, me: (i, 0))
+
+    def hidden_stage(parts, steps):
+        rows = steps * group
+        return grouped(
+            hidden_kernel,
+            me,
+            parts,
+            cap,
+            (up,),
+            [vmem],
+            (shape((rows, width), BF16), shape((rows, hidden), BF16), shape((rows, hidden), F32)),
+            (block(width), block(hidden), block(hidden)),
+            steps,
+            {},
+            2 * rows * width * hidden,
+        )
+
+    rows_of = lambda steps, size, dtype: shape((steps * group, size), dtype)
+    backs = (shape((planes, group, width), BF16), shape((planes, 8, group), F32))
+
+    def back_blocks(base):
+        to_plane = lambda i, me: (me[0] ^ (base + i), 0, 0)
+        return (pl.BlockSpec((1, group, width), to_plane), pl.BlockSpec((1, 8, group), to_plane))
+
+    def routed_stage(parts, act, slope, steps):
+        return grouped(
+            routed_kernel,
+            me,
+            parts,
+            cap,
+            (act, slope, up, down),
+            [block(hidden), block(hidden), vmem, vmem],
+            (rows_of(steps, width, BF16), rows_of(steps, hidden, BF16)) + backs,
+            (block(width), block(hidden)) + back_blocks(0),
+            steps,
+            {},
+            4 * steps * group * width * hidden,
+        )
+
+    def far_stage(parts, filled):
+        first = 1 + len(parts) + 2
+        return grouped(
+            far_kernel,
+            me,
+            parts,
+            2 * cap,
+            (up, down) + tuple(filled),
+            [vmem, vmem] + [pl.BlockSpec(memory_space=pl.ANY)] * 2,
+            (
+                rows_of(1, width, BF16),
+                rows_of(1, hidden, BF16),
+                rows_of(1, width, BF16),
+                rows_of(1, hidden, BF16),
+            )
+            + backs,
+            (block(width), block(hidden), block(width), block(hidden)) + back_blocks(3),
+            1,
+            {first: 4, first + 1: 5},
+            6 * group * width * hidden,
+        )
+
+    message, targets = call(
+        functools.partial(message_kernel, planes, shard_count, cap),
+        (shape((tokens + 16, width), BF16), shape((2, tokens), jnp.int32)),
+        resid,
+        ids,
+        gates,
+    )
+    message2 = across(message, 2)
+    message1 = across(message, 1)
+    grad2 = across(out_grad, 2)
+    grad1 = across(out_grad, 1)
+    message3 = across(message2, 1)
+    near_rows, near_keys = pick_rows([message, message1, message2])
+    near_rows = spread_out(near_rows)
+    grad3 = across(grad2, 1)
+    near_grads = pick_grads(near_keys, [out_grad, grad1, grad2])
+    near_grads = spread_out(near_grads)
+    rows_a, act_a, slope_a = hidden_stage(near_rows, 3)
+    far = call(
+        functools.partial(pick_both_kernel, cap),
+        tuple([shape((2 * cap, width), BF16)] * shard_count),
+        me,
+        message3,
+        grad3,
+        in_specs=[smem, vmem, vmem],
+    )
+    far = spread_out(far)
+    act_a, early = lax.optimization_barrier((act_a, early))
+    scaled_a, pre_a, row_grad, term = routed_stage(near_grads, act_a, slope_a, 3)
+    rows_b, act_b, scaled_b, pre_b, row_grad, term = far_stage(far, (row_grad, term))
+    pieces = lambda: (
+        outer_stage(act_a, scaled_a, act_b, scaled_b),
+        outer_stage(rows_a, pre_a, rows_b, pre_b),
+    )
+    return targets, row_grad.reshape(-1, width), term[:, 0, :], pieces, early
+
+
+def plain_experts(resid, out_grad, ids, gates, up, down, cap, experts, swap, early):
+    tokens, width = resid.shape
+    slots = experts * cap
+    send_rows, targets = call(
+        functools.partial(rows_kernel, experts, cap),
+        (shape((slots, width), BF16), shape((2, tokens), jnp.int32)),
+        resid,
+        ids,
+    )
+    rows = swap(send_rows)
+    send_scaled = call(grads_kernel, shape((slots, width), BF16), out_grad, gates, targets)
+    scaled = swap(send_scaled)
+    hidden = jnp.dot(rows, up, preferred_element_type=F32)
+    sigmoid = jax.nn.sigmoid(hidden)
+    act = (hidden * sigmoid).astype(BF16)
+    slope = sigmoid * (1.0 + hidden * (1.0 - sigmoid))
+    pre_grad, row_grad, term = expert_stage(scaled, act, slope, up, down)
+    pieces = lambda: (dot(act, scaled, 0, 0).astype(BF16), dot(rows, pre_grad, 0, 0).astype(BF16))
+    return targets, row_grad, term, pieces, early
+
+
 def spread(heads, width):
     return (iota((heads, width), 1) // (width // heads) == iota((heads, width), 0)).astype(F32)
 
 
 def ends_kernel(inputs_ref, writes_ref, decays_ref, cum_ref, cumt_ref, send_ref):
     decays = decays_ref[...]
-    tokens, heads = decays.shape
+    heads, tokens = decays.shape
     parts, padded, width = send_ref.shape
     upto = (iota((tokens, tokens), 0) >= iota((tokens, tokens), 1)).astype(F32)
-    cum = dot(upto, decays, 1, 0, HIGHEST)
+    cum = dot(upto, decays, 1, 1, HIGHEST)
     cum_ref[...] = cum
-    cumt_ref[...] = dot(decays, upto, 0, 1, HIGHEST)
+    cumt_ref[...] = dot(decays, upto, 1, 1, HIGHEST)
     total = cum[tokens - 1 : tokens, :]
     wide = spread(heads, width)
     remaining = dot(jnp.exp(total - cum), wide, 1, 0, HIGHEST)
@@ -318,6 +652,7 @@
     state_ref,
     adjoint_ref,
     cum_ref,
+    cumt_ref,
     dx_ref,
     dwrite_in_ref,
     dcum_ref,
@@ -340,13 +675,13 @@
     shares = dot(moved * inputs, wide, 1, 1, HIGHEST)
     kept = state_ref[...].astype(F32) * adjoint.astype(F32)
     kept = jnp.broadcast_to(jnp.sum(kept, axis=0, keepdims=True), (8, width))
-    tail = dot(kept, wide, 1, 1, HIGHEST)[0:1, :] * jnp.exp(total)
+    tail = dot(wide, kept, 1, 1, HIGHEST)[:, 0:1] * jnp.exp(cumt_ref[...][:, tokens - 1 : tokens])
     after = (iota((tokens, tokens), 1) >= iota((tokens, tokens), 0)).astype(F32)
     before = (iota((tokens, tokens), 1) < iota((tokens, tokens), 0)).astype(F32)
     decay_ref[...] = (
-        dot(after, dcum_ref[...], 1, 0, HIGHEST)
-        - dot(after, dcumt_ref[...], 1, 1, HIGHEST)
-        + dot(before, shares, 1, 0, HIGHEST)
+        dot(dcum_ref[...], after, 0, 1, HIGHEST)
+        - dot(dcumt_ref[...], after, 1, 1, HIGHEST)
+        + dot(shares, before, 0, 1, HIGHEST)
         + tail
     )
 
@@ -378,16 +713,6 @@
     def swap(x, axes):
         return lax.all_to_all(x, axes, split_axis=0, concat_axis=0, tiled=True)
 
-    send_rows, targets = call(
-        functools.partial(rows_kernel, experts, cap),
-        (shape((slots, width), BF16), shape((2, tokens), jnp.int32)),
-        resid,
-        ids,
-    )
-    rows = swap(send_rows, everyone)
-    send_scaled = call(grads_kernel, shape((slots, width), BF16), out_grad, gates, targets)
-    scaled = swap(send_scaled, everyone)
-
     state_rows = n // shard_count
     padded = -(-(state_rows + 2) // 16) * 16
     cum, cumt, send_ends = call(
@@ -399,23 +724,27 @@
         ),
         mixer_input,
         write_proj,
-        log_decay,
+        log_decay.T,
     )
     ends = swap(send_ends, "seq")
     parts = shape((shard_count, state_rows, width), BF16)
     starts = call(functools.partial(scan_kernel, False), parts, ends, ends)
     state = swap(starts, "seq").reshape(n, width)
 
-    hidden = jnp.dot(rows, up, preferred_element_type=F32)
-    sigmoid = jax.nn.sigmoid(hidden)
-    act = (hidden * sigmoid).astype(BF16)
-    slope = sigmoid * (1.0 + hidden * (1.0 - sigmoid))
-    pre_grad, row_grad, term = expert_stage(scaled, act, slope, up, down)
+    planes = experts // shard_count
+    if planes == 4 and shard_count <= 8 and cap % 16 == 0 and tokens <= width:
+        targets, row_grad, term, outers, state = routed_experts(
+            resid, out_grad, ids, gates, up, down, cap, shard_count, planes, state
+        )
+    else:
+        targets, row_grad, term, outers, state = plain_experts(
+            resid, out_grad, ids, gates, up, down, cap, experts, lambda x: swap(x, everyone), state
+        )
     back = swap(row_grad, everyone)
-    terms = swap(term.astype(BF16).reshape(experts, cap), everyone)
-    down_grad = dot(act, scaled, 0, 0).astype(BF16)
-    up_grad = dot(rows, pre_grad, 0, 0).astype(BF16)
-
+    down_grad, up_grad = outers()
+    back, down_grad, up_grad = lax.optimization_barrier((back, down_grad, up_grad))
+    terms, back = lax.optimization_barrier((term.astype(BF16).reshape(experts, cap), back))
+    terms = swap(terms, everyone)
     resid_grad, send_adjoint = call(
         home_kernel,
         (shape((tokens, width), BF16), shape((n, width), BF16)),
@@ -426,10 +755,13 @@
         read_proj,
         cum,
     )
+    send_adjoint, terms = lax.optimization_barrier((send_adjoint, terms))
     adjoints = swap(send_adjoint.reshape(shard_count, state_rows, width), "seq")
+    dx, dwrite, read_grad, dcum, dcumt = inside_stage(
+        mixer_input, resid_grad, write_proj, read_proj, state, cum, cumt
+    )
     later = call(functools.partial(scan_kernel, True), parts, adjoints, ends)
     adjoint = swap(later, "seq").reshape(n, width)
-
     gate_grad = call(
         gate_kernel,
         shape((2, tokens), F32),
@@ -439,17 +771,15 @@
     )
     gate_grad = gate_grad.T.astype(BF16)
 
-    dx, dwrite, read_grad, dcum, dcumt = inside_stage(
-        mixer_input, resid_grad, write_proj, read_proj, state, cum, cumt
-    )
     input_grad, write_grad, decay_grad = call(
         last_kernel,
-        (shape((tokens, width), BF16), shape((tokens, n), F32), shape((tokens, heads), F32)),
+        (shape((tokens, width), BF16), shape((tokens, n), F32), shape((heads, tokens), F32)),
         mixer_input,
         write_proj,
         state,
         adjoint,
         cum,
+        cumt,
         dx,
         dwrite,
         dcum,
@@ -459,7 +789,7 @@
         input_grad,
         write_grad,
         read_grad,
-        decay_grad,
+        decay_grad.T,
         resid_grad,
         gate_grad,
         up_grad[None],

time: 251 us -> 243 us (0.968)
  blocking collectives: 54.9 us -> 0 us
  local copies, waits for them, and re-layouts: 7.95 us -> 53.6 us
  starting transfers between devices: 31.1 us -> 67.4 us
  matrix products: 19.1 us -> 0 us
  waiting for transfers between devices: 90.1 us -> 71.5 us
    all_to_all x1 -> x0, blocking collectives: 54.9 us -> none  [swap(): return lax.all_to_all(x, axes, split_axis=0, concat_axis=0, tiled=True)]
    all_to_all x7 -> x6, waiting for transfers between devices: 90.1 us -> 38.2 us  [swap(): return lax.all_to_all(x, axes, split_axis=0, concat_axis=0, tiled=True)]
    unnamed x21 -> x154, local copies, waits for them, and re-layouts: 5.16 us -> 49.4 us
    ppermute x0 -> x27, starting transfers between devices: none -> 42.2 us  [the longest x21 35.8 us: spread_out(): lax.ppermute(part, 'seq', [(i, i ^ x) for i in range(shard_count)])]
    ppermute x0 -> x27, waiting for transfers between devices: none -> 33.3 us  [the longest x6 25 us: across(): return lax.ppermute(x, 'grp', [(i, i ^ bit) for i in range(planes)])]
    dot_general x3 -> x0, matrix products: 19.1 us -> none  [the longest x2 11.4 us: dot(): lax.dot_general(a, b, (((ca,), (cb,)), ((), ())), precision=precision, pr...]
    pallas_call x0 -> x3, Pallas kernels: none -> 15.3 us  [grouped(): pl.pallas_call(functools.partial(kernel, len(parts)), out_shape=outs, gri...]
    pallas_call x10 -> x13, Pallas kernels: 44.4 us -> 31.2 us  [call(): pl.pallas_call(kernel, out_shape=outs, in_specs=in_specs if in_specs is n...]
  transfers between devices with their start and end apart: 7 -> 33, of which waited for: 2 -> 7; matrix products, arithmetic and copies ran while one was open for 10% -> 1% of each run, Pallas kernels for 13% -> 16%
where the time goes in v1:
time: 243 us; the launch traced here: 241 us
  waiting for transfers between devices  71.5 us (29%)
  starting transfers between devices  67.4 us (28%)
  local copies, waits for them, and re-layouts  53.6 us (22%)
  Pallas kernels  46.5 us (19%)
    unnamed x154, local copies, waits for them, and re-layouts  49.4 us
    all_to_all x6, waiting for transfers between devices, swap(): return lax.all_to_all(x, axes, split_axis=0, concat_axis=0, tiled=True)  38.2 us
    ppermute x21, starting transfers between devices, spread_out(): lax.ppermute(part, 'seq', [(i, i ^ x) for i in range(shard_count)])  35.8 us
    pallas_call x13, Pallas kernels, call(): pl.pallas_call(kernel, out_shape=outs, in_specs=in_specs if in_specs is n...  31.2 us
    all_to_all x6, starting transfers between devices, swap(): return lax.all_to_all(x, axes, split_axis=0, concat_axis=0, tiled=True)  25.3 us
    ppermute x6, waiting for transfers between devices, across(): return lax.ppermute(x, 'grp', [(i, i ^ bit) for i in range(planes)])  25 us
    pallas_call x3, Pallas kernels, grouped(): pl.pallas_call(functools.partial(kernel, len(parts)), out_shape=outs, gri...  15.3 us
    ppermute x21, waiting for transfers between devices, spread_out(): lax.ppermute(part, 'seq', [(i, i ^ x) for i in range(shard_count)])  8.31 us
  transfers between devices with their start and end apart: 33, of which 7 were waited for; matrix products, arithmetic and copies ran while one was open for 1% of the time, Pallas kernels for 16%

profile of v1, /device:TPU:1, one launch (start us, length us, event | category | flops | bytes accessed | tf_op | source)
XLA Modules:
  0.0 240.7 jit_solution(3244908233566670588)
XLA Ops:
  3.4 2.2 collective-permute-start
  5.6 2.3 collective-permute-start.1
  8.1 21.7 %collective-permute-done.refs_1_ = bf16[272,1024]{1,0:T(8,128)(2,1)S(1)} collective-permute-done((bf16[272,1024]{1,0:T(8,128)(2,1)S(1)}, bf16[272,1024]{1,0:T(8,128)(2,1)S(1)}, u32[]{:S(2)}, u32[]{:S(2)}) %collective-permute-start) | collective-permute-done | bytes 557088 | tf_op jit(solution)/shard_map/ppermute | solution.py:319
  29.8 2.4 %shard_map.162 = (bf16[96,1024]{1,0:T(8,128)(2,1)S(1)}, bf16[96,1024]{1,0:T(8,128)(2,1)S(1)}, bf16[96,1024]{1,0:T(8,128)(2,1)S(1)}, bf16[96,1024]{1,0:T(8,128)(2...) custom-call(s32[2]{0:T(128)S(1)} %pad_add_fusion.me_ref, ...), custom_call_target="tpu_custom_call" | custom-call | tf_op jit(solution)/shard_map/pallas_call | solution.py:34
  32.9 16.4 %collective-permute-start.2 = (bf16[96,1024]{1,0:T(8,128)(2,1)S(1)}, bf16[96,1024]{1,0:T(8,128)(2,1)S(1)}, u32[]{:S(2)}, u32[]{:S(2)}) collective-permute-start(bf16[96,1024]{1,0:T(8,128)(2,1)S(1)} %get-tuple-element.72), channel_id=1, source_target_pairs={{0,1},{1,0},{2,3},{3,2},{4,5},{5,4},{6,7},{7,6},{8,9},{9,8},{10,11... | collective-permute-start | bytes 589832 | tf_op jit(solution)/shard_map/ppermute | solution.py:323
  49.3 1.2 collective-permute-start.3
  50.9 3.3 %collective-permute-done.10.refs_2_ = bf16[256,1024]{1,0:T(8,128)(2,1)} collective-permute-done((bf16[256,1024]{1,0:T(8,128)(2,1)}, bf16[256,1024]{1,0:T(8,128)(2,1)}, u32[]{:S(2)}, u32[]{:S(2)}) %collective-permute-start.10) | collective-permute-done | bytes 524320 | tf_op jit(solution)/shard_map/ppermute | solution.py:319
  54.3 1.2 collective-permute-start.5
  56.2 2.2 collective-permute-start.6
  59.1 1.7 collective-permute-start.11
  60.8 2.5 %shard_map.164 = (f32[256,16]{1,0:T(8,128)S(1)}, f32[16,256]{1,0:T(8,128)S(1)}, bf16[8,32,1024]{2,1,0:T(8,128)(2,1)}) custom-call(bf16[256,1024]{1,0:T(8,128)(2,1)S(1)} %copy-done.1, bf16[256,128]{1,0:T(8,128)(2,1)S(1)} %copy-done.12, f32[16,256]{1,0:T(8,128)S(1)} %bitcast.36), custom_call_target="tpu_custom_call" | custom-call | tf_op jit(solution)/shard_map/pallas_call | solution.py:34
  63.4 3.8 %all-to-all-start = ((bf16[8,32,1024]{2,1,0:T(8,128)(2,1)}), bf16[8,32,1024]{2,1,0:T(8,128)(2,1)S(1)}, u32[]{:S(2)}, u32[]{:S(2)}) async-start(bf16[8,32,1024]{2,1,0:T(8,128)(2,1)} %get-tuple-element.80), calls=%async_computation | async-start | bytes 1048576 | tf_op jit(solution)/shard_map/all_to_all | solution.py:714
  67.9 2.3 collective-permute-start.7
  70.1 2.4 shard_map.167
  76.0 4.2 %collective-permute-done.7.refs_6_ = bf16[96,1024]{1,0:T(8,128)(2,1)S(1)} collective-permute-done((bf16[96,1024]{1,0:T(8,128)(2,1)}, bf16[96,1024]{1,0:T(8,128)(2,1)S(1)}, u32[]{:S(2)}, u32[]{:S(2)}) %collective-permute-start.7) | collective-permute-done | bytes 196640 | tf_op jit(solution)/shard_map/ppermute | solution.py:323
  81.1 4.1 %collective-permute-done.8.refs_7_ = bf16[96,1024]{1,0:T(8,128)(2,1)S(1)} collective-permute-done((bf16[96,1024]{1,0:T(8,128)(2,1)}, bf16[96,1024]{1,0:T(8,128)(2,1)S(1)}, u32[]{:S(2)}, u32[]{:S(2)}) %collective-permute-start.8) | collective-permute-done | bytes 196640 | tf_op jit(solution)/shard_map/ppermute | solution.py:323
  87.6 4.6 %all-to-all-start.1 = ((bf16[8,16,1024]{2,1,0:T(8,128)(2,1)}), bf16[8,16,1024]{2,1,0:T(8,128)(2,1)S(1)}, u32[]{:S(2)}, u32[]{:S(2)}) async-start(bf16[8,16,1024]{2,1,0:T(8,128)(2,1)} %copy-done.11), calls=%async_computation.1 | async-start | bytes 524288 | tf_op jit(solution)/shard_map/all_to_all | solution.py:714
  92.2 1.6 collective-permute-start.24
  95.1 1.5 collective-permute-start.26
  97.2 2.3 shard_map.166
  103.5 1.2 collective-permute-start.13
  110.9 4.1 %shard_map.163 = (bf16[768,1024]{1,0:T(8,128)(2,1)S(1)}, bf16[768,1024]{1,0:T(8,128)(2,1)S(1)}, f32[768,1024]{1,0:T(8,128)S(1)}) custom-call(s32[2]{0:T(128)S(1)} %copy-done.28, bf16[96,1024]{1,0:T(8,128)(2,1)S(1)} %copy-done.41, bf16[96,1024]{1,0:T(8,128)(2,1)S(1)} %copy-done.43, bf16[96,1024]{1,0:T(8,128)(2,1)S(1)} %copy-done.45, ...), custom_call_target="tpu_custom_call" | custom-call | flops 1610612736 | bytes 6291456 | tf_op jit(solution)/shard_map/pallas_call | solution.py:264
  115.0 1.7 copy-done.65
  120.0 1.4 collective-permute-start.16
  122.5 1.7 collective-permute-start.18
  124.2 1.6 copy-done.7
  125.8 1.6 copy-done.9
  129.9 1.9 copy-done.66
  131.8 1.4 copy-done.68
  133.2 7.1 %shard_map.168 = (bf16[768,1024]{1,0:T(8,128)(2,1)S(1)}, bf16[768,1024]{1,0:T(8,128)(2,1)S(1)}, bf16[4,256,1024]{2,1,0:T(8,128)(2,1)S(1)}, f32[4,8,256]{2,1,0:T(8,128)S(1)}) custom-call(s32[2]{0:T(128)S(1)} %copy-done.29, bf16[96,1024]{1,0:T(8,128)(2,1)S(1)} %copy-done.49, bf16[96,1024]{1,0:T(8,128)(2,1)S(1)} %copy-done.51, ...), custom_call_target="tpu_custom_call" | custom-call | flops 3221225472 | bytes 6291456 | tf_op jit(solution)/shard_map/pallas_call | solution.py:264
  140.5 4.1 %shard_map.169 = (bf16[256,1024]{1,0:T(8,128)(2,1)S(1)}, bf16[256,1024]{1,0:T(8,128)(2,1)S(1)}, bf16[256,1024]{1,0:T(8,128)(2,1)S(1)}, bf16[256,1024]{1,0:T(8,12...) custom-call(s32[2]{0:T(128)S(1)} %copy-done.29, ...), custom_call_target="tpu_custom_call", output_to_operand_aliasing={{4}: (11, {}), {5}: (12, {})} | custom-call | flops 1610612736 | bytes 6291456 | tf_op jit(solution)/shard_map/pallas_call | solution.py:264
  144.7 1.3 copy-done
  149.8 3.6 %all-to-all-start.2 = ((bf16[32,32,1024]{2,1,0:T(8,128)(2,1)}), bf16[32,32,1024]{2,1,0:T(8,128)(2,1)S(1)}, u32[]{:S(2)}, u32[]{:S(2)}) async-start(bf16[32,32,1024]{2,1,0:T(8,128)(2,1)} %bitcast.25), calls=%async_computation.2 | async-start | bytes 4194304 | tf_op jit(solution)/shard_map/all_to_all | solution.py:714
  153.4 1.4 fusion
  154.7 1.4 convert_element_type.11
  158.2 1.4 copy-done.69
  159.6 1.4 copy-done.73
  161.0 4.3 %shard_map.170 = bf16[1024,1024]{1,0:T(8,128)(2,1)} custom-call(bf16[768,1024]{1,0:T(8,128)(2,1)S(1)} %copy-done.69, bf16[768,1024]{1,0:T(8,128)(2,1)S(1)} %copy-done.73, bf16[256,1024]{1,0:T(8,128)(2,1)S(1)} %copy-done.37, bf16[256,1024]{1,0:T(8,128)(2,1)S(1)} %copy-done.39), custom_call_target="tpu_custom_call" | custom-call | flops 2147483648 | bytes 6291456 | tf_op jit(solution)/shard_map/pallas_call | solution.py:34
  165.4 4.3 %shard_map.171 = bf16[1024,1024]{1,0:T(8,128)(2,1)} custom-call(bf16[768,1024]{1,0:T(8,128)(2,1)S(1)} %copy-done.75, bf16[768,1024]{1,0:T(8,128)(2,1)S(1)} %copy-done.71, bf16[256,1024]{1,0:T(8,128)(2,1)S(1)} %copy-done.33, bf16[256,1024]{1,0:T(8,128)(2,1)S(1)} %copy-done.35), custom_call_target="tpu_custom_call" | custom-call | flops 2147483648 | bytes 6291456 | tf_op jit(solution)/shard_map/pallas_call | solution.py:34
  169.7 31.8 %all-to-all-done.2 = bf16[32,32,1024]{2,1,0:T(8,128)(2,1)S(1)} async-done(((bf16[32,32,1024]{2,1,0:T(8,128)(2,1)}), bf16[32,32,1024]{2,1,0:T(8,128)(2,1)S(1)}, u32[]{:S(2)}, u32[]{:S(2)}) %all-to-all-start.2) | async-done | bytes 2097184 | tf_op jit(solution)/shard_map/all_to_all | solution.py:714
  201.5 1.3 copy.21
  202.8 4.7 %all-to-all-start.3 = ((bf16[32,1,32]{2,1,0:T(2,128)(2,1)}), bf16[32,1,32]{2,1,0:T(2,128)(2,1)}, u32[]{:S(2)}, u32[]{:S(2)}) async-start(bf16[32,1,32]{2,1,0:T(2,128)(2,1)} %copy.21), calls=%async_computation.3 | async-start | bytes 32768 | tf_op jit(solution)/shard_map/all_to_all | solution.py:714
  211.2 1.9 shard_map.172
  215.1 3.9 %all-to-all-start.4 = ((bf16[8,16,1024]{2,1,0:T(8,128)(2,1)}), bf16[8,16,1024]{2,1,0:T(8,128)(2,1)S(1)}, u32[]{:S(2)}, u32[]{:S(2)}) async-start(bf16[8,16,1024]{2,1,0:T(8,128)(2,1)} %bitcast.34), calls=%async_computation.4 | async-start | bytes 524288 | tf_op jit(solution)/shard_map/all_to_all | solution.py:714
  219.0 5.7 %all-to-all-done.4.ends_ref = bf16[8,16,1024]{2,1,0:T(8,128)(2,1)S(1)} async-done(((bf16[8,16,1024]{2,1,0:T(8,128)(2,1)}), bf16[8,16,1024]{2,1,0:T(8,128)(2,1)S(1)}, u32[]{:S(2)}, u32[]{:S(2)}) %all-to-all-start.4) | async-done | bytes 262176 | tf_op jit(solution)/shard_map/all_to_all | solution.py:714
  225.5 4.5 %all-to-all-start.5 = ((bf16[8,16,1024]{2,1,0:T(8,128)(2,1)}), bf16[8,16,1024]{2,1,0:T(8,128)(2,1)S(1)}, u32[]{:S(2)}, u32[]{:S(2)}) async-start(bf16[8,16,1024]{2,1,0:T(8,128)(2,1)} %shard_map.173), calls=%async_computation.5 | async-start | bytes 524288 | tf_op jit(solution)/shard_map/all_to_all | solution.py:714
  230.1 5.8 %shard_map.174 = (f32[256,1024]{1,0:T(8,128)S(1)}, f32[256,128]{1,0:T(8,128)S(1)}, f32[256,128]{1,0:T(8,128)}, f32[256,16]{1,0:T(8,128)S(1)}, f32[16,1,256]{2,1,0:T(1,128)S(1)}) custom-call(bf16[256,1024]{1,0:T(8,128)(2,1)S(1)} %copy-done.1, bf16[256,1024]{1,0:T(8,128)(2,1)S(1)} %copy-done.31, bf16[256,128]{1,0:T(8,128)(2,1)S(1)} %copy-done.13, ...), custom_call_target="tpu_custom_call" | custom-call | flops 536870912 | bytes 2097152 | tf_op jit(solution)/shard_map/pallas_call | solution.py:34
  236.8 3.9 %shard_map.175 = (bf16[256,1024]{1,0:T(8,128)(2,1)}, f32[256,128]{1,0:T(8,128)}, f32[16,256]{1,0:T(8,128)}) custom-call(bf16[256,1024]{1,0:T(8,128)(2,1)S(1)} %copy-done.1, bf16[256,128]{1,0:T(8,128)(2,1)S(1)} %copy-done.13, bf16[128,1024]{1,0:T(8,128)(2,1)S(1)} %bitcast.32, bf16[128,1024]{1,0:T(8,128)(2,1)S(1)} %bitcast.33, ...), custom_call_target="tpu_custom_call" | custom-call | tf_op jit(solution)/shard_map/pallas_call | solution.py:34
  (196 shorter events, 45.2 us)
Async XLA Ops:
  0.6 69.5 %copy-start.2 = (bf16[256,1024]{1,0:T(8,128)(2,1)S(1)}, bf16[256,1024]{1,0:T(8,128)(2,1)}, u32[]{:S(2)}) copy-start(bf16[256,1024]{1,0:T(8,128)(2,1)} %out_grad_ref.1) | copy-start | bytes 1572868
  0.6 60.2 %copy-start.1 = (bf16[256,1024]{1,0:T(8,128)(2,1)S(1)}, bf16[256,1024]{1,0:T(8,128)(2,1)}, u32[]{:S(2)}) copy-start(bf16[256,1024]{1,0:T(8,128)(2,1)} %inputs_ref.5) | copy-start | bytes 1572868
  3.1 57.7 %copy-start.12 = (bf16[256,128]{1,0:T(8,128)(2,1)S(1)}, bf16[256,128]{1,0:T(8,128)(2,1)}, u32[]{:S(2)}) copy-start(bf16[256,128]{1,0:T(8,128)(2,1)} %writes_ref.5) | copy-start | bytes 196612
  3.2 57.7 %copy-start.20 = (f32[256,16]{0,1:T(8,128)S(1)}, f32[256,16]{0,1:T(8,128)}, u32[]{:S(2)}) copy-start(f32[256,16]{0,1:T(8,128)} %param.13) | copy-start | bytes 49156
  3.4 69.2 %copy-start.23 = (s32[2,256]{1,0:T(2,128)}, s32[2,256]{1,0:T(2,128)S(1)}, u32[]{:S(2)}) copy-start(s32[2,256]{1,0:T(2,128)S(1)} %get-tuple-element.114.targets_ref) | copy-start | bytes 6148
  3.4 26.4 %collective-permute-start = (bf16[272,1024]{1,0:T(8,128)(2,1)S(1)}, bf16[272,1024]{1,0:T(8,128)(2,1)S(1)}, u32[]{:S(2)}, u32[]{:S(2)}) collective-permute-start(bf16[272,1024]{1,0:T(8,128)(2,1)S(1)} %get-tuple-element.70.refs_0_), channel_id=1, source_target_pairs={{0,8},{8,0},{16,24},{24,16},{1,9},{9,1},{17,25},{25,17},{2,10},{10... | collective-permute-start | bytes 1671176 | tf_op jit(solution)/shard_map/ppermute | solution.py:319
  5.6 24.3 %collective-permute-start.1 = (bf16[272,1024]{1,0:T(8,128)(2,1)S(1)}, bf16[272,1024]{1,0:T(8,128)(2,1)}, u32[]{:S(2)}, u32[]{:S(2)}) collective-permute-start(bf16[272,1024]{1,0:T(8,128)(2,1)S(1)} %get-tuple-element.70.refs_0_), channel_id=1, source_target_pairs={{0,16},{8,24},{16,0},{24,8},{1,17},{9,25},{17,1},{25,9},{2,18},{10... | collective-permute-start | bytes 1671176 | tf_op jit(solution)/shard_map/ppermute | solution.py:319
  7.9 46.4 %collective-permute-start.10 = (bf16[256,1024]{1,0:T(8,128)(2,1)}, bf16[256,1024]{1,0:T(8,128)(2,1)}, u32[]{:S(2)}, u32[]{:S(2)}) collective-permute-start(bf16[256,1024]{1,0:T(8,128)(2,1)} %out_grad_ref.1), channel_id=1, source_target_pairs={{0,16},{8,24},{16,0},{24,8},{1,17},{9,25},{17,1},{25,9},{2,18},{10... | collective-permute-start | bytes 1572872 | tf_op jit(solution)/shard_map/ppermute | solution.py:319
  7.9 46.4 %collective-permute-start.19 = (bf16[256,1024]{1,0:T(8,128)(2,1)}, bf16[256,1024]{1,0:T(8,128)(2,1)S(1)}, u32[]{:S(2)}, u32[]{:S(2)}) collective-permute-start(bf16[256,1024]{1,0:T(8,128)(2,1)} %out_grad_ref.1), channel_id=1, source_target_pairs={{0,8},{8,0},{16,24},{24,16},{1,9},{9,1},{17,25},{25,17},{2,10},{10... | collective-permute-start | bytes 1572872 | tf_op jit(solution)/shard_map/ppermute | solution.py:319
  8.1 64.4 %copy-start.26 = (s32[2]{0:T(128)}, s32[2]{0:T(128)S(1)}, u32[]{:S(2)}) copy-start(s32[2]{0:T(128)S(1)} %pad_add_fusion.me_ref) | copy-start | bytes 28
  32.9 30.4 %copy-start.40 = (bf16[96,1024]{1,0:T(8,128)(2,1)}, bf16[96,1024]{1,0:T(8,128)(2,1)S(1)}, u32[]{:S(2)}) copy-start(bf16[96,1024]{1,0:T(8,128)(2,1)S(1)} %get-tuple-element.71.refs_0_) | copy-start | bytes 589828
  32.9 22.6 %collective-permute-start.2 = (bf16[96,1024]{1,0:T(8,128)(2,1)S(1)}, bf16[96,1024]{1,0:T(8,128)(2,1)S(1)}, u32[]{:S(2)}, u32[]{:S(2)}) collective-permute-start(bf16[96,1024]{1,0:T(8,128)(2,1)S(1)} %get-tuple-element.72), channel_id=1, source_target_pairs={{0,1},{1,0},{2,3},{3,2},{4,5},{5,4},{6,7},{7,6},{8,9},{9,8},{10,11... | collective-permute-start | bytes 589832 | tf_op jit(solution)/shard_map/ppermute | solution.py:323
  49.3 9.1 %collective-permute-start.3 = (bf16[96,1024]{1,0:T(8,128)(2,1)S(1)}, bf16[96,1024]{1,0:T(8,128)(2,1)S(1)}, u32[]{:S(2)}, u32[]{:S(2)}) collective-permute-start(bf16[96,1024]{1,0:T(8,128)(2,1)S(1)} %get-tuple-element.73), channel_id=1, source_target_pairs={{0,2},{1,3},{2,0},{3,1},{4,6},{5,7},{6,4},{7,5},{8,10},{9,11},{10,... | collective-permute-start | bytes 589832 | tf_op jit(solution)/shard_map/ppermute | solution.py:323
  50.5 16.7 %collective-permute-start.4 = (bf16[96,1024]{1,0:T(8,128)(2,1)S(1)}, bf16[96,1024]{1,0:T(8,128)(2,1)S(1)}, u32[]{:S(2)}, u32[]{:S(2)}) collective-permute-start(bf16[96,1024]{1,0:T(8,128)(2,1)S(1)} %get-tuple-element.74), channel_id=1, source_target_pairs={{0,3},{1,2},{2,1},{3,0},{4,7},{5,6},{6,5},{7,4},{8,11},{9,10},{10,... | collective-permute-start | bytes 589832 | tf_op jit(solution)/shard_map/ppermute | solution.py:323
  54.3 40.8 %collective-permute-start.9 = (bf16[272,1024]{1,0:T(8,128)(2,1)}, bf16[272,1024]{1,0:T(8,128)(2,1)}, u32[]{:S(2)}, u32[]{:S(2)}) collective-permute-start(bf16[272,1024]{1,0:T(8,128)(2,1)} %collective-permute-done.1.refs_2_), channel_id=1, source_target_pairs={{0,8},{8,0},{16,24},{24,16},{1,9},{9,1},{17,25},{25,17},{2,10},{10... | collective-permute-start | bytes 1671176 | tf_op jit(solution)/shard_map/ppermute | solution.py:319
  54.3 20.9 %collective-permute-start.5 = (bf16[96,1024]{1,0:T(8,128)(2,1)}, bf16[96,1024]{1,0:T(8,128)(2,1)}, u32[]{:S(2)}, u32[]{:S(2)}) collective-permute-start(bf16[96,1024]{1,0:T(8,128)(2,1)} %get-tuple-element.75), channel_id=1, source_target_pairs={{0,4},{1,5},{2,6},{3,7},{4,0},{5,1},{6,2},{7,3},{8,12},{9,13},{10,... | collective-permute-start | bytes 589832 | tf_op jit(solution)/shard_map/ppermute | solution.py:323
  56.2 19.3 %collective-permute-start.6 = (bf16[96,1024]{1,0:T(8,128)(2,1)}, bf16[96,1024]{1,0:T(8,128)(2,1)}, u32[]{:S(2)}, u32[]{:S(2)}) collective-permute-start(bf16[96,1024]{1,0:T(8,128)(2,1)} %get-tuple-element.76), channel_id=1, source_target_pairs={{0,5},{1,4},{2,7},{3,6},{4,1},{5,0},{6,3},{7,2},{8,13},{9,12},{10,... | collective-permute-start | bytes 589832 | tf_op jit(solution)/shard_map/ppermute | solution.py:323
  59.1 34.8 %collective-permute-start.11 = (bf16[256,1024]{1,0:T(8,128)(2,1)}, bf16[256,1024]{1,0:T(8,128)(2,1)}, u32[]{:S(2)}, u32[]{:S(2)}) collective-permute-start(bf16[256,1024]{1,0:T(8,128)(2,1)} %collective-permute-done.10.refs_2_), channel_id=1, source_target_pairs={{0,8},{8,0},{16,24},{24,16},{1,9},{9,1},{17,25},{25,17},{2,10},{10... | collective-permute-start | bytes 1572872 | tf_op jit(solution)/shard_map/ppermute | solution.py:319
  63.4 23.5 %all-to-all-start = ((bf16[8,32,1024]{2,1,0:T(8,128)(2,1)}), bf16[8,32,1024]{2,1,0:T(8,128)(2,1)S(1)}, u32[]{:S(2)}, u32[]{:S(2)}) async-start(bf16[8,32,1024]{2,1,0:T(8,128)(2,1)} %get-tuple-element.80), calls=%async_computation | async-start | bytes 1048576 | tf_op jit(solution)/shard_map/all_to_all | solution.py:714
  67.9 12.3 %collective-permute-start.7 = (bf16[96,1024]{1,0:T(8,128)(2,1)}, bf16[96,1024]{1,0:T(8,128)(2,1)S(1)}, u32[]{:S(2)}, u32[]{:S(2)}) collective-permute-start(bf16[96,1024]{1,0:T(8,128)(2,1)} %get-tuple-element.77), channel_id=1, source_target_pairs={{0,6},{1,7},{2,4},{3,5},{4,2},{5,3},{6,0},{7,1},{8,14},{9,15},{10,... | collective-permute-start | bytes 589832 | tf_op jit(solution)/shard_map/ppermute | solution.py:323
  75.2 29.5 %copy-start.6 = (bf16[1,1024,1024]{2,1,0:T(8,128)(2,1)S(1)}, bf16[1,1024,1024]{2,1,0:T(8,128)(2,1)}, u32[]{:S(2)}) copy-start(bf16[1,1024,1024]{2,1,0:T(8,128)(2,1)} %param.18) | copy-start | bytes 6291460
  75.2 10.0 %collective-permute-start.8 = (bf16[96,1024]{1,0:T(8,128)(2,1)}, bf16[96,1024]{1,0:T(8,128)(2,1)S(1)}, u32[]{:S(2)}, u32[]{:S(2)}) collective-permute-start(bf16[96,1024]{1,0:T(8,128)(2,1)} %copy-done.59), channel_id=1, source_target_pairs={{0,7},{1,6},{2,5},{3,4},{4,3},{5,2},{6,1},{7,0},{8,15},{9,14},{10,... | collective-permute-start | bytes 589832 | tf_op jit(solution)/shard_map/ppermute | solution.py:323
  75.5 10.4 %collective-permute-start.20 = (bf16[96,1024]{1,0:T(8,128)(2,1)S(1)}, bf16[96,1024]{1,0:T(8,128)(2,1)S(1)}, u32[]{:S(2)}, u32[]{:S(2)}) collective-permute-start(bf16[96,1024]{1,0:T(8,128)(2,1)S(1)} %get-tuple-element.92), channel_id=1, source_target_pairs={{0,1},{1,0},{2,3},{3,2},{4,5},{5,4},{6,7},{7,6},{8,9},{9,8},{10,11... | collective-permute-start | bytes 589832 | tf_op jit(solution)/shard_map/ppermute | solution.py:323
  80.8 11.4 %collective-permute-start.21 = (bf16[96,1024]{1,0:T(8,128)(2,1)}, bf16[96,1024]{1,0:T(8,128)(2,1)}, u32[]{:S(2)}, u32[]{:S(2)}) collective-permute-start(bf16[96,1024]{1,0:T(8,128)(2,1)} %get-tuple-element.93), channel_id=1, source_target_pairs={{0,2},{1,3},{2,0},{3,1},{4,6},{5,7},{6,4},{7,5},{8,10},{9,11},{10,... | collective-permute-start | bytes 589832 | tf_op jit(solution)/shard_map/ppermute | solution.py:323
  85.9 17.5 %collective-permute-start.22 = (bf16[96,1024]{1,0:T(8,128)(2,1)}, bf16[96,1024]{1,0:T(8,128)(2,1)}, u32[]{:S(2)}, u32[]{:S(2)}) collective-permute-start(bf16[96,1024]{1,0:T(8,128)(2,1)} %get-tuple-element.94), channel_id=1, source_target_pairs={{0,3},{1,2},{2,1},{3,0},{4,7},{5,6},{6,5},{7,4},{8,11},{9,10},{10,... | collective-permute-start | bytes 589832 | tf_op jit(solution)/shard_map/ppermute | solution.py:323
  86.6 17.0 %collective-permute-start.23 = (bf16[96,1024]{1,0:T(8,128)(2,1)}, bf16[96,1024]{1,0:T(8,128)(2,1)}, u32[]{:S(2)}, u32[]{:S(2)}) collective-permute-start(bf16[96,1024]{1,0:T(8,128)(2,1)} %get-tuple-element.95), channel_id=1, source_target_pairs={{0,4},{1,5},{2,6},{3,7},{4,0},{5,1},{6,2},{7,3},{8,12},{9,13},{10,... | collective-permute-start | bytes 589832 | tf_op jit(solution)/shard_map/ppermute | solution.py:323
  87.6 31.4 %all-to-all-start.1 = ((bf16[8,16,1024]{2,1,0:T(8,128)(2,1)}), bf16[8,16,1024]{2,1,0:T(8,128)(2,1)S(1)}, u32[]{:S(2)}, u32[]{:S(2)}) async-start(bf16[8,16,1024]{2,1,0:T(8,128)(2,1)} %copy-done.11), calls=%async_computation.1 | async-start | bytes 524288 | tf_op jit(solution)/shard_map/all_to_all | solution.py:714
  92.2 26.7 %collective-permute-start.24 = (bf16[96,1024]{1,0:T(8,128)(2,1)}, bf16[96,1024]{1,0:T(8,128)(2,1)}, u32[]{:S(2)}, u32[]{:S(2)}) collective-permute-start(bf16[96,1024]{1,0:T(8,128)(2,1)} %copy-done.54), channel_id=1, source_target_pairs={{0,5},{1,4},{2,7},{3,6},{4,1},{5,0},{6,3},{7,2},{8,13},{9,12},{10,... | collective-permute-start | bytes 589832 | tf_op jit(solution)/shard_map/ppermute | solution.py:323
  93.9 26.0 %collective-permute-start.25 = (bf16[96,1024]{1,0:T(8,128)(2,1)}, bf16[96,1024]{1,0:T(8,128)(2,1)}, u32[]{:S(2)}, u32[]{:S(2)}) collective-permute-start(bf16[96,1024]{1,0:T(8,128)(2,1)} %copy-done.53), channel_id=1, source_target_pairs={{0,6},{1,7},{2,4},{3,5},{4,2},{5,3},{6,0},{7,1},{8,14},{9,15},{10,... | collective-permute-start | bytes 589832 | tf_op jit(solution)/shard_map/ppermute | solution.py:323
  95.1 24.9 %collective-permute-start.26 = (bf16[96,1024]{1,0:T(8,128)(2,1)}, bf16[96,1024]{1,0:T(8,128)(2,1)}, u32[]{:S(2)}, u32[]{:S(2)}) collective-permute-start(bf16[96,1024]{1,0:T(8,128)(2,1)} %copy-done.52), channel_id=1, source_target_pairs={{0,7},{1,6},{2,5},{3,4},{4,3},{5,2},{6,1},{7,0},{8,15},{9,14},{10,... | collective-permute-start | bytes 589832 | tf_op jit(solution)/shard_map/ppermute | solution.py:323
  103.4 18.0 %collective-permute-start.12 = (bf16[64,1024]{1,0:T(8,128)(2,1)}, bf16[64,1024]{1,0:T(8,128)(2,1)}, u32[]{:S(2)}, u32[]{:S(2)}) collective-permute-start(bf16[64,1024]{1,0:T(8,128)(2,1)} %get-tuple-element.83), channel_id=1, source_target_pairs={{0,1},{1,0},{2,3},{3,2},{4,5},{5,4},{6,7},{7,6},{8,9},{9,8},{10,11... | collective-permute-start | bytes 393224 | tf_op jit(solution)/shard_map/ppermute | solution.py:323
  103.5 19.0 %collective-permute-start.13 = (bf16[64,1024]{1,0:T(8,128)(2,1)}, bf16[64,1024]{1,0:T(8,128)(2,1)}, u32[]{:S(2)}, u32[]{:S(2)}) collective-permute-start(bf16[64,1024]{1,0:T(8,128)(2,1)} %get-tuple-element.84), channel_id=1, source_target_pairs={{0,2},{1,3},{2,0},{3,1},{4,6},{5,7},{6,4},{7,5},{8,10},{9,11},{10,... | collective-permute-start | bytes 393224 | tf_op jit(solution)/shard_map/ppermute | solution.py:323
  119.0 21.4 %collective-permute-start.14 = (bf16[64,1024]{1,0:T(8,128)(2,1)}, bf16[64,1024]{1,0:T(8,128)(2,1)S(1)}, u32[]{:S(2)}, u32[]{:S(2)}) collective-permute-start(bf16[64,1024]{1,0:T(8,128)(2,1)} %copy-done.64), channel_id=1, source_target_pairs={{0,3},{1,2},{2,1},{3,0},{4,7},{5,6},{6,5},{7,4},{8,11},{9,10},{10,... | collective-permute-start | bytes 393224 | tf_op jit(solution)/shard_map/ppermute | solution.py:323
  119.8 20.6 %collective-permute-start.15 = (bf16[64,1024]{1,0:T(8,128)(2,1)}, bf16[64,1024]{1,0:T(8,128)(2,1)S(1)}, u32[]{:S(2)}, u32[]{:S(2)}) collective-permute-start(bf16[64,1024]{1,0:T(8,128)(2,1)} %copy-done.63), channel_id=1, source_target_pairs={{0,4},{1,5},{2,6},{3,7},{4,0},{5,1},{6,2},{7,3},{8,12},{9,13},{10,... | collective-permute-start | bytes 393224 | tf_op jit(solution)/shard_map/ppermute | solution.py:323
  120.0 20.5 %collective-permute-start.16 = (bf16[64,1024]{1,0:T(8,128)(2,1)}, bf16[64,1024]{1,0:T(8,128)(2,1)S(1)}, u32[]{:S(2)}, u32[]{:S(2)}) collective-permute-start(bf16[64,1024]{1,0:T(8,128)(2,1)} %copy-done.62), channel_id=1, source_target_pairs={{0,5},{1,4},{2,7},{3,6},{4,1},{5,0},{6,3},{7,2},{8,13},{9,12},{10,... | collective-permute-start | bytes 393224 | tf_op jit(solution)/shard_map/ppermute | solution.py:323
  121.4 19.1 %collective-permute-start.17 = (bf16[64,1024]{1,0:T(8,128)(2,1)}, bf16[64,1024]{1,0:T(8,128)(2,1)S(1)}, u32[]{:S(2)}, u32[]{:S(2)}) collective-permute-start(bf16[64,1024]{1,0:T(8,128)(2,1)} %copy-done.61), channel_id=1, source_target_pairs={{0,6},{1,7},{2,4},{3,5},{4,2},{5,3},{6,0},{7,1},{8,14},{9,15},{10,... | collective-permute-start | bytes 393224 | tf_op jit(solution)/shard_map/ppermute | solution.py:323
  122.5 18.0 %collective-permute-start.18 = (bf16[64,1024]{1,0:T(8,128)(2,1)}, bf16[64,1024]{1,0:T(8,128)(2,1)S(1)}, u32[]{:S(2)}, u32[]{:S(2)}) collective-permute-start(bf16[64,1024]{1,0:T(8,128)(2,1)} %copy-done.60), channel_id=1, source_target_pairs={{0,7},{1,6},{2,5},{3,4},{4,3},{5,2},{6,1},{7,0},{8,15},{9,14},{10,... | collective-permute-start | bytes 393224 | tf_op jit(solution)/shard_map/ppermute | solution.py:323
  133.2 7.2 %copy-start.10 = (bf16[1,1024,1024]{2,1,0:T(8,128)(2,1)S(1)}, bf16[1,1024,1024]{2,1,0:T(8,128)(2,1)}, u32[]{:S(2)}) copy-start(bf16[1,1024,1024]{2,1,0:T(8,128)(2,1)} %param.19) | copy-start | bytes 6291460
  133.2 7.2 %copy-start.16 = (bf16[64,1024]{1,0:T(8,128)(2,1)S(1)}, bf16[64,1024]{1,0:T(8,128)(2,1)}, u32[]{:S(2)}) copy-start(bf16[64,1024]{1,0:T(8,128)(2,1)} %copy-done.15) | copy-start | bytes 393220
  149.8 51.8 %all-to-all-start.2 = ((bf16[32,32,1024]{2,1,0:T(8,128)(2,1)}), bf16[32,32,1024]{2,1,0:T(8,128)(2,1)S(1)}, u32[]{:S(2)}, u32[]{:S(2)}) async-start(bf16[32,32,1024]{2,1,0:T(8,128)(2,1)} %bitcast.25), calls=%async_computation.2 | async-start | bytes 4194304 | tf_op jit(solution)/shard_map/all_to_all | solution.py:714
  202.8 11.5 %all-to-all-start.3 = ((bf16[32,1,32]{2,1,0:T(2,128)(2,1)}), bf16[32,1,32]{2,1,0:T(2,128)(2,1)}, u32[]{:S(2)}, u32[]{:S(2)}) async-start(bf16[32,1,32]{2,1,0:T(2,128)(2,1)} %copy.21), calls=%async_computation.3 | async-start | bytes 32768 | tf_op jit(solution)/shard_map/all_to_all | solution.py:714
  213.7 16.3 %copy-start.13 = (bf16[256,128]{1,0:T(8,128)(2,1)S(1)}, bf16[256,128]{1,0:T(8,128)(2,1)}, u32[]{:S(2)}) copy-start(bf16[256,128]{1,0:T(8,128)(2,1)} %writes_ref.5) | copy-start | bytes 196612
  213.7 16.3 %copy-start.18 = (bf16[256,128]{1,0:T(8,128)(2,1)S(1)}, bf16[256,128]{1,0:T(8,128)(2,1)}, u32[]{:S(2)}) copy-start(bf16[256,128]{1,0:T(8,128)(2,1)} %reads_ref.3) | copy-start | bytes 196612
  213.7 16.3 %copy-start.31 = (bf16[256,1024]{1,0:T(8,128)(2,1)S(1)}, bf16[256,1024]{1,0:T(8,128)(2,1)}, u32[]{:S(2)}) copy-start(bf16[256,1024]{1,0:T(8,128)(2,1)} %get-tuple-element.66.grads_ref) | copy-start | bytes 1572868
  215.1 20.9 %copy-start.22 = (f32[256,2]{0,1:T(2,128)S(1)}, f32[256,2]{0,1:T(2,128)}, u32[]{:S(2)}) copy-start(f32[256,2]{0,1:T(2,128)} %param.16) | copy-start | bytes 6148
  215.1 20.9 %copy-start.25 = (s32[2,256]{1,0:T(2,128)S(1)}, s32[2,256]{1,0:T(2,128)}, u32[]{:S(2)}) copy-start(s32[2,256]{1,0:T(2,128)} %copy-done.23) | copy-start | bytes 6148
  215.1 9.6 %all-to-all-start.4 = ((bf16[8,16,1024]{2,1,0:T(8,128)(2,1)}), bf16[8,16,1024]{2,1,0:T(8,128)(2,1)S(1)}, u32[]{:S(2)}, u32[]{:S(2)}) async-start(bf16[8,16,1024]{2,1,0:T(8,128)(2,1)} %bitcast.34), calls=%async_computation.4 | async-start | bytes 524288 | tf_op jit(solution)/shard_map/all_to_all | solution.py:714
  225.5 11.3 %all-to-all-start.5 = ((bf16[8,16,1024]{2,1,0:T(8,128)(2,1)}), bf16[8,16,1024]{2,1,0:T(8,128)(2,1)S(1)}, u32[]{:S(2)}, u32[]{:S(2)}) async-start(bf16[8,16,1024]{2,1,0:T(8,128)(2,1)} %shard_map.173), calls=%async_computation.5 | async-start | bytes 524288 | tf_op jit(solution)/shard_map/all_to_all | solution.py:714
  (61 other events, 81.8 us)

commit v2 on v1

--- a/solution.py
+++ b/solution.py
@@ -9,7 +9,6 @@
 
 
 EPSILON = 1e-06
-HIGHEST = lax.Precision.HIGHEST
 F32 = jnp.float32
 BF16 = jnp.bfloat16
 VMEM_LIMIT = 20 * 1024 * 1024
@@ -45,8 +44,51 @@
     )(*args)
 
 
+def pieces_of(x, count):
+    parts = []
+    for _ in range(count):
+        part = x.astype(BF16)
+        parts.append(part)
+        x = x - part.astype(F32)
+    return parts
+
+
+def fine_dot(a, exact, ca, cb, count):
+    return sum(dot(part, exact, ca, cb) for part in pieces_of(a, count))
+
+
 def shape(dims, dtype):
     return jax.ShapeDtypeStruct(dims, dtype)
+
+
+def far_shape(dims, dtype):
+    return pltpu.HBM(dims, dtype)
+
+
+def from_hbm(*arrays):
+    return [pltpu.with_memory_space_constraint(x, pltpu.HBM) for x in arrays]
+
+
+def one_step(dims):
+    return pl.BlockSpec(dims, lambda i: (0,) * len(dims))
+
+
+def streamed(kernel, outs, *args, near=(), scalars=None):
+    fixed = [x if k in near else from_hbm(x)[0] for k, x in enumerate(args)]
+    specs = [one_step(x.shape) for x in args]
+    if scalars is not None:
+        fixed = [scalars] + fixed
+        specs = [pl.BlockSpec(memory_space=pltpu.SMEM)] + specs
+    many = isinstance(outs, (tuple, list))
+    blocks = tuple(one_step(out.shape) for out in outs) if many else one_step(outs.shape)
+    return call(
+        kernel,
+        outs,
+        *fixed,
+        grid=(1,),
+        in_specs=specs,
+        out_specs=blocks,
+    )
 
 
 def one_hot(targets, slots):
@@ -241,7 +283,8 @@
 
 def routed_kernel(count, me_ref, *refs):
     parts = refs[:count]
-    act_ref, slope_ref, up_ref, down_ref, scaled_ref, pre_ref, row_ref, term_ref = refs[count:]
+    act_ref, slope_ref, up_ref, down_ref = refs[count : count + 4]
+    scaled_ref, pre_ref, row_ref, term_ref = refs[-4:]
     scaled = gather_group(me_ref, parts, scaled_ref)
     backward_group(
         scaled, act_ref[...], slope_ref[...], up_ref, down_ref, pre_ref, row_ref, term_ref
@@ -257,6 +300,39 @@
     act_ref[...] = act
     scaled = gather_group(me_ref, [part.at[cap:, :] for part in refs[:count]], scaled_ref)
     backward_group(scaled, act, slope, up_ref, down_ref, pre_ref, row_ref, term_ref)
+
+
+def mix_kernel(planes, cap, me_ref, *refs):
+    blocks, outs = refs[:planes], refs[planes:]
+    group = blocks[0].shape[1]
+    table = jnp.concatenate(
+        [block[0:1, :] for block in blocks] + [jnp.zeros((8 - planes, group), F32)], axis=0
+    )
+    for x, out in enumerate(outs):
+        place, lane = iota((group, 128), 0), iota((group, 128), 1)
+        take = (place == (me_ref[1] ^ x) * cap + lane) & (lane < cap)
+        out[...] = fine_dot(table, jnp.where(take, 1.0, 0.0).astype(BF16), 1, 0, 2)
+
+
+def found_kernel(cap, shard_count, me_ref, targets_ref, gates_ref, *refs):
+    tables, out_ref = refs[:-1], refs[-1]
+    targets = targets_ref[...].astype(F32)
+    expert = jnp.floor((targets + 0.5) * (1.0 / cap))
+    rank = (targets - expert * cap).astype(jnp.int32)
+    plane = jnp.floor((expert + 0.5) * (1.0 / shard_count))
+    shard = (expert - plane * shard_count).astype(jnp.int32)
+    row = (shard ^ me_ref[1]) * 8 + (plane.astype(jnp.int32) ^ me_ref[0])
+    table = jnp.concatenate([ref[...] for ref in tables], axis=0)
+    gates = gates_ref[...].astype(BF16).astype(F32)
+    tokens = targets.shape[1]
+    found = []
+    for k in range(2):
+        hit = iota((table.shape[0], tokens), 0) == row[k : k + 1, :]
+        hit = jnp.where(hit, 1.0, 0.0).astype(BF16)
+        values = fine_dot(table, hit, 0, 0, 2)
+        mine = iota(values.shape, 0) == rank[k : k + 1, :]
+        found.append(jnp.sum(jnp.where(mine, values, 0.0), axis=0, keepdims=True))
+    out_ref[...] = jnp.concatenate(found, axis=0) / gates
 
 
 def grouped(kernel, me, parts, each, extras, extra_specs, outs, out_specs, steps, aliases, flops):
@@ -275,30 +351,29 @@
         cost_estimate=pl.CostEstimate(
             flops=flops, bytes_accessed=6 * width * width, transcendentals=0
         ),
-    )(me, *parts, *extras)
-
-
-def outer_kernel(a1_ref, b1_ref, a2_ref, b2_ref, out_ref):
-    out_ref[...] = (
-        dot(a1_ref[...], b1_ref[...], 0, 0) + dot(a2_ref[...], b2_ref[...], 0, 0)
-    ).astype(BF16)
-
-
-def outer_stage(a1, b1, a2, b2):
-    left, right = a1.shape[1], b1.shape[1]
+    )(me, *from_hbm(*parts), *extras)
+
+
+def outer_kernel(*refs):
+    pairs, out_ref = zip(refs[0:-1:2], refs[1:-1:2]), refs[-1]
+    out_ref[...] = sum(dot(a[...], b[...], 0, 0) for a, b in pairs).astype(BF16)
+
+
+def outer_stage(*pairs):
+    left, right = pairs[0][0].shape[1], pairs[0][1].shape[1]
     tile = min(256, right)
-    whole = pl.BlockSpec(memory_space=pltpu.VMEM)
     column = lambda b: pl.BlockSpec((b.shape[0], tile), lambda i: (0, i))
-    rows = a1.shape[0] + a2.shape[0]
+    specs, args = [], []
+    for a, b in pairs:
+        specs += [one_step(a.shape), column(b)]
+        args += from_hbm(a, b)
+    rows = sum(a.shape[0] for a, _ in pairs)
     return call(
         outer_kernel,
-        shape((left, right), BF16),
-        a1,
-        b1,
-        a2,
-        b2,
+        far_shape((left, right), BF16),
+        *args,
         grid=(right // tile,),
-        in_specs=[whole, column(b1), whole, column(b2)],
+        in_specs=specs,
         out_specs=pl.BlockSpec((left, tile), lambda i: (0, i)),
         cost=pl.CostEstimate(
             flops=2 * rows * left * right, bytes_accessed=6 * left * right, transcendentals=0
@@ -328,20 +403,25 @@
 
     def pick_rows(messages):
         count = len(messages)
-        outs = [shape((count * cap, width), BF16)] * shard_count
-        *parts, keys = call(
+        outs = [far_shape((count * cap, width), BF16)] * shard_count
+        *parts, keys = streamed(
             functools.partial(pick_rows_kernel, count, cap),
-            tuple(outs + [shape((count, 8, tokens), F32)]),
-            me,
+            tuple(outs + [far_shape((count, 8, tokens), F32)]),
             *messages,
-            in_specs=[smem] + [vmem] * count,
+            scalars=me,
         )
         return parts, keys
 
     def pick_grads(keys, grads):
         count = len(grads)
-        outs = [shape((count * cap, width), BF16)] * shard_count
-        return call(functools.partial(pick_grads_kernel, count, cap), tuple(outs), keys, *grads)
+        outs = [far_shape((count * cap, width), BF16)] * shard_count
+        kernel = functools.partial(pick_grads_kernel, count, cap)
+        return streamed(kernel, tuple(outs), keys, *grads)
+
+    def pick_both(message, grad):
+        outs = [far_shape((2 * cap, width), BF16)] * shard_count
+        kernel = functools.partial(pick_both_kernel, cap)
+        return streamed(kernel, tuple(outs), message, grad, scalars=me)
 
     def block(width):
         return pl.BlockSpec((group, width), lambda i, me: (i, 0))
@@ -355,60 +435,64 @@
             cap,
             (up,),
             [vmem],
-            (shape((rows, width), BF16), shape((rows, hidden), BF16), shape((rows, hidden), F32)),
+            (far_shape((rows, width), BF16), far_shape((rows, hidden), BF16), shape((rows, hidden), F32)),
             (block(width), block(hidden), block(hidden)),
             steps,
             {},
             2 * rows * width * hidden,
         )
 
-    rows_of = lambda steps, size, dtype: shape((steps * group, size), dtype)
-    backs = (shape((planes, group, width), BF16), shape((planes, 8, group), F32))
+    rows_of = lambda steps, size, dtype: far_shape((steps * group, size), dtype)
+
+    def backs(steps):
+        return (far_shape((planes, group, width), BF16), far_shape((steps, 8, group), F32))
 
     def back_blocks(base):
-        to_plane = lambda i, me: (me[0] ^ (base + i), 0, 0)
-        return (pl.BlockSpec((1, group, width), to_plane), pl.BlockSpec((1, 8, group), to_plane))
-
-    def routed_stage(parts, act, slope, steps):
+        return (
+            pl.BlockSpec((1, group, width), lambda i, me: (me[0] ^ (base + i), 0, 0)),
+            pl.BlockSpec((1, 8, group), lambda i, me: (i, 0, 0)),
+        )
+
+    def routed_stage(parts, act, slope, steps, base, filled):
         return grouped(
             routed_kernel,
             me,
             parts,
             cap,
-            (act, slope, up, down),
-            [block(hidden), block(hidden), vmem, vmem],
-            (rows_of(steps, width, BF16), rows_of(steps, hidden, BF16)) + backs,
-            (block(width), block(hidden)) + back_blocks(0),
+            (act, slope, up, down, filled),
+            [block(hidden), block(hidden), vmem, vmem, pl.BlockSpec(memory_space=pl.ANY)],
+            (rows_of(steps, width, BF16), rows_of(steps, hidden, BF16)) + backs(steps),
+            (block(width), block(hidden)) + back_blocks(base),
             steps,
-            {},
+            {1 + len(parts) + 4: 2},
             4 * steps * group * width * hidden,
         )
 
-    def far_stage(parts, filled):
-        first = 1 + len(parts) + 2
+    def whole_stage(parts, base, filled):
+        extra = () if filled is None else (filled,)
         return grouped(
             far_kernel,
             me,
             parts,
             2 * cap,
-            (up, down) + tuple(filled),
-            [vmem, vmem] + [pl.BlockSpec(memory_space=pl.ANY)] * 2,
+            (up, down) + extra,
+            [vmem, vmem] + [pl.BlockSpec(memory_space=pl.ANY)] * len(extra),
             (
                 rows_of(1, width, BF16),
                 rows_of(1, hidden, BF16),
                 rows_of(1, width, BF16),
                 rows_of(1, hidden, BF16),
             )
-            + backs,
-            (block(width), block(hidden), block(width), block(hidden)) + back_blocks(3),
+            + backs(1),
+            (block(width), block(hidden), block(width), block(hidden)) + back_blocks(base),
             1,
-            {first: 4, first + 1: 5},
+            {1 + len(parts) + 2: 4} if extra else {},
             6 * group * width * hidden,
         )
 
-    message, targets = call(
+    message, targets = streamed(
         functools.partial(message_kernel, planes, shard_count, cap),
-        (shape((tokens + 16, width), BF16), shape((2, tokens), jnp.int32)),
+        (far_shape((tokens + 16, width), BF16), far_shape((2, tokens), jnp.int32)),
         resid,
         ids,
         gates,
@@ -418,29 +502,49 @@
     grad2 = across(out_grad, 2)
     grad1 = across(out_grad, 1)
     message3 = across(message2, 1)
-    near_rows, near_keys = pick_rows([message, message1, message2])
+    own = pick_both(message, out_grad)
+    own = spread_out(own)
+    rows_0, act_0, scaled_0, pre_0, row_grad, own_terms = whole_stage(own, 0, None)
+    near_rows, near_keys = pick_rows([message1, message2])
     near_rows = spread_out(near_rows)
+    arrived, early = lax.optimization_barrier((near_rows[1], early))
+    near_rows[1] = arrived
     grad3 = across(grad2, 1)
-    near_grads = pick_grads(near_keys, [out_grad, grad1, grad2])
+    near_grads = pick_grads(near_keys, [grad1, grad2])
     near_grads = spread_out(near_grads)
-    rows_a, act_a, slope_a = hidden_stage(near_rows, 3)
-    far = call(
-        functools.partial(pick_both_kernel, cap),
-        tuple([shape((2 * cap, width), BF16)] * shard_count),
-        me,
-        message3,
-        grad3,
-        in_specs=[smem, vmem, vmem],
-    )
+    rows_1, act_1, slope_1 = hidden_stage(near_rows, 2)
+    far = pick_both(message3, grad3)
     far = spread_out(far)
-    act_a, early = lax.optimization_barrier((act_a, early))
-    scaled_a, pre_a, row_grad, term = routed_stage(near_grads, act_a, slope_a, 3)
-    rows_b, act_b, scaled_b, pre_b, row_grad, term = far_stage(far, (row_grad, term))
-    pieces = lambda: (
-        outer_stage(act_a, scaled_a, act_b, scaled_b),
-        outer_stage(rows_a, pre_a, rows_b, pre_b),
-    )
-    return targets, row_grad.reshape(-1, width), term[:, 0, :], pieces, early
+    scaled_1, pre_1, row_grad, near_terms = routed_stage(near_grads, act_1, slope_1, 2, 1, row_grad)
+    rows_2, act_2, scaled_2, pre_2, row_grad, far_terms = whole_stage(far, 3, row_grad)
+
+    def finish():
+        blocks = [own_terms[0]]
+        blocks += [across(near_terms[bit - 1], bit) for bit in (1, 2)]
+        blocks += [across(far_terms[0], 3)]
+        mixed = call(
+            functools.partial(mix_kernel, planes, cap),
+            tuple([shape((8, 128), F32)] * shard_count),
+            me,
+            *blocks,
+            in_specs=[smem] + [vmem] * planes,
+        )
+        down_grad = outer_stage((act_0, scaled_0), (act_1, scaled_1), (act_2, scaled_2))
+        mixed = spread_out(mixed)
+        up_grad = outer_stage((rows_0, pre_0), (rows_1, pre_1), (rows_2, pre_2))
+        gate_grad = call(
+            functools.partial(found_kernel, cap, shard_count),
+            far_shape((2, tokens), F32),
+            me,
+            targets,
+            gates,
+            *mixed,
+            in_specs=[smem] + [vmem] * (2 + shard_count),
+            out_specs=vmem,
+        )
+        return down_grad, up_grad, gate_grad
+
+    return targets, row_grad.reshape(-1, width), finish, early
 
 
 def plain_experts(resid, out_grad, ids, gates, up, down, cap, experts, swap, early):
@@ -460,30 +564,51 @@
     act = (hidden * sigmoid).astype(BF16)
     slope = sigmoid * (1.0 + hidden * (1.0 - sigmoid))
     pre_grad, row_grad, term = expert_stage(scaled, act, slope, up, down)
-    pieces = lambda: (dot(act, scaled, 0, 0).astype(BF16), dot(rows, pre_grad, 0, 0).astype(BF16))
-    return targets, row_grad, term, pieces, early
+
+    def finish():
+        terms = swap(term.astype(BF16).reshape(experts, cap))
+        gate_grad = call(
+            gate_kernel,
+            shape((2, tokens), F32),
+            jnp.broadcast_to(terms.reshape(1, slots), (8, slots)),
+            targets,
+            gates,
+        )
+        return (
+            dot(act, scaled, 0, 0).astype(BF16),
+            dot(rows, pre_grad, 0, 0).astype(BF16),
+            gate_grad,
+        )
+
+    return targets, row_grad, finish, early
 
 
 def spread(heads, width):
     return (iota((heads, width), 1) // (width // heads) == iota((heads, width), 0)).astype(F32)
 
 
-def ends_kernel(inputs_ref, writes_ref, decays_ref, cum_ref, cumt_ref, send_ref):
+def ends_kernel(
+    inputs_ref, writes_ref, decays_ref, cum_ref, cumt_ref, grown_ref, left_ref, faded_ref, send_ref
+):
     decays = decays_ref[...]
     heads, tokens = decays.shape
     parts, padded, width = send_ref.shape
-    upto = (iota((tokens, tokens), 0) >= iota((tokens, tokens), 1)).astype(F32)
-    cum = dot(upto, decays, 1, 1, HIGHEST)
+    upto = (iota((tokens, tokens), 0) >= iota((tokens, tokens), 1)).astype(BF16)
+    cum = sum(dot(upto, part, 1, 1) for part in pieces_of(decays, 3))
     cum_ref[...] = cum
-    cumt_ref[...] = dot(decays, upto, 1, 1, HIGHEST)
+    cumt = fine_dot(decays, upto, 1, 1, 3)
+    for head in range(heads):
+        cumt_ref[head] = cumt[head : head + 1, :]
     total = cum[tokens - 1 : tokens, :]
-    wide = spread(heads, width)
-    remaining = dot(jnp.exp(total - cum), wide, 1, 0, HIGHEST)
+    wide = spread(heads, width).astype(BF16)
+    grown_ref[...] = fine_dot(jnp.exp(cum), wide, 1, 0, 1).astype(BF16)
+    remaining = fine_dot(jnp.exp(total - cum), wide, 1, 0, 2)
+    left_ref[...] = remaining.astype(BF16)
     scaled = (inputs_ref[...].astype(F32) * remaining).astype(BF16)
+    faded_ref[...] = scaled
     ends = dot(writes_ref[...], scaled, 0, 0)
-    kept = dot(jnp.exp(jnp.broadcast_to(total, (8, heads))), wide, 1, 0, HIGHEST)[0:1, :]
-    high = kept.astype(BF16)
-    low = (kept - high.astype(F32)).astype(BF16)
+    kept = fine_dot(jnp.exp(jnp.broadcast_to(total, (8, heads))), wide, 1, 0, 3)[0:1, :]
+    high, low = pieces_of(kept, 2)
     rows = ends.shape[0] // parts
     for part in range(parts):
         send_ref[part, 0:rows, :] = ends[part * rows : (part + 1) * rows, :].astype(BF16)
@@ -505,11 +630,9 @@
 
 
 def home_kernel(
-    back_ref, targets_ref, resid_ref, out_grad_ref, reads_ref, cum_ref, grad_ref, adjoint_ref
+    back_ref, targets_ref, resid_ref, out_grad_ref, reads_ref, grown_ref, grad_ref, adjoint_ref
 ):
-    slots, width = back_ref.shape
-    heads = cum_ref.shape[1]
-    hit0, hit1 = one_hot(targets_ref[...], slots)
+    hit0, hit1 = one_hot(targets_ref[...], back_ref.shape[0])
     select = jnp.where(hit0 | hit1, 1.0, 0.0).astype(BF16)
     d_normed = dot(select, back_ref[...], 0, 0)
     resid = resid_ref[...].astype(F32)
@@ -518,12 +641,12 @@
     mean = jnp.mean(d_normed * normed, axis=1, keepdims=True)
     grad = (out_grad_ref[...].astype(F32) + inverse * (d_normed - normed * mean)).astype(BF16)
     grad_ref[...] = grad
-    grown = dot(jnp.exp(cum_ref[...]), spread(heads, width), 1, 0, HIGHEST)
-    scaled = (grad.astype(F32) * grown).astype(BF16)
+    scaled = (grad.astype(F32) * grown_ref[...].astype(F32)).astype(BF16)
     adjoint_ref[...] = dot(reads_ref[...], scaled, 0, 0).astype(BF16)
 
 
 def inside_kernel(
+    base,
     inputs_ref,
     grads_ref,
     writes_ref,
@@ -567,7 +690,7 @@
     inter = grads.astype(F32) * read_state
     total = jnp.zeros((tokens, tokens), F32)
     for k in range(each):
-        head = step * each + k
+        head = (base + step) * each + k
         at_t = jnp.sum(jnp.where(column == head, cum, 0.0), axis=1, keepdims=True)
         at_s = cumt_ref[k]
         decay = jnp.exp(jnp.where(causal, at_t - at_s, -1e30))
@@ -586,7 +709,7 @@
         grown = grown + jnp.where(mine, grow, 0.0)
     total_ref[...] += total
     dcum_ref[...] += sums
-    dx_ref[...] = dx
+    dx_ref[...] = dx.astype(BF16)
     dread_ref[...] += dot((grown * grads.astype(F32)).astype(BF16), state, 1, 1)
 
     @pl.when(step == steps - 1)
@@ -596,93 +719,100 @@
         dwrite_ref[...] = dot(total_b, reads_ref[...], 0, 0)
 
 
-def inside_stage(inputs, grads, writes, reads, state, cum, cumt):
+def inside_stage(inputs, grads, writes, reads, state, cum, cumt, half):
     tokens, width = inputs.shape
     heads = cum.shape[1]
     n = writes.shape[1]
     lanes = max(128, width // heads)
-    steps = width // lanes
-    each = heads // steps
-    part = pl.BlockSpec((tokens, lanes), lambda i: (0, i))
-    whole = pl.BlockSpec(memory_space=pltpu.VMEM)
-    fixed = lambda dims: pl.BlockSpec(dims, lambda i: (0,) * len(dims))
+    steps = width // lanes // 2
+    each = heads // (width // lanes)
+    base = half * steps
+    part = pl.BlockSpec((tokens, lanes), lambda i: (0, base + i))
     return call(
-        inside_kernel,
+        functools.partial(inside_kernel, base),
         (
-            shape((tokens, width), F32),
-            shape((tokens, n), F32),
-            shape((tokens, n), F32),
-            shape((tokens, heads), F32),
-            shape((heads, 1, tokens), F32),
+            far_shape((tokens, width // 2), BF16),
+            far_shape((tokens, n), F32),
+            far_shape((tokens, n), F32),
+            far_shape((tokens, heads), F32),
+            far_shape((heads // 2, 1, tokens), F32),
         ),
-        inputs,
-        grads,
-        writes,
-        reads,
-        state,
-        cum,
-        cumt.reshape(heads, 1, tokens),
+        *from_hbm(inputs, grads, writes, reads, state, cum, cumt),
         grid=(steps,),
         in_specs=[
             part,
             part,
-            whole,
-            whole,
-            pl.BlockSpec((n, lanes), lambda i: (0, i)),
-            whole,
-            pl.BlockSpec((each, 1, tokens), lambda i: (i, 0, 0)),
+            one_step((tokens, n)),
+            one_step((tokens, n)),
+            pl.BlockSpec((n, lanes), lambda i: (0, base + i)),
+            one_step((tokens, heads)),
+            pl.BlockSpec((each, 1, tokens), lambda i: (base + i, 0, 0)),
         ],
         out_specs=(
-            part,
-            fixed((tokens, n)),
-            fixed((tokens, n)),
-            fixed((tokens, heads)),
+            pl.BlockSpec((tokens, lanes), lambda i: (0, i)),
+            one_step((tokens, n)),
+            one_step((tokens, n)),
+            one_step((tokens, heads)),
             pl.BlockSpec((each, 1, tokens), lambda i: (i, 0, 0)),
         ),
         scratch=[pltpu.VMEM((tokens, tokens), F32), pltpu.VMEM((tokens, tokens), F32)],
         cost=pl.CostEstimate(
-            flops=8 * heads * tokens * tokens * 64, bytes_accessed=8 * tokens * width, transcendentals=heads * tokens * tokens
+            flops=4 * tokens * tokens * width,
+            bytes_accessed=4 * tokens * width,
+            transcendentals=heads * tokens * tokens // 2,
         ),
     )
 
 
 def last_kernel(
-    inputs_ref,
     writes_ref,
     state_ref,
     adjoint_ref,
-    cum_ref,
     cumt_ref,
-    dx_ref,
-    dwrite_in_ref,
-    dcum_ref,
-    dcumt_ref,
+    left_ref,
+    faded_ref,
+    dx0_ref,
+    dwrite0_ref,
+    dread0_ref,
+    dcum0_ref,
+    dcumt0_ref,
+    dx1_ref,
+    dwrite1_ref,
+    dread1_ref,
+    dcum1_ref,
+    dcumt1_ref,
     input_grad_ref,
     dwrite_ref,
+    dread_ref,
     decay_ref,
 ):
-    tokens, width = inputs_ref.shape
-    heads = cum_ref.shape[1]
-    cum = cum_ref[...]
-    total = cum[tokens - 1 : tokens, :]
-    wide = spread(heads, width)
-    remaining = dot(jnp.exp(total - cum), wide, 1, 0, HIGHEST)
+    tokens, width = left_ref.shape
+    heads = cumt_ref.shape[0]
+    half = width // 2
+    wide = spread(heads, width).astype(BF16)
     adjoint = adjoint_ref[...]
-    inputs = inputs_ref[...].astype(F32)
-    moved = remaining * dot(writes_ref[...], adjoint, 1, 0)
-    input_grad_ref[...] = (dx_ref[...] + moved).astype(BF16)
-    dwrite_ref[...] = dwrite_in_ref[...] + dot((remaining * inputs).astype(BF16), adjoint, 1, 1)
-    shares = dot(moved * inputs, wide, 1, 1, HIGHEST)
-    kept = state_ref[...].astype(F32) * adjoint.astype(F32)
-    kept = jnp.broadcast_to(jnp.sum(kept, axis=0, keepdims=True), (8, width))
-    tail = dot(wide, kept, 1, 1, HIGHEST)[:, 0:1] * jnp.exp(cumt_ref[...][:, tokens - 1 : tokens])
-    after = (iota((tokens, tokens), 1) >= iota((tokens, tokens), 0)).astype(F32)
-    before = (iota((tokens, tokens), 1) < iota((tokens, tokens), 0)).astype(F32)
+    faded = faded_ref[...]
+    values = dot(writes_ref[...], adjoint, 1, 0)
+    moved = left_ref[...].astype(F32) * values
+    input_grad_ref[:, 0:half] = (dx0_ref[...].astype(F32) + moved[:, 0:half]).astype(BF16)
+    input_grad_ref[:, half:] = (dx1_ref[...].astype(F32) + moved[:, half:]).astype(BF16)
+    dwrite_ref[...] = dwrite0_ref[...] + dwrite1_ref[...] + dot(faded, adjoint, 1, 1)
+    dread_ref[...] = dread0_ref[...] + dread1_ref[...]
+    shares = pieces_of(values * faded.astype(F32), 2)
+    shares = sum(dot(wide, part, 1, 1) for part in shares)
+    kept = jnp.sum(state_ref[...].astype(F32) * adjoint.astype(F32), axis=0, keepdims=True)
+    kept = pieces_of(jnp.broadcast_to(kept, (8, width)), 3)
+    kept = sum(dot(wide, part, 1, 1) for part in kept)[:, 0:1]
+    flow = [ref[h] for ref in (dcumt0_ref, dcumt1_ref) for h in range(heads // 2)]
+    total = jnp.concatenate([cumt_ref[h][:, tokens - 1 : tokens] for h in range(heads)], axis=0)
+    after = (iota((tokens, tokens), 1) >= iota((tokens, tokens), 0)).astype(BF16)
+    rows = -jnp.concatenate(flow, axis=0) - shares
+    columns = dcum0_ref[...] + dcum1_ref[...]
     decay_ref[...] = (
-        dot(dcum_ref[...], after, 0, 1, HIGHEST)
-        - dot(dcumt_ref[...], after, 1, 1, HIGHEST)
-        + dot(shares, before, 0, 1, HIGHEST)
-        + tail
+        sum(dot(part, after, 0, 1) for part in pieces_of(columns, 3))
+        + sum(dot(part, after, 1, 1) for part in pieces_of(rows, 3))
+        + jnp.sum(shares, axis=1, keepdims=True)
+        + kept * jnp.exp(total)
     )
 
 
@@ -704,7 +834,6 @@
     shard_count = lax.axis_size("seq")
     experts = lax.axis_size("grp") * shard_count
     cap = 4 * tokens // experts
-    slots = experts * cap
     everyone = ("grp", "seq")
     up, down = expert_up[0], expert_down[0]
     ids = expert_ids.T
@@ -714,76 +843,72 @@
         return lax.all_to_all(x, axes, split_axis=0, concat_axis=0, tiled=True)
 
     state_rows = n // shard_count
-    padded = -(-(state_rows + 2) // 16) * 16
-    cum, cumt, send_ends = call(
+    padded = -(-(state_rows + 2) // 8) * 8
+    cum, cumt, grown, left, faded, send_ends = streamed(
         ends_kernel,
         (
-            shape((tokens, heads), F32),
-            shape((heads, tokens), F32),
-            shape((shard_count, padded, width), BF16),
+            far_shape((tokens, heads), F32),
+            far_shape((heads, 1, tokens), F32),
+            far_shape((tokens, width), BF16),
+            far_shape((tokens, width), BF16),
+            far_shape((tokens, width), BF16),
+            far_shape((shard_count, padded, width), BF16),
         ),
         mixer_input,
         write_proj,
         log_decay.T,
     )
     ends = swap(send_ends, "seq")
-    parts = shape((shard_count, state_rows, width), BF16)
+    parts = far_shape((shard_count, state_rows, width), BF16)
     starts = call(functools.partial(scan_kernel, False), parts, ends, ends)
     state = swap(starts, "seq").reshape(n, width)
 
     planes = experts // shard_count
-    if planes == 4 and shard_count <= 8 and cap % 16 == 0 and tokens <= width:
-        targets, row_grad, term, outers, state = routed_experts(
+    if planes == 4 and shard_count <= 8 and cap in (16, 32, 64, 128) and tokens <= width:
+        targets, row_grad, finish, state = routed_experts(
             resid, out_grad, ids, gates, up, down, cap, shard_count, planes, state
         )
     else:
-        targets, row_grad, term, outers, state = plain_experts(
+        targets, row_grad, finish, state = plain_experts(
             resid, out_grad, ids, gates, up, down, cap, experts, lambda x: swap(x, everyone), state
         )
     back = swap(row_grad, everyone)
-    down_grad, up_grad = outers()
+    down_grad, up_grad, gate_grad = finish()
     back, down_grad, up_grad = lax.optimization_barrier((back, down_grad, up_grad))
-    terms, back = lax.optimization_barrier((term.astype(BF16).reshape(experts, cap), back))
-    terms = swap(terms, everyone)
-    resid_grad, send_adjoint = call(
+    resid_grad, send_adjoint = streamed(
         home_kernel,
-        (shape((tokens, width), BF16), shape((n, width), BF16)),
+        (far_shape((tokens, width), BF16), far_shape((n, width), BF16)),
         back,
         targets,
         resid,
         out_grad,
         read_proj,
-        cum,
-    )
-    send_adjoint, terms = lax.optimization_barrier((send_adjoint, terms))
+        grown,
+        near=(0,),
+    )
     adjoints = swap(send_adjoint.reshape(shard_count, state_rows, width), "seq")
-    dx, dwrite, read_grad, dcum, dcumt = inside_stage(
-        mixer_input, resid_grad, write_proj, read_proj, state, cum, cumt
-    )
+    inside = (mixer_input, resid_grad, write_proj, read_proj, state, cum, cumt)
+    first = inside_stage(*inside, 0)
     later = call(functools.partial(scan_kernel, True), parts, adjoints, ends)
     adjoint = swap(later, "seq").reshape(n, width)
-    gate_grad = call(
-        gate_kernel,
-        shape((2, tokens), F32),
-        jnp.broadcast_to(terms.reshape(1, slots), (8, slots)),
-        targets,
-        gates,
-    )
-    gate_grad = gate_grad.T.astype(BF16)
-
-    input_grad, write_grad, decay_grad = call(
+    second = inside_stage(*inside, 1)
+    input_grad, write_grad, read_grad, decay_grad = streamed(
         last_kernel,
-        (shape((tokens, width), BF16), shape((tokens, n), F32), shape((heads, tokens), F32)),
-        mixer_input,
+        (
+            far_shape((tokens, width), BF16),
+            far_shape((tokens, n), F32),
+            far_shape((tokens, n), F32),
+            far_shape((heads, tokens), F32),
+        ),
         write_proj,
         state,
         adjoint,
-        cum,
         cumt,
-        dx,
-        dwrite,
-        dcum,
-        dcumt.reshape(heads, tokens),
+        left,
+        faded,
+        *first,
+        *second,
+        near=(2,),
     )
     return (
         input_grad,
@@ -791,7 +916,7 @@
         read_grad,
         decay_grad.T,
         resid_grad,
-        gate_grad,
+        gate_grad.T.astype(BF16),
         up_grad[None],
         down_grad[None],
     )

time: 243 us -> 239 us (0.984)
  local copies, waits for them, and re-layouts: 53.6 us -> 5.59 us
  Pallas kernels: 46.5 us -> 69.5 us
  waiting for transfers between devices: 71.5 us -> 83.9 us
  starting transfers between devices: 67.4 us -> 76 us
    unnamed x154 -> x76, local copies, waits for them, and re-layouts: 49.4 us -> 5.59 us
    pallas_call x13 -> x16, Pallas kernels: 31.2 us -> 49.1 us  [call(): pl.pallas_call(kernel, out_shape=outs, in_specs=in_specs if in_specs is n...]
    ppermute x6 -> x9, waiting for transfers between devices: 25 us -> 33.2 us  [across(): return lax.ppermute(x, 'grp', [(i, i ^ bit) for i in range(planes)])]
    ppermute x21 -> x35, waiting for transfers between devices: 8.31 us -> 15.3 us  [spread_out(): lax.ppermute(part, 'seq', [(i, i ^ x) for i in range(shard_count)])]
    ppermute x21 -> x35, starting transfers between devices: 35.8 us -> 42.5 us  [spread_out(): lax.ppermute(part, 'seq', [(i, i ^ x) for i in range(shard_count)])]
    pallas_call x3 -> x4, Pallas kernels: 15.3 us -> 20.4 us  [grouped(): pl.pallas_call(functools.partial(kernel, len(parts)), out_shape=outs, gri...]
    ppermute x6 -> x9, starting transfers between devices: 6.42 us -> 10.6 us  [across(): return lax.ppermute(x, 'grp', [(i, i ^ bit) for i in range(planes)])]
    all_to_all x6 -> x5, waiting for transfers between devices: 38.2 us -> 35.4 us  [swap(): return lax.all_to_all(x, axes, split_axis=0, concat_axis=0, tiled=True)]
  transfers between devices with their start and end apart: 33 -> 49, of which waited for: 7 -> 13; matrix products, arithmetic and copies ran while one was open for 1% -> 1% of each run, Pallas kernels for 16% -> 23%
where the time goes in v2:
time: 239 us; the launch traced here: 237 us
  waiting for transfers between devices  83.9 us (35%)
  starting transfers between devices  76 us (32%)
  Pallas kernels  69.5 us (29%)
  local copies, waits for them, and re-layouts  5.59 us (2%)
    pallas_call x16, Pallas kernels, call(): pl.pallas_call(kernel, out_shape=outs, in_specs=in_specs if in_specs is n...  49.1 us
    ppermute x35, starting transfers between devices, spread_out(): lax.ppermute(part, 'seq', [(i, i ^ x) for i in range(shard_count)])  42.5 us
    all_to_all x5, waiting for transfers between devices, swap(): return lax.all_to_all(x, axes, split_axis=0, concat_axis=0, tiled=True)  35.4 us
    ppermute x9, waiting for transfers between devices, across(): return lax.ppermute(x, 'grp', [(i, i ^ bit) for i in range(planes)])  33.2 us
    all_to_all x5, starting transfers between devices, swap(): return lax.all_to_all(x, axes, split_axis=0, concat_axis=0, tiled=True)  22.9 us
    pallas_call x4, Pallas kernels, grouped(): pl.pallas_call(functools.partial(kernel, len(parts)), out_shape=outs, gri...  20.4 us
    ppermute x35, waiting for transfers between devices, spread_out(): lax.ppermute(part, 'seq', [(i, i ^ x) for i in range(shard_count)])  15.3 us
    ppermute x9, starting transfers between devices, across(): return lax.ppermute(x, 'grp', [(i, i ^ bit) for i in range(planes)])  10.6 us
  transfers between devices with their start and end apart: 49, of which 13 were waited for; matrix products, arithmetic and copies ran while one was open for 1% of the time, Pallas kernels for 23%

profile of v2, /device:TPU:1, one launch (start us, length us, event | category | flops | bytes accessed | tf_op | source)
XLA Modules:
  0.0 237.4 jit_solution(18320882406491101707)
XLA Ops:
  0.6 2.1 shard_map.161
  2.7 3.1 %collective-permute-start.1 = (bf16[272,1024]{1,0:T(8,128)(2,1)}, bf16[272,1024]{1,0:T(8,128)(2,1)S(1)}, u32[]{:S(2)}, u32[]{:S(2)}) collective-permute-start(bf16[272,1024]{1,0:T(8,128)(2,1)} %get-tuple-element.97.message_ref), channel_id=1, source_target_pairs={{0,16},{8,24},{16,0},{24,8},{1,17},{9,25},{17,1},{25,9},{2,18},{10... | collective-permute-start | bytes 1671176 | tf_op jit(solution)/shard_map/ppermute | solution.py:394
  7.3 2.6 %shard_map.168 = (bf16[64,1024]{1,0:T(8,128)(2,1)}, bf16[64,1024]{1,0:T(8,128)(2,1)}, bf16[64,1024]{1,0:T(8,128)(2,1)}, bf16[64,1024]{1,0:T(8,128)(2,1)}, bf16[6...) custom-call(s32[2]{0:T(128)S(1)} %pad_add_fusion.me_ref, ...), custom_call_target="tpu_custom_call" | custom-call | tf_op jit(solution)/shard_map/pallas_call | solution.py:33
  9.8 1.5 collective-permute-start.27
  13.8 3.7 %collective-permute-done.28.refs_2_ = bf16[64,1024]{1,0:T(8,128)(2,1)S(1)} collective-permute-done((bf16[64,1024]{1,0:T(8,128)(2,1)}, bf16[64,1024]{1,0:T(8,128)(2,1)S(1)}, u32[]{:S(2)}, u32[]{:S(2)}) %collective-permute-start.28) | collective-permute-done | bytes 131104 | tf_op jit(solution)/shard_map/ppermute | solution.py:398
  17.5 2.3 collective-permute-start.29
  19.8 21.8 %collective-permute-done.1.refs_1_ = bf16[272,1024]{1,0:T(8,128)(2,1)S(1)} collective-permute-done((bf16[272,1024]{1,0:T(8,128)(2,1)}, bf16[272,1024]{1,0:T(8,128)(2,1)S(1)}, u32[]{:S(2)}, u32[]{:S(2)}) %collective-permute-start.1) | collective-permute-done | bytes 557088 | tf_op jit(solution)/shard_map/ppermute | solution.py:394
  44.1 8.8 %collective-permute-done.4.refs_1_ = bf16[256,1024]{1,0:T(8,128)(2,1)} collective-permute-done((bf16[256,1024]{1,0:T(8,128)(2,1)}, bf16[256,1024]{1,0:T(8,128)(2,1)}, u32[]{:S(2)}, u32[]{:S(2)}) %collective-permute-start.4) | collective-permute-done | bytes 524320 | tf_op jit(solution)/shard_map/ppermute | solution.py:394
  54.1 1.9 collective-permute-start.31
  58.3 3.2 %shard_map.163 = (f32[256,16]{1,0:T(8,128)}, f32[16,1,256]{2,1,0:T(1,128)}, bf16[256,1024]{1,0:T(8,128)(2,1)}, bf16[256,1024]{1,0:T(8,128)(2,1)}, bf16[256,1024]...) custom-call(bf16[256,1024]{1,0:T(8,128)(2,1)} %inputs_ref.5, bf16[256,128]{1,0:T(8,128)(2,1)} %writes_ref.7, f32[16,256]{1,0:T(8,128)} %bitcast.40), custom_call_target="tpu_custom_call" | custom-call | tf_op jit(solution)/shard_map/pallas_call | solution.py:33
  61.5 3.8 %all-to-all-start = ((bf16[8,24,1024]{2,1,0:T(8,128)(2,1)}), bf16[8,24,1024]{2,1,0:T(8,128)(2,1)S(1)}, u32[]{:S(2)}, u32[]{:S(2)}) async-start(bf16[8,24,1024]{2,1,0:T(8,128)(2,1)} %get-tuple-element.99), calls=%async_computation | async-start | bytes 786432 | tf_op jit(solution)/shard_map/all_to_all | solution.py:843
  65.4 2.6 %shard_map.162 = (bf16[64,1024]{1,0:T(8,128)(2,1)}, bf16[64,1024]{1,0:T(8,128)(2,1)}, bf16[64,1024]{1,0:T(8,128)(2,1)}, bf16[64,1024]{1,0:T(8,128)(2,1)}, bf16[6...) custom-call(s32[2]{0:T(128)S(1)} %pad_add_fusion.me_ref, ...), custom_call_target="tpu_custom_call" | custom-call | tf_op jit(solution)/shard_map/pallas_call | solution.py:33
  68.0 2.7 %shard_map.166 = (bf16[64,1024]{1,0:T(8,128)(2,1)}, bf16[64,1024]{1,0:T(8,128)(2,1)}, bf16[64,1024]{1,0:T(8,128)(2,1)}, bf16[64,1024]{1,0:T(8,128)(2,1)}, bf16[6...) custom-call(f32[2,8,256]{2,1,0:T(8,128)} %get-tuple-element.109.keys_ref, ...), custom_call_target="tpu_custom_call" | custom-call | tf_op jit(solution)/shard_map/pallas_call | solution.py:33
  72.2 1.6 collective-permute-start.15
  77.4 1.5 collective-permute-start.2
  78.9 1.7 collective-permute-done.16.refs_3_
  80.6 1.5 collective-permute-start.21
  83.8 1.8 collective-permute-done.21.refs_2_
  85.6 3.0 %collective-permute-start.24 = (bf16[64,1024]{1,0:T(8,128)(2,1)}, bf16[64,1024]{1,0:T(8,128)(2,1)}, u32[]{:S(2)}, u32[]{:S(2)}) collective-permute-start(bf16[64,1024]{1,0:T(8,128)(2,1)} %get-tuple-element.123), channel_id=1, source_target_pairs={{0,5},{1,4},{2,7},{3,6},{4,1},{5,0},{6,3},{7,2},{8,13},{9,12},{10,... | collective-permute-start | bytes 393224 | tf_op jit(solution)/shard_map/ppermute | solution.py:398
  91.0 4.6 %all-to-all-start.1 = ((bf16[8,16,1024]{2,1,0:T(8,128)(2,1)}), bf16[8,16,1024]{2,1,0:T(8,128)(2,1)S(1)}, u32[]{:S(2)}, u32[]{:S(2)}) async-start(bf16[8,16,1024]{2,1,0:T(8,128)(2,1)} %shard_map.164), calls=%async_computation.1 | async-start | bytes 524288 | tf_op jit(solution)/shard_map/all_to_all | solution.py:843
  95.6 2.6 %shard_map.165 = (bf16[64,1024]{1,0:T(8,128)(2,1)}, bf16[64,1024]{1,0:T(8,128)(2,1)}, bf16[64,1024]{1,0:T(8,128)(2,1)}, bf16[64,1024]{1,0:T(8,128)(2,1)}, bf16[6...) custom-call(s32[2]{0:T(128)S(1)} %pad_add_fusion.me_ref, ...), custom_call_target="tpu_custom_call" | custom-call | tf_op jit(solution)/shard_map/pallas_call | solution.py:33
  98.2 1.7 collective-permute-start.18
  101.0 1.5 collective-permute-start.20
  103.8 1.6 copy-done.1
  105.4 5.0 %shard_map.169 = (bf16[256,1024]{1,0:T(8,128)(2,1)}, bf16[256,1024]{1,0:T(8,128)(2,1)}, bf16[256,1024]{1,0:T(8,128)(2,1)}, bf16[256,1024]{1,0:T(8,128)(2,1)}, bf...) custom-call(s32[2]{0:T(128)S(1)} %pad_add_fusion.me_ref, bf16[64,1024]{1,0:T(8,128)(2,1)} %get-tuple-element.128.refs_0_, ...), custom_call_target="tpu_custom_call" | custom-call | flops 1610612736 | bytes 6291456 | tf_op jit(solution)/shard_map/pallas_call | solution.py:340
  110.5 4.6 %shard_map.167 = (bf16[512,1024]{1,0:T(8,128)(2,1)}, bf16[512,1024]{1,0:T(8,128)(2,1)}, f32[512,1024]{1,0:T(8,128)S(1)}) custom-call(s32[2]{0:T(128)S(1)} %pad_add_fusion.me_ref, bf16[64,1024]{1,0:T(8,128)(2,1)} %get-tuple-element.118.refs_0_, bf16[64,1024]{1,0:T(8,128)(2,1)} %copy-done.35, bf16[64,1024]{1,0:T(8,128)(2,1)} %copy-done.36, ...), custom_call_target="tpu_custom_call" | custom-call | flops 1073741824 | bytes 6291456 | tf_op jit(solution)/shard_map/pallas_call | solution.py:340
  118.8 1.8 collective-permute-start.12
  121.8 5.9 %shard_map.170 = (bf16[512,1024]{1,0:T(8,128)(2,1)}, bf16[512,1024]{1,0:T(8,128)(2,1)}, bf16[4,256,1024]{2,1,0:T(8,128)(2,1)}, f32[2,8,256]{2,1,0:T(8,128)}) custom-call(s32[2]{0:T(128)S(1)} %pad_add_fusion.me_ref, bf16[64,1024]{1,0:T(8,128)(2,1)} %get-tuple-element.110.refs_0_, bf16[64,1024]{1,0:T(8,128)(2,1)} %copy-done.11, ...), custom_call_target="tpu_custom_call", output_to_operand_aliasing={{2}: (13, {})} | custom-call | flops 2147483648 | bytes 6291456 | tf_op jit(solution)/shard_map/pallas_call | solution.py:340
  127.7 2.1 collective-permute-done.10.refs_5_
  130.6 4.9 %shard_map.171 = (bf16[256,1024]{1,0:T(8,128)(2,1)}, bf16[256,1024]{1,0:T(8,128)(2,1)}, bf16[256,1024]{1,0:T(8,128)(2,1)}, bf16[256,1024]{1,0:T(8,128)(2,1)}, bf...) custom-call(s32[2]{0:T(128)S(1)} %pad_add_fusion.me_ref, ...), custom_call_target="tpu_custom_call", output_to_operand_aliasing={{4}: (11, {})} | custom-call | flops 1610612736 | bytes 6291456 | tf_op jit(solution)/shard_map/pallas_call | solution.py:340
  135.5 6.2 %all-to-all-start.2 = ((bf16[32,32,1024]{2,1,0:T(8,128)(2,1)}), bf16[32,32,1024]{2,1,0:T(8,128)(2,1)S(1)}, u32[]{:S(2)}, u32[]{:S(2)}) async-start(bf16[32,32,1024]{2,1,0:T(8,128)(2,1)} %bitcast.35), calls=%async_computation.2 | async-start | bytes 4194304 | tf_op jit(solution)/shard_map/all_to_all | solution.py:843
  141.7 6.3 %shard_map.172 = bf16[1024,1024]{1,0:T(8,128)(2,1)} custom-call(bf16[256,1024]{1,0:T(8,128)(2,1)} %get-tuple-element.139.refs_0_, bf16[256,1024]{1,0:T(8,128)(2,1)} %get-tuple-element.140.refs_1_, bf16[512,1024]{1,0:T(8,128)(2,1)} %get-tuple-element.126.refs_8_.refs_2_, bf16[512,1024]{1,0:T(8,128)(2,1)} %get-tuple-element.141.refs_3_, ...), custom_call_target="tpu_custom_call" | custom-call | flops 2147483648 | bytes 6291456 | tf_op jit(solution)/shard_map/pallas_call | solution.py:33
  148.0 6.3 %shard_map.173 = bf16[1024,1024]{1,0:T(8,128)(2,1)} custom-call(bf16[256,1024]{1,0:T(8,128)(2,1)} %get-tuple-element.144.refs_0_, bf16[256,1024]{1,0:T(8,128)(2,1)} %get-tuple-element.145.refs_1_, bf16[512,1024]{1,0:T(8,128)(2,1)} %get-tuple-element.146.refs_2_, bf16[512,1024]{1,0:T(8,128)(2,1)} %get-tuple-element.147.refs_3_, ...), custom_call_target="tpu_custom_call" | custom-call | flops 2147483648 | bytes 6291456 | tf_op jit(solution)/shard_map/pallas_call | solution.py:33
  154.4 35.3 %all-to-all-done.2 = bf16[32,32,1024]{2,1,0:T(8,128)(2,1)S(1)} async-done(((bf16[32,32,1024]{2,1,0:T(8,128)(2,1)}), bf16[32,32,1024]{2,1,0:T(8,128)(2,1)S(1)}, u32[]{:S(2)}, u32[]{:S(2)}) %all-to-all-start.2) | async-done | bytes 2097184 | tf_op jit(solution)/shard_map/all_to_all | solution.py:843
  189.7 3.5 %shard_map.174 = (bf16[256,1024]{1,0:T(8,128)(2,1)}, bf16[128,1024]{1,0:T(8,128)(2,1)}) custom-call(bf16[1024,1024]{1,0:T(8,128)(2,1)S(1)} %bitcast.23, s32[2,256]{1,0:T(2,128)} %get-tuple-element.151.targets_ref, bf16[256,1024]{1,0:T(8,128)(2,1)} %resid_ref.3, bf16[256,1024]{1,0:T(8,128)(2,1)} %out_grad_ref.1, bf16[256,128]{1,0:T(8,128)(2,1)} %reads_ref.5, ...), custom_call_target="tpu_custom_call" | custom-call | tf_op jit(solution)/shard_map/pallas_call | solution.py:33
  193.2 4.7 %all-to-all-start.3 = ((bf16[8,16,1024]{2,1,0:T(8,128)(2,1)}), bf16[8,16,1024]{2,1,0:T(8,128)(2,1)S(1)}, u32[]{:S(2)}, u32[]{:S(2)}) async-start(bf16[8,16,1024]{2,1,0:T(8,128)(2,1)} %bitcast.39), calls=%async_computation.3 | async-start | bytes 524288 | tf_op jit(solution)/shard_map/all_to_all | solution.py:843
  198.1 1.7 collective-permute-start.34
  199.8 1.7 collective-permute-start.36
  201.5 2.6 %collective-permute-done.36.refs_3_ = f32[8,256]{1,0:T(8,128)S(1)} collective-permute-done((f32[8,256]{1,0:T(8,128)S(1)}, f32[8,256]{1,0:T(8,128)S(1)}, u32[]{:S(2)}, u32[]{:S(2)}) %collective-permute-start.36) | collective-permute-done | bytes 8224 | tf_op jit(solution)/shard_map/ppermute | solution.py:394
  204.9 1.8 collective-permute-start.37
  206.7 1.7 collective-permute-start.38
  208.5 1.7 collective-permute-start.40
  210.4 2.4 collective-permute-start.42
  213.8 2.9 %collective-permute-done.43.refs_7_ = f32[8,128]{1,0:T(8,128)S(1)} collective-permute-done((f32[8,128]{1,0:T(8,128)S(1)}, f32[8,128]{1,0:T(8,128)S(1)}, u32[]{:S(2)}, u32[]{:S(2)}) %collective-permute-start.43) | collective-permute-done | bytes 4128 | tf_op jit(solution)/shard_map/ppermute | solution.py:398
  218.9 3.7 %all-to-all-start.4 = ((bf16[8,16,1024]{2,1,0:T(8,128)(2,1)}), bf16[8,16,1024]{2,1,0:T(8,128)(2,1)S(1)}, u32[]{:S(2)}, u32[]{:S(2)}) async-start(bf16[8,16,1024]{2,1,0:T(8,128)(2,1)} %shard_map.175), calls=%async_computation.4 | async-start | bytes 524288 | tf_op jit(solution)/shard_map/all_to_all | solution.py:843
  223.8 5.0 %shard_map.177 = (bf16[256,512]{1,0:T(8,128)(2,1)}, f32[256,128]{1,0:T(8,128)}, f32[256,128]{1,0:T(8,128)}, f32[256,16]{1,0:T(8,128)}, f32[8,1,256]{2,1,0:T(1,128)}) custom-call(bf16[256,1024]{1,0:T(8,128)(2,1)} %inputs_ref.5, bf16[256,1024]{1,0:T(8,128)(2,1)} %get-tuple-element.93.grads_ref, bf16[256,128]{1,0:T(8,128)(2,1)} %writes_ref.7, ...), custom_call_target="tpu_custom_call" | custom-call | flops 268435456 | bytes 1048576 | tf_op jit(solution)/shard_map/pallas_call | solution.py:33
  228.8 4.9 %shard_map.176 = (bf16[256,512]{1,0:T(8,128)(2,1)}, f32[256,128]{1,0:T(8,128)}, f32[256,128]{1,0:T(8,128)}, f32[256,16]{1,0:T(8,128)}, f32[8,1,256]{2,1,0:T(1,128)}) custom-call(bf16[256,1024]{1,0:T(8,128)(2,1)} %inputs_ref.5, bf16[256,1024]{1,0:T(8,128)(2,1)} %get-tuple-element.93.grads_ref, bf16[256,128]{1,0:T(8,128)(2,1)} %writes_ref.7, ...), custom_call_target="tpu_custom_call" | custom-call | flops 268435456 | bytes 1048576 | tf_op jit(solution)/shard_map/pallas_call | solution.py:33
  233.7 3.6 %shard_map.178 = (bf16[256,1024]{1,0:T(8,128)(2,1)}, f32[256,128]{1,0:T(8,128)}, f32[256,128]{1,0:T(8,128)}, f32[16,256]{1,0:T(8,128)}) custom-call(bf16[256,128]{1,0:T(8,128)(2,1)} %writes_ref.7, bf16[128,1024]{1,0:T(8,128)(2,1)} %bitcast.38, bf16[128,1024]{1,0:T(8,128)(2,1)S(1)} %bitcast.31, f32[16,1,256]{2,1,0:T(1,128)} %get-tuple-element.154.cumt_ref, ...), custom_call_target="tpu_custom_call" | custom-call | tf_op jit(solution)/shard_map/pallas_call | solution.py:33
  (149 shorter events, 33.0 us)
Async XLA Ops:
  2.7 38.9 %collective-permute-start.1 = (bf16[272,1024]{1,0:T(8,128)(2,1)}, bf16[272,1024]{1,0:T(8,128)(2,1)S(1)}, u32[]{:S(2)}, u32[]{:S(2)}) collective-permute-start(bf16[272,1024]{1,0:T(8,128)(2,1)} %get-tuple-element.97.message_ref), channel_id=1, source_target_pairs={{0,16},{8,24},{16,0},{24,8},{1,17},{9,25},{17,1},{25,9},{2,18},{10... | collective-permute-start | bytes 1671176 | tf_op jit(solution)/shard_map/ppermute | solution.py:394
  5.8 47.1 %collective-permute-start.4 = (bf16[256,1024]{1,0:T(8,128)(2,1)}, bf16[256,1024]{1,0:T(8,128)(2,1)}, u32[]{:S(2)}, u32[]{:S(2)}) collective-permute-start(bf16[256,1024]{1,0:T(8,128)(2,1)} %out_grad_ref.1), channel_id=1, source_target_pairs={{0,16},{8,24},{16,0},{24,8},{1,17},{9,25},{17,1},{25,9},{2,18},{10... | collective-permute-start | bytes 1572872 | tf_op jit(solution)/shard_map/ppermute | solution.py:394
  5.9 51.3 %collective-permute-start = (bf16[272,1024]{1,0:T(8,128)(2,1)}, bf16[272,1024]{1,0:T(8,128)(2,1)S(1)}, u32[]{:S(2)}, u32[]{:S(2)}) collective-permute-start(bf16[272,1024]{1,0:T(8,128)(2,1)} %get-tuple-element.97.message_ref), channel_id=1, source_target_pairs={{0,8},{8,0},{16,24},{24,16},{1,9},{9,1},{17,25},{25,17},{2,10},{10... | collective-permute-start | bytes 1671176 | tf_op jit(solution)/shard_map/ppermute | solution.py:394
  11.4 44.7 %collective-permute-start.13 = (bf16[256,1024]{1,0:T(8,128)(2,1)}, bf16[256,1024]{1,0:T(8,128)(2,1)S(1)}, u32[]{:S(2)}, u32[]{:S(2)}) collective-permute-start(bf16[256,1024]{1,0:T(8,128)(2,1)} %out_grad_ref.1), channel_id=1, source_target_pairs={{0,8},{8,0},{16,24},{24,16},{1,9},{9,1},{17,25},{25,17},{2,10},{10... | collective-permute-start | bytes 1572872 | tf_op jit(solution)/shard_map/ppermute | solution.py:394
  12.6 4.9 %collective-permute-start.28 = (bf16[64,1024]{1,0:T(8,128)(2,1)}, bf16[64,1024]{1,0:T(8,128)(2,1)S(1)}, u32[]{:S(2)}, u32[]{:S(2)}) collective-permute-start(bf16[64,1024]{1,0:T(8,128)(2,1)} %get-tuple-element.130), channel_id=1, source_target_pairs={{0,2},{1,3},{2,0},{3,1},{4,6},{5,7},{6,4},{7,5},{8,10},{9,11},{10,... | collective-permute-start | bytes 393224 | tf_op jit(solution)/shard_map/ppermute | solution.py:398
  17.5 25.4 %collective-permute-start.29 = (bf16[64,1024]{1,0:T(8,128)(2,1)}, bf16[64,1024]{1,0:T(8,128)(2,1)S(1)}, u32[]{:S(2)}, u32[]{:S(2)}) collective-permute-start(bf16[64,1024]{1,0:T(8,128)(2,1)} %get-tuple-element.131), channel_id=1, source_target_pairs={{0,3},{1,2},{2,1},{3,0},{4,7},{5,6},{6,5},{7,4},{8,11},{9,10},{10,... | collective-permute-start | bytes 393224 | tf_op jit(solution)/shard_map/ppermute | solution.py:398
  41.6 48.2 %collective-permute-start.3 = (bf16[272,1024]{1,0:T(8,128)(2,1)S(1)}, bf16[272,1024]{1,0:T(8,128)(2,1)}, u32[]{:S(2)}, u32[]{:S(2)}) collective-permute-start(bf16[272,1024]{1,0:T(8,128)(2,1)S(1)} %collective-permute-done.1.refs_1_), channel_id=1, source_target_pairs={{0,8},{8,0},{16,24},{24,16},{1,9},{9,1},{17,25},{25,17},{2,10},{10... | collective-permute-start | bytes 1671176 | tf_op jit(solution)/shard_map/ppermute | solution.py:394
  42.9 11.2 %collective-permute-start.30 = (bf16[64,1024]{1,0:T(8,128)(2,1)}, bf16[64,1024]{1,0:T(8,128)(2,1)S(1)}, u32[]{:S(2)}, u32[]{:S(2)}) collective-permute-start(bf16[64,1024]{1,0:T(8,128)(2,1)} %get-tuple-element.132), channel_id=1, source_target_pairs={{0,4},{1,5},{2,6},{3,7},{4,0},{5,1},{6,2},{7,3},{8,12},{9,13},{10,... | collective-permute-start | bytes 393224 | tf_op jit(solution)/shard_map/ppermute | solution.py:398
  52.9 35.7 %collective-permute-start.5 = (bf16[256,1024]{1,0:T(8,128)(2,1)}, bf16[256,1024]{1,0:T(8,128)(2,1)}, u32[]{:S(2)}, u32[]{:S(2)}) collective-permute-start(bf16[256,1024]{1,0:T(8,128)(2,1)} %collective-permute-done.4.refs_1_), channel_id=1, source_target_pairs={{0,8},{8,0},{16,24},{24,16},{1,9},{9,1},{17,25},{25,17},{2,10},{10... | collective-permute-start | bytes 1572872 | tf_op jit(solution)/shard_map/ppermute | solution.py:394
  54.1 16.6 %collective-permute-start.31 = (bf16[64,1024]{1,0:T(8,128)(2,1)}, bf16[64,1024]{1,0:T(8,128)(2,1)S(1)}, u32[]{:S(2)}, u32[]{:S(2)}) collective-permute-start(bf16[64,1024]{1,0:T(8,128)(2,1)} %get-tuple-element.133), channel_id=1, source_target_pairs={{0,5},{1,4},{2,7},{3,6},{4,1},{5,0},{6,3},{7,2},{8,13},{9,12},{10,... | collective-permute-start | bytes 393224 | tf_op jit(solution)/shard_map/ppermute | solution.py:398
  56.0 15.4 %collective-permute-start.32 = (bf16[64,1024]{1,0:T(8,128)(2,1)}, bf16[64,1024]{1,0:T(8,128)(2,1)S(1)}, u32[]{:S(2)}, u32[]{:S(2)}) collective-permute-start(bf16[64,1024]{1,0:T(8,128)(2,1)} %get-tuple-element.134), channel_id=1, source_target_pairs={{0,6},{1,7},{2,4},{3,5},{4,2},{5,3},{6,0},{7,1},{8,14},{9,15},{10,... | collective-permute-start | bytes 393224 | tf_op jit(solution)/shard_map/ppermute | solution.py:398
  57.2 16.6 %collective-permute-start.33 = (bf16[64,1024]{1,0:T(8,128)(2,1)}, bf16[64,1024]{1,0:T(8,128)(2,1)S(1)}, u32[]{:S(2)}, u32[]{:S(2)}) collective-permute-start(bf16[64,1024]{1,0:T(8,128)(2,1)} %get-tuple-element.135), channel_id=1, source_target_pairs={{0,7},{1,6},{2,5},{3,4},{4,3},{5,2},{6,1},{7,0},{8,15},{9,14},{10,... | collective-permute-start | bytes 393224 | tf_op jit(solution)/shard_map/ppermute | solution.py:398
  61.5 28.7 %all-to-all-start = ((bf16[8,24,1024]{2,1,0:T(8,128)(2,1)}), bf16[8,24,1024]{2,1,0:T(8,128)(2,1)S(1)}, u32[]{:S(2)}, u32[]{:S(2)}) async-start(bf16[8,24,1024]{2,1,0:T(8,128)(2,1)} %get-tuple-element.99), calls=%async_computation | async-start | bytes 786432 | tf_op jit(solution)/shard_map/all_to_all | solution.py:843
  71.4 3.5 %collective-permute-start.14 = (bf16[64,1024]{1,0:T(8,128)(2,1)}, bf16[64,1024]{1,0:T(8,128)(2,1)S(1)}, u32[]{:S(2)}, u32[]{:S(2)}) collective-permute-start(bf16[64,1024]{1,0:T(8,128)(2,1)} %get-tuple-element.111), channel_id=1, source_target_pairs={{0,1},{1,0},{2,3},{3,2},{4,5},{5,4},{6,7},{7,6},{8,9},{9,8},{10,11... | collective-permute-start | bytes 393224 | tf_op jit(solution)/shard_map/ppermute | solution.py:398
  72.2 5.2 %collective-permute-start.15 = (bf16[64,1024]{1,0:T(8,128)(2,1)}, bf16[64,1024]{1,0:T(8,128)(2,1)S(1)}, u32[]{:S(2)}, u32[]{:S(2)}) collective-permute-start(bf16[64,1024]{1,0:T(8,128)(2,1)} %get-tuple-element.112), channel_id=1, source_target_pairs={{0,2},{1,3},{2,0},{3,1},{4,6},{5,7},{6,4},{7,5},{8,10},{9,11},{10,... | collective-permute-start | bytes 393224 | tf_op jit(solution)/shard_map/ppermute | solution.py:398
  74.4 6.1 %collective-permute-start.16 = (bf16[64,1024]{1,0:T(8,128)(2,1)}, bf16[64,1024]{1,0:T(8,128)(2,1)S(1)}, u32[]{:S(2)}, u32[]{:S(2)}) collective-permute-start(bf16[64,1024]{1,0:T(8,128)(2,1)} %get-tuple-element.113), channel_id=1, source_target_pairs={{0,3},{1,2},{2,1},{3,0},{4,7},{5,6},{6,5},{7,4},{8,11},{9,10},{10,... | collective-permute-start | bytes 393224 | tf_op jit(solution)/shard_map/ppermute | solution.py:398
  74.8 7.2 %collective-permute-start.17 = (bf16[64,1024]{1,0:T(8,128)(2,1)}, bf16[64,1024]{1,0:T(8,128)(2,1)S(1)}, u32[]{:S(2)}, u32[]{:S(2)}) collective-permute-start(bf16[64,1024]{1,0:T(8,128)(2,1)} %get-tuple-element.114), channel_id=1, source_target_pairs={{0,4},{1,5},{2,6},{3,7},{4,0},{5,1},{6,2},{7,3},{8,12},{9,13},{10,... | collective-permute-start | bytes 393224 | tf_op jit(solution)/shard_map/ppermute | solution.py:398
  77.4 5.1 %collective-permute-start.2 = (bf16[64,1024]{1,0:T(8,128)(2,1)}, bf16[64,1024]{1,0:T(8,128)(2,1)S(1)}, u32[]{:S(2)}, u32[]{:S(2)}) collective-permute-start(bf16[64,1024]{1,0:T(8,128)(2,1)} %get-tuple-element.98), channel_id=1, source_target_pairs={{0,1},{1,0},{2,3},{3,2},{4,5},{5,4},{6,7},{7,6},{8,9},{9,8},{10,11... | collective-permute-start | bytes 393224 | tf_op jit(solution)/shard_map/ppermute | solution.py:398
  80.6 5.0 %collective-permute-start.21 = (bf16[64,1024]{1,0:T(8,128)(2,1)}, bf16[64,1024]{1,0:T(8,128)(2,1)S(1)}, u32[]{:S(2)}, u32[]{:S(2)}) collective-permute-start(bf16[64,1024]{1,0:T(8,128)(2,1)} %get-tuple-element.120), channel_id=1, source_target_pairs={{0,2},{1,3},{2,0},{3,1},{4,6},{5,7},{6,4},{7,5},{8,10},{9,11},{10,... | collective-permute-start | bytes 393224 | tf_op jit(solution)/shard_map/ppermute | solution.py:398
  82.0 16.1 %collective-permute-start.22 = (bf16[64,1024]{1,0:T(8,128)(2,1)}, bf16[64,1024]{1,0:T(8,128)(2,1)}, u32[]{:S(2)}, u32[]{:S(2)}) collective-permute-start(bf16[64,1024]{1,0:T(8,128)(2,1)} %get-tuple-element.121), channel_id=1, source_target_pairs={{0,3},{1,2},{2,1},{3,0},{4,7},{5,6},{6,5},{7,4},{8,11},{9,10},{10,... | collective-permute-start | bytes 393224 | tf_op jit(solution)/shard_map/ppermute | solution.py:398
  82.5 17.4 %collective-permute-start.23 = (bf16[64,1024]{1,0:T(8,128)(2,1)}, bf16[64,1024]{1,0:T(8,128)(2,1)}, u32[]{:S(2)}, u32[]{:S(2)}) collective-permute-start(bf16[64,1024]{1,0:T(8,128)(2,1)} %get-tuple-element.122), channel_id=1, source_target_pairs={{0,4},{1,5},{2,6},{3,7},{4,0},{5,1},{6,2},{7,3},{8,12},{9,13},{10,... | collective-permute-start | bytes 393224 | tf_op jit(solution)/shard_map/ppermute | solution.py:398
  85.6 15.4 %collective-permute-start.24 = (bf16[64,1024]{1,0:T(8,128)(2,1)}, bf16[64,1024]{1,0:T(8,128)(2,1)}, u32[]{:S(2)}, u32[]{:S(2)}) collective-permute-start(bf16[64,1024]{1,0:T(8,128)(2,1)} %get-tuple-element.123), channel_id=1, source_target_pairs={{0,5},{1,4},{2,7},{3,6},{4,1},{5,0},{6,3},{7,2},{8,13},{9,12},{10,... | collective-permute-start | bytes 393224 | tf_op jit(solution)/shard_map/ppermute | solution.py:398
  88.6 13.9 %collective-permute-start.25 = (bf16[64,1024]{1,0:T(8,128)(2,1)}, bf16[64,1024]{1,0:T(8,128)(2,1)}, u32[]{:S(2)}, u32[]{:S(2)}) collective-permute-start(bf16[64,1024]{1,0:T(8,128)(2,1)} %get-tuple-element.124), channel_id=1, source_target_pairs={{0,6},{1,7},{2,4},{3,5},{4,2},{5,3},{6,0},{7,1},{8,14},{9,15},{10,... | collective-permute-start | bytes 393224 | tf_op jit(solution)/shard_map/ppermute | solution.py:398
  89.8 12.8 %collective-permute-start.26 = (bf16[64,1024]{1,0:T(8,128)(2,1)}, bf16[64,1024]{1,0:T(8,128)(2,1)}, u32[]{:S(2)}, u32[]{:S(2)}) collective-permute-start(bf16[64,1024]{1,0:T(8,128)(2,1)} %get-tuple-element.125), channel_id=1, source_target_pairs={{0,7},{1,6},{2,5},{3,4},{4,3},{5,2},{6,1},{7,0},{8,15},{9,14},{10,... | collective-permute-start | bytes 393224 | tf_op jit(solution)/shard_map/ppermute | solution.py:398
  91.0 19.4 %all-to-all-start.1 = ((bf16[8,16,1024]{2,1,0:T(8,128)(2,1)}), bf16[8,16,1024]{2,1,0:T(8,128)(2,1)S(1)}, u32[]{:S(2)}, u32[]{:S(2)}) async-start(bf16[8,16,1024]{2,1,0:T(8,128)(2,1)} %shard_map.164), calls=%async_computation.1 | async-start | bytes 524288 | tf_op jit(solution)/shard_map/all_to_all | solution.py:843
  98.2 17.0 %collective-permute-start.18 = (bf16[64,1024]{1,0:T(8,128)(2,1)}, bf16[64,1024]{1,0:T(8,128)(2,1)S(1)}, u32[]{:S(2)}, u32[]{:S(2)}) collective-permute-start(bf16[64,1024]{1,0:T(8,128)(2,1)} %get-tuple-element.115), channel_id=1, source_target_pairs={{0,5},{1,4},{2,7},{3,6},{4,1},{5,0},{6,3},{7,2},{8,13},{9,12},{10,... | collective-permute-start | bytes 393224 | tf_op jit(solution)/shard_map/ppermute | solution.py:398
  99.8 16.2 %collective-permute-start.19 = (bf16[64,1024]{1,0:T(8,128)(2,1)}, bf16[64,1024]{1,0:T(8,128)(2,1)S(1)}, u32[]{:S(2)}, u32[]{:S(2)}) collective-permute-start(bf16[64,1024]{1,0:T(8,128)(2,1)} %get-tuple-element.116), channel_id=1, source_target_pairs={{0,6},{1,7},{2,4},{3,5},{4,2},{5,3},{6,0},{7,1},{8,14},{9,15},{10,... | collective-permute-start | bytes 393224 | tf_op jit(solution)/shard_map/ppermute | solution.py:398
  101.0 15.2 %collective-permute-start.20 = (bf16[64,1024]{1,0:T(8,128)(2,1)}, bf16[64,1024]{1,0:T(8,128)(2,1)}, u32[]{:S(2)}, u32[]{:S(2)}) collective-permute-start(bf16[64,1024]{1,0:T(8,128)(2,1)} %get-tuple-element.117), channel_id=1, source_target_pairs={{0,7},{1,6},{2,5},{3,4},{4,3},{5,2},{6,1},{7,0},{8,15},{9,14},{10,... | collective-permute-start | bytes 393224 | tf_op jit(solution)/shard_map/ppermute | solution.py:398
  102.5 15.2 %collective-permute-start.6 = (bf16[64,1024]{1,0:T(8,128)(2,1)}, bf16[64,1024]{1,0:T(8,128)(2,1)}, u32[]{:S(2)}, u32[]{:S(2)}) collective-permute-start(bf16[64,1024]{1,0:T(8,128)(2,1)} %get-tuple-element.102), channel_id=1, source_target_pairs={{0,1},{1,0},{2,3},{3,2},{4,5},{5,4},{6,7},{7,6},{8,9},{9,8},{10,11... | collective-permute-start | bytes 393224 | tf_op jit(solution)/shard_map/ppermute | solution.py:398
  102.6 16.2 %collective-permute-start.7 = (bf16[64,1024]{1,0:T(8,128)(2,1)}, bf16[64,1024]{1,0:T(8,128)(2,1)}, u32[]{:S(2)}, u32[]{:S(2)}) collective-permute-start(bf16[64,1024]{1,0:T(8,128)(2,1)} %get-tuple-element.103), channel_id=1, source_target_pairs={{0,2},{1,3},{2,0},{3,1},{4,6},{5,7},{6,4},{7,5},{8,10},{9,11},{10,... | collective-permute-start | bytes 393224 | tf_op jit(solution)/shard_map/ppermute | solution.py:398
  115.2 12.5 %collective-permute-start.8 = (bf16[64,1024]{1,0:T(8,128)(2,1)S(1)}, bf16[64,1024]{1,0:T(8,128)(2,1)S(1)}, u32[]{:S(2)}, u32[]{:S(2)}) collective-permute-start(bf16[64,1024]{1,0:T(8,128)(2,1)S(1)} %copy-done.34), channel_id=1, source_target_pairs={{0,3},{1,2},{2,1},{3,0},{4,7},{5,6},{6,5},{7,4},{8,11},{9,10},{10,... | collective-permute-start | bytes 393224 | tf_op jit(solution)/shard_map/ppermute | solution.py:398
  116.1 11.6 %collective-permute-start.9 = (bf16[64,1024]{1,0:T(8,128)(2,1)S(1)}, bf16[64,1024]{1,0:T(8,128)(2,1)S(1)}, u32[]{:S(2)}, u32[]{:S(2)}) collective-permute-start(bf16[64,1024]{1,0:T(8,128)(2,1)S(1)} %copy-done.33), channel_id=1, source_target_pairs={{0,4},{1,5},{2,6},{3,7},{4,0},{5,1},{6,2},{7,3},{8,12},{9,13},{10,... | collective-permute-start | bytes 393224 | tf_op jit(solution)/shard_map/ppermute | solution.py:398
  116.2 13.5 %collective-permute-start.10 = (bf16[64,1024]{1,0:T(8,128)(2,1)S(1)}, bf16[64,1024]{1,0:T(8,128)(2,1)S(1)}, u32[]{:S(2)}, u32[]{:S(2)}) collective-permute-start(bf16[64,1024]{1,0:T(8,128)(2,1)S(1)} %copy-done.32), channel_id=1, source_target_pairs={{0,5},{1,4},{2,7},{3,6},{4,1},{5,0},{6,3},{7,2},{8,13},{9,12},{10,... | collective-permute-start | bytes 393224 | tf_op jit(solution)/shard_map/ppermute | solution.py:398
  117.7 12.1 %collective-permute-start.11 = (bf16[64,1024]{1,0:T(8,128)(2,1)S(1)}, bf16[64,1024]{1,0:T(8,128)(2,1)S(1)}, u32[]{:S(2)}, u32[]{:S(2)}) collective-permute-start(bf16[64,1024]{1,0:T(8,128)(2,1)S(1)} %copy-done.31), channel_id=1, source_target_pairs={{0,6},{1,7},{2,4},{3,5},{4,2},{5,3},{6,0},{7,1},{8,14},{9,15},{10,... | collective-permute-start | bytes 393224 | tf_op jit(solution)/shard_map/ppermute | solution.py:398
  118.8 11.0 %collective-permute-start.12 = (bf16[64,1024]{1,0:T(8,128)(2,1)S(1)}, bf16[64,1024]{1,0:T(8,128)(2,1)S(1)}, u32[]{:S(2)}, u32[]{:S(2)}) collective-permute-start(bf16[64,1024]{1,0:T(8,128)(2,1)S(1)} %copy-done.30), channel_id=1, source_target_pairs={{0,7},{1,6},{2,5},{3,4},{4,3},{5,2},{6,1},{7,0},{8,15},{9,14},{10,... | collective-permute-start | bytes 393224 | tf_op jit(solution)/shard_map/ppermute | solution.py:398
  135.5 54.2 %all-to-all-start.2 = ((bf16[32,32,1024]{2,1,0:T(8,128)(2,1)}), bf16[32,32,1024]{2,1,0:T(8,128)(2,1)S(1)}, u32[]{:S(2)}, u32[]{:S(2)}) async-start(bf16[32,32,1024]{2,1,0:T(8,128)(2,1)} %bitcast.35), calls=%async_computation.2 | async-start | bytes 4194304 | tf_op jit(solution)/shard_map/all_to_all | solution.py:843
  193.2 24.9 %all-to-all-start.3 = ((bf16[8,16,1024]{2,1,0:T(8,128)(2,1)}), bf16[8,16,1024]{2,1,0:T(8,128)(2,1)S(1)}, u32[]{:S(2)}, u32[]{:S(2)}) async-start(bf16[8,16,1024]{2,1,0:T(8,128)(2,1)} %bitcast.39), calls=%async_computation.3 | async-start | bytes 524288 | tf_op jit(solution)/shard_map/all_to_all | solution.py:843
  197.9 3.6 %collective-permute-start.35 = (f32[8,256]{1,0:T(8,128)S(1)}, f32[8,256]{1,0:T(8,128)S(1)}, u32[]{:S(2)}, u32[]{:S(2)}) collective-permute-start(f32[8,256]{1,0:T(8,128)S(1)} %get-tuple-element.186), channel_id=1, source_target_pairs={{0,16},{8,24},{16,0},{24,8},{1,17},{9,25},{17,1},{25,9},{2,18},{10... | collective-permute-start | bytes 24584 | tf_op jit(solution)/shard_map/ppermute | solution.py:394
  198.1 3.4 %collective-permute-start.34 = (f32[8,256]{1,0:T(8,128)S(1)}, f32[8,256]{1,0:T(8,128)S(1)}, u32[]{:S(2)}, u32[]{:S(2)}) collective-permute-start(f32[8,256]{1,0:T(8,128)S(1)} %get-tuple-element.187), channel_id=1, source_target_pairs={{0,8},{8,0},{16,24},{24,16},{1,9},{9,1},{17,25},{25,17},{2,10},{10... | collective-permute-start | bytes 24584 | tf_op jit(solution)/shard_map/ppermute | solution.py:394
  199.8 4.3 %collective-permute-start.36 = (f32[8,256]{1,0:T(8,128)S(1)}, f32[8,256]{1,0:T(8,128)S(1)}, u32[]{:S(2)}, u32[]{:S(2)}) collective-permute-start(f32[8,256]{1,0:T(8,128)S(1)} %bitcast.43), channel_id=1, source_target_pairs={{0,24},{8,16},{16,8},{24,0},{1,25},{9,17},{17,9},{25,1},{2,26},{10... | collective-permute-start | bytes 24584 | tf_op jit(solution)/shard_map/ppermute | solution.py:394
  204.9 5.5 %collective-permute-start.37 = (f32[8,128]{1,0:T(8,128)S(1)}, f32[8,128]{1,0:T(8,128)S(1)}, u32[]{:S(2)}, u32[]{:S(2)}) collective-permute-start(f32[8,128]{1,0:T(8,128)S(1)} %get-tuple-element.177), channel_id=1, source_target_pairs={{0,1},{1,0},{2,3},{3,2},{4,5},{5,4},{6,7},{7,6},{8,9},{9,8},{10,11... | collective-permute-start | bytes 12296 | tf_op jit(solution)/shard_map/ppermute | solution.py:398
  206.7 6.1 %collective-permute-start.38 = (f32[8,128]{1,0:T(8,128)S(1)}, f32[8,128]{1,0:T(8,128)S(1)}, u32[]{:S(2)}, u32[]{:S(2)}) collective-permute-start(f32[8,128]{1,0:T(8,128)S(1)} %get-tuple-element.178), channel_id=1, source_target_pairs={{0,2},{1,3},{2,0},{3,1},{4,6},{5,7},{6,4},{7,5},{8,10},{9,11},{10,... | collective-permute-start | bytes 12296 | tf_op jit(solution)/shard_map/ppermute | solution.py:398
  208.4 4.7 %collective-permute-start.39 = (f32[8,128]{1,0:T(8,128)S(1)}, f32[8,128]{1,0:T(8,128)S(1)}, u32[]{:S(2)}, u32[]{:S(2)}) collective-permute-start(f32[8,128]{1,0:T(8,128)S(1)} %get-tuple-element.179), channel_id=1, source_target_pairs={{0,3},{1,2},{2,1},{3,0},{4,7},{5,6},{6,5},{7,4},{8,11},{9,10},{10,... | collective-permute-start | bytes 12296 | tf_op jit(solution)/shard_map/ppermute | solution.py:398
  208.5 4.6 %collective-permute-start.40 = (f32[8,128]{1,0:T(8,128)S(1)}, f32[8,128]{1,0:T(8,128)S(1)}, u32[]{:S(2)}, u32[]{:S(2)}) collective-permute-start(f32[8,128]{1,0:T(8,128)S(1)} %get-tuple-element.180), channel_id=1, source_target_pairs={{0,4},{1,5},{2,6},{3,7},{4,0},{5,1},{6,2},{7,3},{8,12},{9,13},{10,... | collective-permute-start | bytes 12296 | tf_op jit(solution)/shard_map/ppermute | solution.py:398
  210.1 3.1 %collective-permute-start.41 = (f32[8,128]{1,0:T(8,128)S(1)}, f32[8,128]{1,0:T(8,128)S(1)}, u32[]{:S(2)}, u32[]{:S(2)}) collective-permute-start(f32[8,128]{1,0:T(8,128)S(1)} %get-tuple-element.181), channel_id=1, source_target_pairs={{0,5},{1,4},{2,7},{3,6},{4,1},{5,0},{6,3},{7,2},{8,13},{9,12},{10,... | collective-permute-start | bytes 12296 | tf_op jit(solution)/shard_map/ppermute | solution.py:398
  210.4 3.4 %collective-permute-start.42 = (f32[8,128]{1,0:T(8,128)S(1)}, f32[8,128]{1,0:T(8,128)S(1)}, u32[]{:S(2)}, u32[]{:S(2)}) collective-permute-start(f32[8,128]{1,0:T(8,128)S(1)} %get-tuple-element.182), channel_id=1, source_target_pairs={{0,6},{1,7},{2,4},{3,5},{4,2},{5,3},{6,0},{7,1},{8,14},{9,15},{10,... | collective-permute-start | bytes 12296 | tf_op jit(solution)/shard_map/ppermute | solution.py:398
  212.8 3.9 %collective-permute-start.43 = (f32[8,128]{1,0:T(8,128)S(1)}, f32[8,128]{1,0:T(8,128)S(1)}, u32[]{:S(2)}, u32[]{:S(2)}) collective-permute-start(f32[8,128]{1,0:T(8,128)S(1)} %get-tuple-element.183), channel_id=1, source_target_pairs={{0,7},{1,6},{2,5},{3,4},{4,3},{5,2},{6,1},{7,0},{8,15},{9,14},{10,... | collective-permute-start | bytes 12296 | tf_op jit(solution)/shard_map/ppermute | solution.py:398
  218.9 14.8 %all-to-all-start.4 = ((bf16[8,16,1024]{2,1,0:T(8,128)(2,1)}), bf16[8,16,1024]{2,1,0:T(8,128)(2,1)S(1)}, u32[]{:S(2)}, u32[]{:S(2)}) async-start(bf16[8,16,1024]{2,1,0:T(8,128)(2,1)} %shard_map.175), calls=%async_computation.4 | async-start | bytes 524288 | tf_op jit(solution)/shard_map/all_to_all | solution.py:843
  (39 other events, 499.0 us)

commit v3 on v2

--- a/solution.py
+++ b/solution.py
@@ -351,7 +351,7 @@
         cost_estimate=pl.CostEstimate(
             flops=flops, bytes_accessed=6 * width * width, transcendentals=0
         ),
-    )(me, *from_hbm(*parts), *extras)
+    )(me, *parts, *extras)
 
 
 def outer_kernel(*refs):
@@ -418,15 +418,16 @@
         kernel = functools.partial(pick_grads_kernel, count, cap)
         return streamed(kernel, tuple(outs), keys, *grads)
 
-    def pick_both(message, grad):
+    def pick_both(message, grad, near):
         outs = [far_shape((2 * cap, width), BF16)] * shard_count
         kernel = functools.partial(pick_both_kernel, cap)
-        return streamed(kernel, tuple(outs), message, grad, scalars=me)
+        return streamed(kernel, tuple(outs), message, grad, scalars=me, near=near)
 
     def block(width):
         return pl.BlockSpec((group, width), lambda i, me: (i, 0))
 
     def hidden_stage(parts, steps):
+        parts = from_hbm(*parts)
         rows = steps * group
         return grouped(
             hidden_kernel,
@@ -502,8 +503,9 @@
     grad2 = across(out_grad, 2)
     grad1 = across(out_grad, 1)
     message3 = across(message2, 1)
-    own = pick_both(message, out_grad)
+    own = pick_both(message, out_grad, ())
     own = spread_out(own)
+    own = from_hbm(*own)
     rows_0, act_0, scaled_0, pre_0, row_grad, own_terms = whole_stage(own, 0, None)
     near_rows, near_keys = pick_rows([message1, message2])
     near_rows = spread_out(near_rows)
@@ -513,7 +515,7 @@
     near_grads = pick_grads(near_keys, [grad1, grad2])
     near_grads = spread_out(near_grads)
     rows_1, act_1, slope_1 = hidden_stage(near_rows, 2)
-    far = pick_both(message3, grad3)
+    far = pick_both(message3, grad3, (0, 1))
     far = spread_out(far)
     scaled_1, pre_1, row_grad, near_terms = routed_stage(near_grads, act_1, slope_1, 2, 1, row_grad)
     rows_2, act_2, scaled_2, pre_2, row_grad, far_terms = whole_stage(far, 3, row_grad)
@@ -522,6 +524,9 @@
         blocks = [own_terms[0]]
         blocks += [across(near_terms[bit - 1], bit) for bit in (1, 2)]
         blocks += [across(far_terms[0], 3)]
+        down_grad = outer_stage((act_0, scaled_0), (act_1, scaled_1), (act_2, scaled_2))
+        up_grad = outer_stage((rows_0, pre_0), (rows_1, pre_1), (rows_2, pre_2))
+        blocks, down_grad, up_grad = lax.optimization_barrier((blocks, down_grad, up_grad))
         mixed = call(
             functools.partial(mix_kernel, planes, cap),
             tuple([shape((8, 128), F32)] * shard_count),
@@ -529,9 +534,7 @@
             *blocks,
             in_specs=[smem] + [vmem] * planes,
         )
-        down_grad = outer_stage((act_0, scaled_0), (act_1, scaled_1), (act_2, scaled_2))
         mixed = spread_out(mixed)
-        up_grad = outer_stage((rows_0, pre_0), (rows_1, pre_1), (rows_2, pre_2))
         gate_grad = call(
             functools.partial(found_kernel, cap, shard_count),
             far_shape((2, tokens), F32),

time: 239 us -> 231 us (0.967)
  waiting for transfers between devices: 83.9 us -> 78 us
    all_to_all x5, waiting for transfers between devices: 35.4 us -> 0.01 us  [swap(): return lax.all_to_all(x, axes, split_axis=0, concat_axis=0, tiled=True)]
    ppermute x9, waiting for transfers between devices: 33.2 us -> 63 us  [across(): return lax.ppermute(x, 'grp', [(i, i ^ bit) for i in range(planes)])]
    unnamed x76 -> x58, local copies, waits for them, and re-layouts: 5.59 us -> 5.52 us
  transfers between devices with their start and end apart: 49 -> 49, of which waited for: 13 -> 11; matrix products, arithmetic and copies ran while one was open for 1% -> 1% of each run, Pallas kernels for 23% -> 24%
where the time goes in v3:
time: 231 us; the launch traced here: 229 us
  waiting for transfers between devices  78 us (34%)
  starting transfers between devices  74.7 us (32%)
  Pallas kernels  68.7 us (30%)
  local copies, waits for them, and re-layouts  5.53 us (2%)
    ppermute x9, waiting for transfers between devices, across(): return lax.ppermute(x, 'grp', [(i, i ^ bit) for i in range(planes)])  63 us
    pallas_call x16, Pallas kernels, call(): pl.pallas_call(kernel, out_shape=outs, in_specs=in_specs if in_specs is n...  48.9 us
    ppermute x35, starting transfers between devices, spread_out(): lax.ppermute(part, 'seq', [(i, i ^ x) for i in range(shard_count)])  40.7 us
    all_to_all x5, starting transfers between devices, swap(): return lax.all_to_all(x, axes, split_axis=0, concat_axis=0, tiled=True)  23.5 us
    pallas_call x4, Pallas kernels, grouped(): pl.pallas_call(functools.partial(kernel, len(parts)), out_shape=outs, gri...  19.8 us
    ppermute x35, waiting for transfers between devices, spread_out(): lax.ppermute(part, 'seq', [(i, i ^ x) for i in range(shard_count)])  15 us
    ppermute x9, starting transfers between devices, across(): return lax.ppermute(x, 'grp', [(i, i ^ bit) for i in range(planes)])  10.5 us
    unnamed x58, local copies, waits for them, and re-layouts  5.52 us
  transfers between devices with their start and end apart: 49, of which 11 were waited for; matrix products, arithmetic and copies ran while one was open for 1% of the time, Pallas kernels for 24%

profile of v3, /device:TPU:1, one launch (start us, length us, event | category | flops | bytes accessed | tf_op | source)
XLA Modules:
  0.0 229.1 jit_solution(15269780602494805657)
XLA Ops:
  0.6 2.1 shard_map.161
  2.7 3.1 %collective-permute-start.1 = (bf16[272,1024]{1,0:T(8,128)(2,1)}, bf16[272,1024]{1,0:T(8,128)(2,1)}, u32[]{:S(2)}, u32[]{:S(2)}) collective-permute-start(bf16[272,1024]{1,0:T(8,128)(2,1)} %get-tuple-element.103.message_ref), channel_id=1, source_target_pairs={{0,16},{8,24},{16,0},{24,8},{1,17},{9,25},{17,1},{25,9},{2,18},{10... | collective-permute-start | bytes 1671176 | tf_op jit(solution)/shard_map/ppermute | solution.py:394
  5.9 1.3 collective-permute-start
  7.3 2.6 %shard_map.168 = (bf16[64,1024]{1,0:T(8,128)(2,1)}, bf16[64,1024]{1,0:T(8,128)(2,1)}, bf16[64,1024]{1,0:T(8,128)(2,1)}, bf16[64,1024]{1,0:T(8,128)(2,1)}, bf16[6...) custom-call(s32[2]{0:T(128)S(1)} %pad_add_fusion.me_ref, ...), custom_call_target="tpu_custom_call" | custom-call | tf_op jit(solution)/shard_map/pallas_call | solution.py:33
  9.8 1.5 collective-permute-start.27
  13.8 3.8 %collective-permute-done.28.refs_2_ = bf16[64,1024]{1,0:T(8,128)(2,1)S(1)} collective-permute-done((bf16[64,1024]{1,0:T(8,128)(2,1)}, bf16[64,1024]{1,0:T(8,128)(2,1)S(1)}, u32[]{:S(2)}, u32[]{:S(2)}) %collective-permute-start.28) | collective-permute-done | bytes 131104 | tf_op jit(solution)/shard_map/ppermute | solution.py:398
  17.6 2.2 collective-permute-start.29
  19.8 21.9 %collective-permute-done.1.refs_1_ = bf16[272,1024]{1,0:T(8,128)(2,1)} collective-permute-done((bf16[272,1024]{1,0:T(8,128)(2,1)}, bf16[272,1024]{1,0:T(8,128)(2,1)}, u32[]{:S(2)}, u32[]{:S(2)}) %collective-permute-start.1) | collective-permute-done | bytes 557088 | tf_op jit(solution)/shard_map/ppermute | solution.py:394
  44.1 8.8 %collective-permute-done.4.refs_1_ = bf16[256,1024]{1,0:T(8,128)(2,1)} collective-permute-done((bf16[256,1024]{1,0:T(8,128)(2,1)}, bf16[256,1024]{1,0:T(8,128)(2,1)}, u32[]{:S(2)}, u32[]{:S(2)}) %collective-permute-start.4) | collective-permute-done | bytes 524320 | tf_op jit(solution)/shard_map/ppermute | solution.py:394
  54.1 1.9 collective-permute-start.31
  58.4 3.2 %shard_map.163 = (f32[256,16]{1,0:T(8,128)}, f32[16,1,256]{2,1,0:T(1,128)}, bf16[256,1024]{1,0:T(8,128)(2,1)}, bf16[256,1024]{1,0:T(8,128)(2,1)}, bf16[256,1024]...) custom-call(bf16[256,1024]{1,0:T(8,128)(2,1)} %inputs_ref.5, bf16[256,128]{1,0:T(8,128)(2,1)} %writes_ref.7, f32[16,256]{1,0:T(8,128)} %bitcast.37), custom_call_target="tpu_custom_call" | custom-call | tf_op jit(solution)/shard_map/pallas_call | solution.py:33
  61.6 3.8 %all-to-all-start = ((bf16[8,24,1024]{2,1,0:T(8,128)(2,1)}), bf16[8,24,1024]{2,1,0:T(8,128)(2,1)S(1)}, u32[]{:S(2)}, u32[]{:S(2)}) async-start(bf16[8,24,1024]{2,1,0:T(8,128)(2,1)} %get-tuple-element.105), calls=%async_computation | async-start | bytes 786432 | tf_op jit(solution)/shard_map/all_to_all | solution.py:846
  65.5 2.6 %shard_map.162 = (bf16[64,1024]{1,0:T(8,128)(2,1)}, bf16[64,1024]{1,0:T(8,128)(2,1)}, bf16[64,1024]{1,0:T(8,128)(2,1)}, bf16[64,1024]{1,0:T(8,128)(2,1)}, bf16[6...) custom-call(s32[2]{0:T(128)S(1)} %pad_add_fusion.me_ref, ...), custom_call_target="tpu_custom_call" | custom-call | tf_op jit(solution)/shard_map/pallas_call | solution.py:33
  68.1 2.7 %shard_map.166 = (bf16[64,1024]{1,0:T(8,128)(2,1)}, bf16[64,1024]{1,0:T(8,128)(2,1)}, bf16[64,1024]{1,0:T(8,128)(2,1)}, bf16[64,1024]{1,0:T(8,128)(2,1)}, bf16[6...) custom-call(f32[2,8,256]{2,1,0:T(8,128)} %get-tuple-element.115.keys_ref, ...), custom_call_target="tpu_custom_call" | custom-call | tf_op jit(solution)/shard_map/pallas_call | solution.py:33
  72.2 1.6 collective-permute-start.15
  74.9 1.4 collective-permute-start.17
  77.4 1.5 collective-permute-start.2
  78.9 1.8 collective-permute-done.16.refs_3_
  80.6 1.4 collective-permute-start.21
  85.6 3.0 %collective-permute-start.24 = (bf16[64,1024]{1,0:T(8,128)(2,1)}, bf16[64,1024]{1,0:T(8,128)(2,1)}, u32[]{:S(2)}, u32[]{:S(2)}) collective-permute-start(bf16[64,1024]{1,0:T(8,128)(2,1)} %get-tuple-element.129), channel_id=1, source_target_pairs={{0,5},{1,4},{2,7},{3,6},{4,1},{5,0},{6,3},{7,2},{8,13},{9,12},{10,... | collective-permute-start | bytes 393224 | tf_op jit(solution)/shard_map/ppermute | solution.py:398
  91.0 5.2 %all-to-all-start.1 = ((bf16[8,16,1024]{2,1,0:T(8,128)(2,1)}), bf16[8,16,1024]{2,1,0:T(8,128)(2,1)}, u32[]{:S(2)}, u32[]{:S(2)}) async-start(bf16[8,16,1024]{2,1,0:T(8,128)(2,1)} %shard_map.164), calls=%async_computation.1 | async-start | bytes 524288 | tf_op jit(solution)/shard_map/all_to_all | solution.py:846
  96.2 2.4 %shard_map.165 = (bf16[64,1024]{1,0:T(8,128)(2,1)}, bf16[64,1024]{1,0:T(8,128)(2,1)}, bf16[64,1024]{1,0:T(8,128)(2,1)}, bf16[64,1024]{1,0:T(8,128)(2,1)}, bf16[6...) custom-call(s32[2]{0:T(128)S(1)} %pad_add_fusion.me_ref, ...), custom_call_target="tpu_custom_call" | custom-call | tf_op jit(solution)/shard_map/pallas_call | solution.py:33
  98.6 1.6 collective-permute-start.18
  101.4 1.5 collective-permute-start.20
  104.3 1.6 copy-done.1
  105.8 5.0 %shard_map.169 = (bf16[256,1024]{1,0:T(8,128)(2,1)}, bf16[256,1024]{1,0:T(8,128)(2,1)}, bf16[256,1024]{1,0:T(8,128)(2,1)}, bf16[256,1024]{1,0:T(8,128)(2,1)}, bf...) custom-call(s32[2]{0:T(128)S(1)} %pad_add_fusion.me_ref, bf16[64,1024]{1,0:T(8,128)(2,1)} %get-tuple-element.134.refs_0_, ...), custom_call_target="tpu_custom_call" | custom-call | flops 1610612736 | bytes 6291456 | tf_op jit(solution)/shard_map/pallas_call | solution.py:340
  110.9 4.5 %shard_map.167 = (bf16[512,1024]{1,0:T(8,128)(2,1)}, bf16[512,1024]{1,0:T(8,128)(2,1)}, f32[512,1024]{1,0:T(8,128)S(1)}) custom-call(s32[2]{0:T(128)S(1)} %pad_add_fusion.me_ref, bf16[64,1024]{1,0:T(8,128)(2,1)} %get-tuple-element.124.refs_0_, bf16[64,1024]{1,0:T(8,128)(2,1)} %copy-done.26, bf16[64,1024]{1,0:T(8,128)(2,1)} %copy-done.27, ...), custom_call_target="tpu_custom_call" | custom-call | flops 1073741824 | bytes 6291456 | tf_op jit(solution)/shard_map/pallas_call | solution.py:340
  116.5 1.5 collective-permute-start.10
  119.1 1.8 collective-permute-start.12
  122.0 5.6 %shard_map.170 = (bf16[512,1024]{1,0:T(8,128)(2,1)}, bf16[512,1024]{1,0:T(8,128)(2,1)}, bf16[4,256,1024]{2,1,0:T(8,128)(2,1)}, f32[2,8,256]{2,1,0:T(8,128)}) custom-call(s32[2]{0:T(128)S(1)} %pad_add_fusion.me_ref, bf16[64,1024]{1,0:T(8,128)(2,1)S(1)} %copy-done.4, ...), custom_call_target="tpu_custom_call", output_to_operand_aliasing={{2}: (13, {})} | custom-call | flops 2147483648 | bytes 6291456 | tf_op jit(solution)/shard_map/pallas_call | solution.py:340
  127.7 2.4 %collective-permute-done.10.refs_5_ = bf16[64,1024]{1,0:T(8,128)(2,1)S(1)} collective-permute-done((bf16[64,1024]{1,0:T(8,128)(2,1)S(1)}, bf16[64,1024]{1,0:T(8,128)(2,1)S(1)}, u32[]{:S(2)}, u32[]{:S(2)}) %collective-permute-start.10) | collective-permute-done | bytes 131104 | tf_op jit(solution)/shard_map/ppermute | solution.py:398
  130.1 4.6 %shard_map.171 = (bf16[256,1024]{1,0:T(8,128)(2,1)}, bf16[256,1024]{1,0:T(8,128)(2,1)}, bf16[256,1024]{1,0:T(8,128)(2,1)}, bf16[256,1024]{1,0:T(8,128)(2,1)}, bf...) custom-call(s32[2]{0:T(128)S(1)} %pad_add_fusion.me_ref, ...), custom_call_target="tpu_custom_call", output_to_operand_aliasing={{4}: (11, {})} | custom-call | flops 1610612736 | bytes 6291456 | tf_op jit(solution)/shard_map/pallas_call | solution.py:340
  134.7 6.0 %all-to-all-start.2 = ((bf16[32,32,1024]{2,1,0:T(8,128)(2,1)}), bf16[32,32,1024]{2,1,0:T(8,128)(2,1)S(1)}, u32[]{:S(2)}, u32[]{:S(2)}) async-start(bf16[32,32,1024]{2,1,0:T(8,128)(2,1)} %bitcast.35), calls=%async_computation.2 | async-start | bytes 4194304 | tf_op jit(solution)/shard_map/all_to_all | solution.py:846
  140.8 2.3 %collective-permute-start.35 = (f32[8,256]{1,0:T(8,128)S(1)}, f32[8,256]{1,0:T(8,128)S(1)}, u32[]{:S(2)}, u32[]{:S(2)}) collective-permute-start(f32[8,256]{1,0:T(8,128)S(1)} %get-tuple-element.198), channel_id=1, source_target_pairs={{0,16},{8,24},{16,0},{24,8},{1,17},{9,25},{17,1},{25,9},{2,18},{10... | collective-permute-start | bytes 24584 | tf_op jit(solution)/shard_map/ppermute | solution.py:394
  144.4 6.3 %shard_map.172 = bf16[1024,1024]{1,0:T(8,128)(2,1)} custom-call(bf16[256,1024]{1,0:T(8,128)(2,1)} %get-tuple-element.148.refs_0_, bf16[256,1024]{1,0:T(8,128)(2,1)} %get-tuple-element.149.refs_1_, bf16[512,1024]{1,0:T(8,128)(2,1)} %get-tuple-element.132.refs_8_.refs_2_, bf16[512,1024]{1,0:T(8,128)(2,1)} %get-tuple-element.150.refs_3_, ...), custom_call_target="tpu_custom_call" | custom-call | flops 2147483648 | bytes 6291456 | tf_op jit(solution)/shard_map/pallas_call | solution.py:33
  150.7 6.3 %shard_map.173 = bf16[1024,1024]{1,0:T(8,128)(2,1)} custom-call(bf16[256,1024]{1,0:T(8,128)(2,1)} %get-tuple-element.153.refs_0_, bf16[256,1024]{1,0:T(8,128)(2,1)} %get-tuple-element.154.refs_1_, bf16[512,1024]{1,0:T(8,128)(2,1)} %get-tuple-element.155.refs_2_, bf16[512,1024]{1,0:T(8,128)(2,1)} %get-tuple-element.156.refs_3_, ...), custom_call_target="tpu_custom_call" | custom-call | flops 2147483648 | bytes 6291456 | tf_op jit(solution)/shard_map/pallas_call | solution.py:33
  157.0 32.3 %collective-permute-done.35.refs_2_ = f32[8,256]{1,0:T(8,128)S(1)} collective-permute-done((f32[8,256]{1,0:T(8,128)S(1)}, f32[8,256]{1,0:T(8,128)S(1)}, u32[]{:S(2)}, u32[]{:S(2)}) %collective-permute-start.35) | collective-permute-done | bytes 8224 | tf_op jit(solution)/shard_map/ppermute | solution.py:394
  189.3 3.5 %shard_map.174 = (bf16[256,1024]{1,0:T(8,128)(2,1)}, bf16[128,1024]{1,0:T(8,128)(2,1)}) custom-call(bf16[1024,1024]{1,0:T(8,128)(2,1)S(1)} %bitcast.23, s32[2,256]{1,0:T(2,128)} %get-tuple-element.162.targets_ref, bf16[256,1024]{1,0:T(8,128)(2,1)} %resid_ref.3, bf16[256,1024]{1,0:T(8,128)(2,1)} %out_grad_ref.1, bf16[256,128]{1,0:T(8,128)(2,1)} %reads_ref.5, ...), custom_call_target="tpu_custom_call" | custom-call | tf_op jit(solution)/shard_map/pallas_call | solution.py:33
  192.8 4.8 %all-to-all-start.3 = ((bf16[8,16,1024]{2,1,0:T(8,128)(2,1)}), bf16[8,16,1024]{2,1,0:T(8,128)(2,1)S(1)}, u32[]{:S(2)}, u32[]{:S(2)}) async-start(bf16[8,16,1024]{2,1,0:T(8,128)(2,1)} %bitcast.36), calls=%async_computation.3 | async-start | bytes 524288 | tf_op jit(solution)/shard_map/all_to_all | solution.py:846
  198.4 1.7 collective-permute-start.38
  200.5 1.4 collective-permute-start.40
  202.2 2.4 %collective-permute-start.42 = (f32[8,128]{1,0:T(8,128)S(1)}, f32[8,128]{1,0:T(8,128)S(1)}, u32[]{:S(2)}, u32[]{:S(2)}) collective-permute-start(f32[8,128]{1,0:T(8,128)S(1)} %get-tuple-element.194), channel_id=1, source_target_pairs={{0,6},{1,7},{2,4},{3,5},{4,2},{5,3},{6,0},{7,1},{8,14},{9,15},{10,... | collective-permute-start | bytes 12296 | tf_op jit(solution)/shard_map/ppermute | solution.py:398
  205.5 2.9 %collective-permute-done.43.refs_7_ = f32[8,128]{1,0:T(8,128)S(1)} collective-permute-done((f32[8,128]{1,0:T(8,128)S(1)}, f32[8,128]{1,0:T(8,128)S(1)}, u32[]{:S(2)}, u32[]{:S(2)}) %collective-permute-start.43) | collective-permute-done | bytes 4128 | tf_op jit(solution)/shard_map/ppermute | solution.py:398
  208.5 1.4 shard_map.180
  210.7 3.7 %all-to-all-start.4 = ((bf16[8,16,1024]{2,1,0:T(8,128)(2,1)}), bf16[8,16,1024]{2,1,0:T(8,128)(2,1)S(1)}, u32[]{:S(2)}, u32[]{:S(2)}) async-start(bf16[8,16,1024]{2,1,0:T(8,128)(2,1)} %shard_map.175), calls=%async_computation.4 | async-start | bytes 524288 | tf_op jit(solution)/shard_map/all_to_all | solution.py:846
  215.6 4.9 %shard_map.177 = (bf16[256,512]{1,0:T(8,128)(2,1)}, f32[256,128]{1,0:T(8,128)}, f32[256,128]{1,0:T(8,128)}, f32[256,16]{1,0:T(8,128)}, f32[8,1,256]{2,1,0:T(1,128)}) custom-call(bf16[256,1024]{1,0:T(8,128)(2,1)} %inputs_ref.5, bf16[256,1024]{1,0:T(8,128)(2,1)} %get-tuple-element.99.grads_ref, bf16[256,128]{1,0:T(8,128)(2,1)} %writes_ref.7, ...), custom_call_target="tpu_custom_call" | custom-call | flops 268435456 | bytes 1048576 | tf_op jit(solution)/shard_map/pallas_call | solution.py:33
  220.5 5.0 %shard_map.176 = (bf16[256,512]{1,0:T(8,128)(2,1)}, f32[256,128]{1,0:T(8,128)}, f32[256,128]{1,0:T(8,128)}, f32[256,16]{1,0:T(8,128)}, f32[8,1,256]{2,1,0:T(1,128)}) custom-call(bf16[256,1024]{1,0:T(8,128)(2,1)} %inputs_ref.5, bf16[256,1024]{1,0:T(8,128)(2,1)} %get-tuple-element.99.grads_ref, bf16[256,128]{1,0:T(8,128)(2,1)} %writes_ref.7, ...), custom_call_target="tpu_custom_call" | custom-call | flops 268435456 | bytes 1048576 | tf_op jit(solution)/shard_map/pallas_call | solution.py:33
  225.5 3.6 %shard_map.178 = (bf16[256,1024]{1,0:T(8,128)(2,1)}, f32[256,128]{1,0:T(8,128)}, f32[256,128]{1,0:T(8,128)}, f32[16,256]{1,0:T(8,128)}) custom-call(bf16[256,128]{1,0:T(8,128)(2,1)} %writes_ref.7, bf16[128,1024]{1,0:T(8,128)(2,1)} %bitcast.5.state_ref, bf16[128,1024]{1,0:T(8,128)(2,1)S(1)} %bitcast.31, f32[16,1,256]{2,1,0:T(1,128)} %get-tuple-element.165.cumt_ref, ...), custom_call_target="tpu_custom_call" | custom-call | tf_op jit(solution)/shard_map/pallas_call | solution.py:33
  (131 shorter events, 29.8 us)
Async XLA Ops:
  2.7 39.0 %collective-permute-start.1 = (bf16[272,1024]{1,0:T(8,128)(2,1)}, bf16[272,1024]{1,0:T(8,128)(2,1)}, u32[]{:S(2)}, u32[]{:S(2)}) collective-permute-start(bf16[272,1024]{1,0:T(8,128)(2,1)} %get-tuple-element.103.message_ref), channel_id=1, source_target_pairs={{0,16},{8,24},{16,0},{24,8},{1,17},{9,25},{17,1},{25,9},{2,18},{10... | collective-permute-start | bytes 1671176 | tf_op jit(solution)/shard_map/ppermute | solution.py:394
  5.8 47.1 %collective-permute-start.4 = (bf16[256,1024]{1,0:T(8,128)(2,1)}, bf16[256,1024]{1,0:T(8,128)(2,1)}, u32[]{:S(2)}, u32[]{:S(2)}) collective-permute-start(bf16[256,1024]{1,0:T(8,128)(2,1)} %out_grad_ref.1), channel_id=1, source_target_pairs={{0,16},{8,24},{16,0},{24,8},{1,17},{9,25},{17,1},{25,9},{2,18},{10... | collective-permute-start | bytes 1572872 | tf_op jit(solution)/shard_map/ppermute | solution.py:394
  5.9 51.3 %collective-permute-start = (bf16[272,1024]{1,0:T(8,128)(2,1)}, bf16[272,1024]{1,0:T(8,128)(2,1)S(1)}, u32[]{:S(2)}, u32[]{:S(2)}) collective-permute-start(bf16[272,1024]{1,0:T(8,128)(2,1)} %get-tuple-element.103.message_ref), channel_id=1, source_target_pairs={{0,8},{8,0},{16,24},{24,16},{1,9},{9,1},{17,25},{25,17},{2,10},{10... | collective-permute-start | bytes 1671176 | tf_op jit(solution)/shard_map/ppermute | solution.py:394
  11.4 44.7 %collective-permute-start.13 = (bf16[256,1024]{1,0:T(8,128)(2,1)}, bf16[256,1024]{1,0:T(8,128)(2,1)S(1)}, u32[]{:S(2)}, u32[]{:S(2)}) collective-permute-start(bf16[256,1024]{1,0:T(8,128)(2,1)} %out_grad_ref.1), channel_id=1, source_target_pairs={{0,8},{8,0},{16,24},{24,16},{1,9},{9,1},{17,25},{25,17},{2,10},{10... | collective-permute-start | bytes 1572872 | tf_op jit(solution)/shard_map/ppermute | solution.py:394
  12.6 5.0 %collective-permute-start.28 = (bf16[64,1024]{1,0:T(8,128)(2,1)}, bf16[64,1024]{1,0:T(8,128)(2,1)S(1)}, u32[]{:S(2)}, u32[]{:S(2)}) collective-permute-start(bf16[64,1024]{1,0:T(8,128)(2,1)} %get-tuple-element.136), channel_id=1, source_target_pairs={{0,2},{1,3},{2,0},{3,1},{4,6},{5,7},{6,4},{7,5},{8,10},{9,11},{10,... | collective-permute-start | bytes 393224 | tf_op jit(solution)/shard_map/ppermute | solution.py:398
  17.6 25.3 %collective-permute-start.29 = (bf16[64,1024]{1,0:T(8,128)(2,1)}, bf16[64,1024]{1,0:T(8,128)(2,1)S(1)}, u32[]{:S(2)}, u32[]{:S(2)}) collective-permute-start(bf16[64,1024]{1,0:T(8,128)(2,1)} %get-tuple-element.137), channel_id=1, source_target_pairs={{0,3},{1,2},{2,1},{3,0},{4,7},{5,6},{6,5},{7,4},{8,11},{9,10},{10,... | collective-permute-start | bytes 393224 | tf_op jit(solution)/shard_map/ppermute | solution.py:398
  41.7 48.1 %collective-permute-start.3 = (bf16[272,1024]{1,0:T(8,128)(2,1)}, bf16[272,1024]{1,0:T(8,128)(2,1)S(1)}, u32[]{:S(2)}, u32[]{:S(2)}) collective-permute-start(bf16[272,1024]{1,0:T(8,128)(2,1)} %collective-permute-done.1.refs_1_), channel_id=1, source_target_pairs={{0,8},{8,0},{16,24},{24,16},{1,9},{9,1},{17,25},{25,17},{2,10},{10... | collective-permute-start | bytes 1671176 | tf_op jit(solution)/shard_map/ppermute | solution.py:394
  42.9 11.2 %collective-permute-start.30 = (bf16[64,1024]{1,0:T(8,128)(2,1)}, bf16[64,1024]{1,0:T(8,128)(2,1)S(1)}, u32[]{:S(2)}, u32[]{:S(2)}) collective-permute-start(bf16[64,1024]{1,0:T(8,128)(2,1)} %get-tuple-element.138), channel_id=1, source_target_pairs={{0,4},{1,5},{2,6},{3,7},{4,0},{5,1},{6,2},{7,3},{8,12},{9,13},{10,... | collective-permute-start | bytes 393224 | tf_op jit(solution)/shard_map/ppermute | solution.py:398
  52.9 35.7 %collective-permute-start.5 = (bf16[256,1024]{1,0:T(8,128)(2,1)}, bf16[256,1024]{1,0:T(8,128)(2,1)}, u32[]{:S(2)}, u32[]{:S(2)}) collective-permute-start(bf16[256,1024]{1,0:T(8,128)(2,1)} %collective-permute-done.4.refs_1_), channel_id=1, source_target_pairs={{0,8},{8,0},{16,24},{24,16},{1,9},{9,1},{17,25},{25,17},{2,10},{10... | collective-permute-start | bytes 1572872 | tf_op jit(solution)/shard_map/ppermute | solution.py:394
  54.1 16.6 %collective-permute-start.31 = (bf16[64,1024]{1,0:T(8,128)(2,1)}, bf16[64,1024]{1,0:T(8,128)(2,1)S(1)}, u32[]{:S(2)}, u32[]{:S(2)}) collective-permute-start(bf16[64,1024]{1,0:T(8,128)(2,1)} %get-tuple-element.139), channel_id=1, source_target_pairs={{0,5},{1,4},{2,7},{3,6},{4,1},{5,0},{6,3},{7,2},{8,13},{9,12},{10,... | collective-permute-start | bytes 393224 | tf_op jit(solution)/shard_map/ppermute | solution.py:398
  56.0 15.5 %collective-permute-start.32 = (bf16[64,1024]{1,0:T(8,128)(2,1)}, bf16[64,1024]{1,0:T(8,128)(2,1)S(1)}, u32[]{:S(2)}, u32[]{:S(2)}) collective-permute-start(bf16[64,1024]{1,0:T(8,128)(2,1)} %get-tuple-element.140), channel_id=1, source_target_pairs={{0,6},{1,7},{2,4},{3,5},{4,2},{5,3},{6,0},{7,1},{8,14},{9,15},{10,... | collective-permute-start | bytes 393224 | tf_op jit(solution)/shard_map/ppermute | solution.py:398
  57.2 16.6 %collective-permute-start.33 = (bf16[64,1024]{1,0:T(8,128)(2,1)}, bf16[64,1024]{1,0:T(8,128)(2,1)S(1)}, u32[]{:S(2)}, u32[]{:S(2)}) collective-permute-start(bf16[64,1024]{1,0:T(8,128)(2,1)} %get-tuple-element.141), channel_id=1, source_target_pairs={{0,7},{1,6},{2,5},{3,4},{4,3},{5,2},{6,1},{7,0},{8,15},{9,14},{10,... | collective-permute-start | bytes 393224 | tf_op jit(solution)/shard_map/ppermute | solution.py:398
  61.6 28.7 %all-to-all-start = ((bf16[8,24,1024]{2,1,0:T(8,128)(2,1)}), bf16[8,24,1024]{2,1,0:T(8,128)(2,1)S(1)}, u32[]{:S(2)}, u32[]{:S(2)}) async-start(bf16[8,24,1024]{2,1,0:T(8,128)(2,1)} %get-tuple-element.105), calls=%async_computation | async-start | bytes 786432 | tf_op jit(solution)/shard_map/all_to_all | solution.py:846
  71.4 3.5 %collective-permute-start.14 = (bf16[64,1024]{1,0:T(8,128)(2,1)}, bf16[64,1024]{1,0:T(8,128)(2,1)S(1)}, u32[]{:S(2)}, u32[]{:S(2)}) collective-permute-start(bf16[64,1024]{1,0:T(8,128)(2,1)} %get-tuple-element.117), channel_id=1, source_target_pairs={{0,1},{1,0},{2,3},{3,2},{4,5},{5,4},{6,7},{7,6},{8,9},{9,8},{10,11... | collective-permute-start | bytes 393224 | tf_op jit(solution)/shard_map/ppermute | solution.py:398
  72.2 5.2 %collective-permute-start.15 = (bf16[64,1024]{1,0:T(8,128)(2,1)}, bf16[64,1024]{1,0:T(8,128)(2,1)S(1)}, u32[]{:S(2)}, u32[]{:S(2)}) collective-permute-start(bf16[64,1024]{1,0:T(8,128)(2,1)} %get-tuple-element.118), channel_id=1, source_target_pairs={{0,2},{1,3},{2,0},{3,1},{4,6},{5,7},{6,4},{7,5},{8,10},{9,11},{10,... | collective-permute-start | bytes 393224 | tf_op jit(solution)/shard_map/ppermute | solution.py:398
  74.5 6.1 %collective-permute-start.16 = (bf16[64,1024]{1,0:T(8,128)(2,1)}, bf16[64,1024]{1,0:T(8,128)(2,1)S(1)}, u32[]{:S(2)}, u32[]{:S(2)}) collective-permute-start(bf16[64,1024]{1,0:T(8,128)(2,1)} %get-tuple-element.119), channel_id=1, source_target_pairs={{0,3},{1,2},{2,1},{3,0},{4,7},{5,6},{6,5},{7,4},{8,11},{9,10},{10,... | collective-permute-start | bytes 393224 | tf_op jit(solution)/shard_map/ppermute | solution.py:398
  74.9 7.2 %collective-permute-start.17 = (bf16[64,1024]{1,0:T(8,128)(2,1)}, bf16[64,1024]{1,0:T(8,128)(2,1)S(1)}, u32[]{:S(2)}, u32[]{:S(2)}) collective-permute-start(bf16[64,1024]{1,0:T(8,128)(2,1)} %get-tuple-element.120), channel_id=1, source_target_pairs={{0,4},{1,5},{2,6},{3,7},{4,0},{5,1},{6,2},{7,3},{8,12},{9,13},{10,... | collective-permute-start | bytes 393224 | tf_op jit(solution)/shard_map/ppermute | solution.py:398
  77.4 5.8 %collective-permute-start.2 = (bf16[64,1024]{1,0:T(8,128)(2,1)}, bf16[64,1024]{1,0:T(8,128)(2,1)S(1)}, u32[]{:S(2)}, u32[]{:S(2)}) collective-permute-start(bf16[64,1024]{1,0:T(8,128)(2,1)} %get-tuple-element.104), channel_id=1, source_target_pairs={{0,1},{1,0},{2,3},{3,2},{4,5},{5,4},{6,7},{7,6},{8,9},{9,8},{10,11... | collective-permute-start | bytes 393224 | tf_op jit(solution)/shard_map/ppermute | solution.py:398
  80.6 5.0 %collective-permute-start.21 = (bf16[64,1024]{1,0:T(8,128)(2,1)}, bf16[64,1024]{1,0:T(8,128)(2,1)S(1)}, u32[]{:S(2)}, u32[]{:S(2)}) collective-permute-start(bf16[64,1024]{1,0:T(8,128)(2,1)} %get-tuple-element.126), channel_id=1, source_target_pairs={{0,2},{1,3},{2,0},{3,1},{4,6},{5,7},{6,4},{7,5},{8,10},{9,11},{10,... | collective-permute-start | bytes 393224 | tf_op jit(solution)/shard_map/ppermute | solution.py:398
  82.7 15.9 %collective-permute-start.22 = (bf16[64,1024]{1,0:T(8,128)(2,1)}, bf16[64,1024]{1,0:T(8,128)(2,1)}, u32[]{:S(2)}, u32[]{:S(2)}) collective-permute-start(bf16[64,1024]{1,0:T(8,128)(2,1)} %get-tuple-element.127), channel_id=1, source_target_pairs={{0,3},{1,2},{2,1},{3,0},{4,7},{5,6},{6,5},{7,4},{8,11},{9,10},{10,... | collective-permute-start | bytes 393224 | tf_op jit(solution)/shard_map/ppermute | solution.py:398
  83.2 17.1 %collective-permute-start.23 = (bf16[64,1024]{1,0:T(8,128)(2,1)}, bf16[64,1024]{1,0:T(8,128)(2,1)}, u32[]{:S(2)}, u32[]{:S(2)}) collective-permute-start(bf16[64,1024]{1,0:T(8,128)(2,1)} %get-tuple-element.128), channel_id=1, source_target_pairs={{0,4},{1,5},{2,6},{3,7},{4,0},{5,1},{6,2},{7,3},{8,12},{9,13},{10,... | collective-permute-start | bytes 393224 | tf_op jit(solution)/shard_map/ppermute | solution.py:398
  85.6 15.8 %collective-permute-start.24 = (bf16[64,1024]{1,0:T(8,128)(2,1)}, bf16[64,1024]{1,0:T(8,128)(2,1)}, u32[]{:S(2)}, u32[]{:S(2)}) collective-permute-start(bf16[64,1024]{1,0:T(8,128)(2,1)} %get-tuple-element.129), channel_id=1, source_target_pairs={{0,5},{1,4},{2,7},{3,6},{4,1},{5,0},{6,3},{7,2},{8,13},{9,12},{10,... | collective-permute-start | bytes 393224 | tf_op jit(solution)/shard_map/ppermute | solution.py:398
  88.7 14.3 %collective-permute-start.25 = (bf16[64,1024]{1,0:T(8,128)(2,1)}, bf16[64,1024]{1,0:T(8,128)(2,1)}, u32[]{:S(2)}, u32[]{:S(2)}) collective-permute-start(bf16[64,1024]{1,0:T(8,128)(2,1)} %get-tuple-element.130), channel_id=1, source_target_pairs={{0,6},{1,7},{2,4},{3,5},{4,2},{5,3},{6,0},{7,1},{8,14},{9,15},{10,... | collective-permute-start | bytes 393224 | tf_op jit(solution)/shard_map/ppermute | solution.py:398
  89.8 13.2 %collective-permute-start.26 = (bf16[64,1024]{1,0:T(8,128)(2,1)}, bf16[64,1024]{1,0:T(8,128)(2,1)}, u32[]{:S(2)}, u32[]{:S(2)}) collective-permute-start(bf16[64,1024]{1,0:T(8,128)(2,1)} %get-tuple-element.131), channel_id=1, source_target_pairs={{0,7},{1,6},{2,5},{3,4},{4,3},{5,2},{6,1},{7,0},{8,15},{9,14},{10,... | collective-permute-start | bytes 393224 | tf_op jit(solution)/shard_map/ppermute | solution.py:398
  91.0 19.8 %all-to-all-start.1 = ((bf16[8,16,1024]{2,1,0:T(8,128)(2,1)}), bf16[8,16,1024]{2,1,0:T(8,128)(2,1)}, u32[]{:S(2)}, u32[]{:S(2)}) async-start(bf16[8,16,1024]{2,1,0:T(8,128)(2,1)} %shard_map.164), calls=%async_computation.1 | async-start | bytes 524288 | tf_op jit(solution)/shard_map/all_to_all | solution.py:846
  98.6 16.8 %collective-permute-start.18 = (bf16[64,1024]{1,0:T(8,128)(2,1)}, bf16[64,1024]{1,0:T(8,128)(2,1)S(1)}, u32[]{:S(2)}, u32[]{:S(2)}) collective-permute-start(bf16[64,1024]{1,0:T(8,128)(2,1)} %get-tuple-element.121), channel_id=1, source_target_pairs={{0,5},{1,4},{2,7},{3,6},{4,1},{5,0},{6,3},{7,2},{8,13},{9,12},{10,... | collective-permute-start | bytes 393224 | tf_op jit(solution)/shard_map/ppermute | solution.py:398
  100.3 16.1 %collective-permute-start.19 = (bf16[64,1024]{1,0:T(8,128)(2,1)}, bf16[64,1024]{1,0:T(8,128)(2,1)S(1)}, u32[]{:S(2)}, u32[]{:S(2)}) collective-permute-start(bf16[64,1024]{1,0:T(8,128)(2,1)} %get-tuple-element.122), channel_id=1, source_target_pairs={{0,6},{1,7},{2,4},{3,5},{4,2},{5,3},{6,0},{7,1},{8,14},{9,15},{10,... | collective-permute-start | bytes 393224 | tf_op jit(solution)/shard_map/ppermute | solution.py:398
  101.4 15.0 %collective-permute-start.20 = (bf16[64,1024]{1,0:T(8,128)(2,1)}, bf16[64,1024]{1,0:T(8,128)(2,1)}, u32[]{:S(2)}, u32[]{:S(2)}) collective-permute-start(bf16[64,1024]{1,0:T(8,128)(2,1)} %get-tuple-element.123), channel_id=1, source_target_pairs={{0,7},{1,6},{2,5},{3,4},{4,3},{5,2},{6,1},{7,0},{8,15},{9,14},{10,... | collective-permute-start | bytes 393224 | tf_op jit(solution)/shard_map/ppermute | solution.py:398
  102.9 15.1 %collective-permute-start.6 = (bf16[64,1024]{1,0:T(8,128)(2,1)}, bf16[64,1024]{1,0:T(8,128)(2,1)}, u32[]{:S(2)}, u32[]{:S(2)}) collective-permute-start(bf16[64,1024]{1,0:T(8,128)(2,1)} %get-tuple-element.108), channel_id=1, source_target_pairs={{0,1},{1,0},{2,3},{3,2},{4,5},{5,4},{6,7},{7,6},{8,9},{9,8},{10,11... | collective-permute-start | bytes 393224 | tf_op jit(solution)/shard_map/ppermute | solution.py:398
  103.0 16.0 %collective-permute-start.7 = (bf16[64,1024]{1,0:T(8,128)(2,1)}, bf16[64,1024]{1,0:T(8,128)(2,1)}, u32[]{:S(2)}, u32[]{:S(2)}) collective-permute-start(bf16[64,1024]{1,0:T(8,128)(2,1)} %get-tuple-element.109), channel_id=1, source_target_pairs={{0,2},{1,3},{2,0},{3,1},{4,6},{5,7},{6,4},{7,5},{8,10},{9,11},{10,... | collective-permute-start | bytes 393224 | tf_op jit(solution)/shard_map/ppermute | solution.py:398
  115.5 12.2 %collective-permute-start.8 = (bf16[64,1024]{1,0:T(8,128)(2,1)S(1)}, bf16[64,1024]{1,0:T(8,128)(2,1)S(1)}, u32[]{:S(2)}, u32[]{:S(2)}) collective-permute-start(bf16[64,1024]{1,0:T(8,128)(2,1)S(1)} %copy-done.25), channel_id=1, source_target_pairs={{0,3},{1,2},{2,1},{3,0},{4,7},{5,6},{6,5},{7,4},{8,11},{9,10},{10,... | collective-permute-start | bytes 393224 | tf_op jit(solution)/shard_map/ppermute | solution.py:398
  116.4 11.3 %collective-permute-start.9 = (bf16[64,1024]{1,0:T(8,128)(2,1)S(1)}, bf16[64,1024]{1,0:T(8,128)(2,1)S(1)}, u32[]{:S(2)}, u32[]{:S(2)}) collective-permute-start(bf16[64,1024]{1,0:T(8,128)(2,1)S(1)} %copy-done.24), channel_id=1, source_target_pairs={{0,4},{1,5},{2,6},{3,7},{4,0},{5,1},{6,2},{7,3},{8,12},{9,13},{10,... | collective-permute-start | bytes 393224 | tf_op jit(solution)/shard_map/ppermute | solution.py:398
  116.5 13.6 %collective-permute-start.10 = (bf16[64,1024]{1,0:T(8,128)(2,1)S(1)}, bf16[64,1024]{1,0:T(8,128)(2,1)S(1)}, u32[]{:S(2)}, u32[]{:S(2)}) collective-permute-start(bf16[64,1024]{1,0:T(8,128)(2,1)S(1)} %copy-done.23), channel_id=1, source_target_pairs={{0,5},{1,4},{2,7},{3,6},{4,1},{5,0},{6,3},{7,2},{8,13},{9,12},{10,... | collective-permute-start | bytes 393224 | tf_op jit(solution)/shard_map/ppermute | solution.py:398
  118.0 12.1 %collective-permute-start.11 = (bf16[64,1024]{1,0:T(8,128)(2,1)S(1)}, bf16[64,1024]{1,0:T(8,128)(2,1)S(1)}, u32[]{:S(2)}, u32[]{:S(2)}) collective-permute-start(bf16[64,1024]{1,0:T(8,128)(2,1)S(1)} %copy-done.22), channel_id=1, source_target_pairs={{0,6},{1,7},{2,4},{3,5},{4,2},{5,3},{6,0},{7,1},{8,14},{9,15},{10,... | collective-permute-start | bytes 393224 | tf_op jit(solution)/shard_map/ppermute | solution.py:398
  119.1 11.0 %collective-permute-start.12 = (bf16[64,1024]{1,0:T(8,128)(2,1)S(1)}, bf16[64,1024]{1,0:T(8,128)(2,1)S(1)}, u32[]{:S(2)}, u32[]{:S(2)}) collective-permute-start(bf16[64,1024]{1,0:T(8,128)(2,1)S(1)} %copy-done.21), channel_id=1, source_target_pairs={{0,7},{1,6},{2,5},{3,4},{4,3},{5,2},{6,1},{7,0},{8,15},{9,14},{10,... | collective-permute-start | bytes 393224 | tf_op jit(solution)/shard_map/ppermute | solution.py:398
  134.7 54.6 %all-to-all-start.2 = ((bf16[32,32,1024]{2,1,0:T(8,128)(2,1)}), bf16[32,32,1024]{2,1,0:T(8,128)(2,1)S(1)}, u32[]{:S(2)}, u32[]{:S(2)}) async-start(bf16[32,32,1024]{2,1,0:T(8,128)(2,1)} %bitcast.35), calls=%async_computation.2 | async-start | bytes 4194304 | tf_op jit(solution)/shard_map/all_to_all | solution.py:846
  140.8 48.5 %collective-permute-start.35 = (f32[8,256]{1,0:T(8,128)S(1)}, f32[8,256]{1,0:T(8,128)S(1)}, u32[]{:S(2)}, u32[]{:S(2)}) collective-permute-start(f32[8,256]{1,0:T(8,128)S(1)} %get-tuple-element.198), channel_id=1, source_target_pairs={{0,16},{8,24},{16,0},{24,8},{1,17},{9,25},{17,1},{25,9},{2,18},{10... | collective-permute-start | bytes 24584 | tf_op jit(solution)/shard_map/ppermute | solution.py:394
  143.1 46.2 %collective-permute-start.34 = (f32[8,256]{1,0:T(8,128)S(1)}, f32[8,256]{1,0:T(8,128)S(1)}, u32[]{:S(2)}, u32[]{:S(2)}) collective-permute-start(f32[8,256]{1,0:T(8,128)S(1)} %get-tuple-element.199), channel_id=1, source_target_pairs={{0,8},{8,0},{16,24},{24,16},{1,9},{9,1},{17,25},{25,17},{2,10},{10... | collective-permute-start | bytes 24584 | tf_op jit(solution)/shard_map/ppermute | solution.py:394
  144.3 45.0 %collective-permute-start.36 = (f32[8,256]{1,0:T(8,128)S(1)}, f32[8,256]{1,0:T(8,128)S(1)}, u32[]{:S(2)}, u32[]{:S(2)}) collective-permute-start(f32[8,256]{1,0:T(8,128)S(1)} %bitcast.40), channel_id=1, source_target_pairs={{0,24},{8,16},{16,8},{24,0},{1,25},{9,17},{17,9},{25,1},{2,26},{10... | collective-permute-start | bytes 24584 | tf_op jit(solution)/shard_map/ppermute | solution.py:394
  192.8 17.1 %all-to-all-start.3 = ((bf16[8,16,1024]{2,1,0:T(8,128)(2,1)}), bf16[8,16,1024]{2,1,0:T(8,128)(2,1)S(1)}, u32[]{:S(2)}, u32[]{:S(2)}) async-start(bf16[8,16,1024]{2,1,0:T(8,128)(2,1)} %bitcast.36), calls=%async_computation.3 | async-start | bytes 524288 | tf_op jit(solution)/shard_map/all_to_all | solution.py:846
  198.3 3.8 %collective-permute-start.37 = (f32[8,128]{1,0:T(8,128)S(1)}, f32[8,128]{1,0:T(8,128)S(1)}, u32[]{:S(2)}, u32[]{:S(2)}) collective-permute-start(f32[8,128]{1,0:T(8,128)S(1)} %get-tuple-element.189), channel_id=1, source_target_pairs={{0,1},{1,0},{2,3},{3,2},{4,5},{5,4},{6,7},{7,6},{8,9},{9,8},{10,11... | collective-permute-start | bytes 12296 | tf_op jit(solution)/shard_map/ppermute | solution.py:398
  198.4 6.1 %collective-permute-start.38 = (f32[8,128]{1,0:T(8,128)S(1)}, f32[8,128]{1,0:T(8,128)S(1)}, u32[]{:S(2)}, u32[]{:S(2)}) collective-permute-start(f32[8,128]{1,0:T(8,128)S(1)} %get-tuple-element.190), channel_id=1, source_target_pairs={{0,2},{1,3},{2,0},{3,1},{4,6},{5,7},{6,4},{7,5},{8,10},{9,11},{10,... | collective-permute-start | bytes 12296 | tf_op jit(solution)/shard_map/ppermute | solution.py:398
  200.1 4.8 %collective-permute-start.39 = (f32[8,128]{1,0:T(8,128)S(1)}, f32[8,128]{1,0:T(8,128)S(1)}, u32[]{:S(2)}, u32[]{:S(2)}) collective-permute-start(f32[8,128]{1,0:T(8,128)S(1)} %get-tuple-element.191), channel_id=1, source_target_pairs={{0,3},{1,2},{2,1},{3,0},{4,7},{5,6},{6,5},{7,4},{8,11},{9,10},{10,... | collective-permute-start | bytes 12296 | tf_op jit(solution)/shard_map/ppermute | solution.py:398
  200.5 4.4 %collective-permute-start.40 = (f32[8,128]{1,0:T(8,128)S(1)}, f32[8,128]{1,0:T(8,128)S(1)}, u32[]{:S(2)}, u32[]{:S(2)}) collective-permute-start(f32[8,128]{1,0:T(8,128)S(1)} %get-tuple-element.192), channel_id=1, source_target_pairs={{0,4},{1,5},{2,6},{3,7},{4,0},{5,1},{6,2},{7,3},{8,12},{9,13},{10,... | collective-permute-start | bytes 12296 | tf_op jit(solution)/shard_map/ppermute | solution.py:398
  201.9 3.1 %collective-permute-start.41 = (f32[8,128]{1,0:T(8,128)S(1)}, f32[8,128]{1,0:T(8,128)S(1)}, u32[]{:S(2)}, u32[]{:S(2)}) collective-permute-start(f32[8,128]{1,0:T(8,128)S(1)} %get-tuple-element.193), channel_id=1, source_target_pairs={{0,5},{1,4},{2,7},{3,6},{4,1},{5,0},{6,3},{7,2},{8,13},{9,12},{10,... | collective-permute-start | bytes 12296 | tf_op jit(solution)/shard_map/ppermute | solution.py:398
  202.2 3.4 %collective-permute-start.42 = (f32[8,128]{1,0:T(8,128)S(1)}, f32[8,128]{1,0:T(8,128)S(1)}, u32[]{:S(2)}, u32[]{:S(2)}) collective-permute-start(f32[8,128]{1,0:T(8,128)S(1)} %get-tuple-element.194), channel_id=1, source_target_pairs={{0,6},{1,7},{2,4},{3,5},{4,2},{5,3},{6,0},{7,1},{8,14},{9,15},{10,... | collective-permute-start | bytes 12296 | tf_op jit(solution)/shard_map/ppermute | solution.py:398
  204.5 3.9 %collective-permute-start.43 = (f32[8,128]{1,0:T(8,128)S(1)}, f32[8,128]{1,0:T(8,128)S(1)}, u32[]{:S(2)}, u32[]{:S(2)}) collective-permute-start(f32[8,128]{1,0:T(8,128)S(1)} %get-tuple-element.195), channel_id=1, source_target_pairs={{0,7},{1,6},{2,5},{3,4},{4,3},{5,2},{6,1},{7,0},{8,15},{9,14},{10,... | collective-permute-start | bytes 12296 | tf_op jit(solution)/shard_map/ppermute | solution.py:398
  210.7 14.8 %all-to-all-start.4 = ((bf16[8,16,1024]{2,1,0:T(8,128)(2,1)}), bf16[8,16,1024]{2,1,0:T(8,128)(2,1)S(1)}, u32[]{:S(2)}, u32[]{:S(2)}) async-start(bf16[8,16,1024]{2,1,0:T(8,128)(2,1)} %shard_map.175), calls=%async_computation.4 | async-start | bytes 524288 | tf_op jit(solution)/shard_map/all_to_all | solution.py:846
  (30 other events, 322.0 us)

commit v4 on v3

--- a/solution.py
+++ b/solution.py
@@ -196,16 +196,14 @@
     named = ids.astype(F32)
     plane = jnp.floor((named + 0.5) * (1.0 / shard_count))
     shard = named - plane * shard_count
-    facts = jnp.concatenate(
-        [plane, shard, ranks, gates_ref[...], jnp.zeros((8, tokens), F32)], axis=0
-    )
+    facts = jnp.concatenate([plane, shard, ranks, gates_ref[...]], axis=0)
     message_ref[tokens:, 0:tokens] = facts.astype(BF16)
     if width > tokens:
-        message_ref[tokens:, tokens:] = jnp.zeros((16, width - tokens), BF16)
+        message_ref[tokens:, tokens:] = jnp.zeros((8, width - tokens), BF16)
 
 
 def named_rows(me_ref, message, slots, cap):
-    tokens = message.shape[0] - 16
+    tokens = message.shape[0] - 8
     facts = message[tokens:, 0:tokens].astype(F32)
     places = (facts[2:4, :].astype(jnp.int32) ^ me_ref[1]) * cap
     places = places + facts[4:6, :].astype(jnp.int32)
@@ -493,7 +491,7 @@
 
     message, targets = streamed(
         functools.partial(message_kernel, planes, shard_count, cap),
-        (far_shape((tokens + 16, width), BF16), far_shape((2, tokens), jnp.int32)),
+        (far_shape((tokens + 8, width), BF16), far_shape((2, tokens), jnp.int32)),
         resid,
         ids,
         gates,

time: 231 us -> 230 us (level)
    unnamed x58 -> x70, local copies, waits for them, and re-layouts: 5.52 us -> 6.2 us
  transfers between devices with their start and end apart: 49 -> 49, of which waited for: 11 -> 11; matrix products, arithmetic and copies ran while one was open for 1% -> 1% of each run, Pallas kernels for 24% -> 23%
where the time goes in v4:
time: 230 us; the launch traced here: 228 us
  waiting for transfers between devices  77.3 us (34%)
  starting transfers between devices  74.9 us (33%)
  Pallas kernels  67.2 us (29%)
  local copies, waits for them, and re-layouts  6.21 us (3%)
    ppermute x9, waiting for transfers between devices, across(): return lax.ppermute(x, 'grp', [(i, i ^ bit) for i in range(planes)])  62.3 us
    pallas_call x16, Pallas kernels, call(): pl.pallas_call(kernel, out_shape=outs, in_specs=in_specs if in_specs is n...  48.4 us
    ppermute x35, starting transfers between devices, spread_out(): lax.ppermute(part, 'seq', [(i, i ^ x) for i in range(shard_count)])  40.9 us
    all_to_all x5, starting transfers between devices, swap(): return lax.all_to_all(x, axes, split_axis=0, concat_axis=0, tiled=True)  23.6 us
    pallas_call x4, Pallas kernels, grouped(): pl.pallas_call(functools.partial(kernel, len(parts)), out_shape=outs, gri...  18.8 us
    ppermute x35, waiting for transfers between devices, spread_out(): lax.ppermute(part, 'seq', [(i, i ^ x) for i in range(shard_count)])  15 us
    ppermute x9, starting transfers between devices, across(): return lax.ppermute(x, 'grp', [(i, i ^ bit) for i in range(planes)])  10.5 us
    unnamed x70, local copies, waits for them, and re-layouts  6.2 us
  transfers between devices with their start and end apart: 49, of which 11 were waited for; matrix products, arithmetic and copies ran while one was open for 1% of the time, Pallas kernels for 23%

profile of v4, /device:TPU:1, one launch (start us, length us, event | category | flops | bytes accessed | tf_op | source)
XLA Modules:
  0.0 227.9 jit_solution(2819737589634055790)
XLA Ops:
  0.6 2.1 shard_map.161
  2.7 3.1 %collective-permute-start.1 = (bf16[264,1024]{1,0:T(8,128)(2,1)}, bf16[264,1024]{1,0:T(8,128)(2,1)}, u32[]{:S(2)}, u32[]{:S(2)}) collective-permute-start(bf16[264,1024]{1,0:T(8,128)(2,1)} %get-tuple-element.103.message_ref), channel_id=1, source_target_pairs={{0,16},{8,24},{16,0},{24,8},{1,17},{9,25},{17,1},{25,9},{2,18},{10... | collective-permute-start | bytes 1622024 | tf_op jit(solution)/shard_map/ppermute | solution.py:392
  5.9 1.3 collective-permute-start
  7.3 2.6 %shard_map.168 = (bf16[64,1024]{1,0:T(8,128)(2,1)}, bf16[64,1024]{1,0:T(8,128)(2,1)}, bf16[64,1024]{1,0:T(8,128)(2,1)}, bf16[64,1024]{1,0:T(8,128)(2,1)}, bf16[6...) custom-call(s32[2]{0:T(128)S(1)} %pad_add_fusion.me_ref, ...), custom_call_target="tpu_custom_call" | custom-call | tf_op jit(solution)/shard_map/pallas_call | solution.py:33
  9.8 1.5 collective-permute-start.27
  13.8 3.8 %collective-permute-done.28.refs_2_ = bf16[64,1024]{1,0:T(8,128)(2,1)S(1)} collective-permute-done((bf16[64,1024]{1,0:T(8,128)(2,1)}, bf16[64,1024]{1,0:T(8,128)(2,1)S(1)}, u32[]{:S(2)}, u32[]{:S(2)}) %collective-permute-start.28) | collective-permute-done | bytes 131104 | tf_op jit(solution)/shard_map/ppermute | solution.py:396
  17.5 2.2 collective-permute-start.29
  19.8 21.2 %collective-permute-done.1.refs_1_ = bf16[264,1024]{1,0:T(8,128)(2,1)} collective-permute-done((bf16[264,1024]{1,0:T(8,128)(2,1)}, bf16[264,1024]{1,0:T(8,128)(2,1)}, u32[]{:S(2)}, u32[]{:S(2)}) %collective-permute-start.1) | collective-permute-done | bytes 540704 | tf_op jit(solution)/shard_map/ppermute | solution.py:392
  43.4 8.8 %collective-permute-done.4.refs_1_ = bf16[256,1024]{1,0:T(8,128)(2,1)} collective-permute-done((bf16[256,1024]{1,0:T(8,128)(2,1)}, bf16[256,1024]{1,0:T(8,128)(2,1)}, u32[]{:S(2)}, u32[]{:S(2)}) %collective-permute-start.4) | collective-permute-done | bytes 524320 | tf_op jit(solution)/shard_map/ppermute | solution.py:392
  53.4 1.9 collective-permute-start.31
  57.7 3.2 %shard_map.163 = (f32[256,16]{1,0:T(8,128)}, f32[16,1,256]{2,1,0:T(1,128)}, bf16[256,1024]{1,0:T(8,128)(2,1)}, bf16[256,1024]{1,0:T(8,128)(2,1)}, bf16[256,1024]...) custom-call(bf16[256,1024]{1,0:T(8,128)(2,1)} %inputs_ref.5, bf16[256,128]{1,0:T(8,128)(2,1)} %writes_ref.7, f32[16,256]{1,0:T(8,128)} %bitcast.37), custom_call_target="tpu_custom_call" | custom-call | tf_op jit(solution)/shard_map/pallas_call | solution.py:33
  60.9 3.9 %all-to-all-start = ((bf16[8,24,1024]{2,1,0:T(8,128)(2,1)}), bf16[8,24,1024]{2,1,0:T(8,128)(2,1)S(1)}, u32[]{:S(2)}, u32[]{:S(2)}) async-start(bf16[8,24,1024]{2,1,0:T(8,128)(2,1)} %get-tuple-element.105), calls=%async_computation | async-start | bytes 786432 | tf_op jit(solution)/shard_map/all_to_all | solution.py:844
  64.8 2.6 %shard_map.162 = (bf16[64,1024]{1,0:T(8,128)(2,1)}, bf16[64,1024]{1,0:T(8,128)(2,1)}, bf16[64,1024]{1,0:T(8,128)(2,1)}, bf16[64,1024]{1,0:T(8,128)(2,1)}, bf16[6...) custom-call(s32[2]{0:T(128)S(1)} %pad_add_fusion.me_ref, ...), custom_call_target="tpu_custom_call" | custom-call | tf_op jit(solution)/shard_map/pallas_call | solution.py:33
  67.3 2.7 %shard_map.166 = (bf16[64,1024]{1,0:T(8,128)(2,1)}, bf16[64,1024]{1,0:T(8,128)(2,1)}, bf16[64,1024]{1,0:T(8,128)(2,1)}, bf16[64,1024]{1,0:T(8,128)(2,1)}, bf16[6...) custom-call(f32[2,8,256]{2,1,0:T(8,128)} %get-tuple-element.115.keys_ref, ...), custom_call_target="tpu_custom_call" | custom-call | tf_op jit(solution)/shard_map/pallas_call | solution.py:33
  70.2 1.6 collective-permute-start.15
  72.9 1.4 collective-permute-start.17
  76.1 1.8 collective-permute-start.2
  79.3 1.5 collective-permute-start.21
  81.6 1.5 collective-permute-start.23
  84.5 2.8 %collective-permute-start.24 = (bf16[64,1024]{1,0:T(8,128)(2,1)}, bf16[64,1024]{1,0:T(8,128)(2,1)}, u32[]{:S(2)}, u32[]{:S(2)}) collective-permute-start(bf16[64,1024]{1,0:T(8,128)(2,1)} %get-tuple-element.129), channel_id=1, source_target_pairs={{0,5},{1,4},{2,7},{3,6},{4,1},{5,0},{6,3},{7,2},{8,13},{9,12},{10,... | collective-permute-start | bytes 393224 | tf_op jit(solution)/shard_map/ppermute | solution.py:396
  89.7 5.2 %all-to-all-start.1 = ((bf16[8,16,1024]{2,1,0:T(8,128)(2,1)}), bf16[8,16,1024]{2,1,0:T(8,128)(2,1)}, u32[]{:S(2)}, u32[]{:S(2)}) async-start(bf16[8,16,1024]{2,1,0:T(8,128)(2,1)} %shard_map.164), calls=%async_computation.1 | async-start | bytes 524288 | tf_op jit(solution)/shard_map/all_to_all | solution.py:844
  95.5 1.9 shard_map.165
  97.5 1.7 collective-permute-start.18
  100.3 1.5 collective-permute-start.20
  103.1 1.6 copy-done.1
  104.7 4.9 %shard_map.169 = (bf16[256,1024]{1,0:T(8,128)(2,1)}, bf16[256,1024]{1,0:T(8,128)(2,1)}, bf16[256,1024]{1,0:T(8,128)(2,1)}, bf16[256,1024]{1,0:T(8,128)(2,1)}, bf...) custom-call(s32[2]{0:T(128)S(1)} %copy-done.15, bf16[64,1024]{1,0:T(8,128)(2,1)} %get-tuple-element.134.refs_0_, ...), custom_call_target="tpu_custom_call" | custom-call | flops 1610612736 | bytes 6291456 | tf_op jit(solution)/shard_map/pallas_call | solution.py:338
  109.7 4.5 %shard_map.167 = (bf16[512,1024]{1,0:T(8,128)(2,1)}, bf16[512,1024]{1,0:T(8,128)(2,1)}, f32[512,1024]{1,0:T(8,128)S(1)}) custom-call(s32[2]{0:T(128)S(1)} %copy-done.16, bf16[64,1024]{1,0:T(8,128)(2,1)} %get-tuple-element.124.refs_0_, bf16[64,1024]{1,0:T(8,128)(2,1)} %copy-done.32, bf16[64,1024]{1,0:T(8,128)(2,1)} %copy-done.33, ...), custom_call_target="tpu_custom_call" | custom-call | flops 1073741824 | bytes 6291456 | tf_op jit(solution)/shard_map/pallas_call | solution.py:338
  115.3 1.5 collective-permute-start.10
  117.8 1.8 collective-permute-start.12
  120.8 4.8 %shard_map.170 = (bf16[512,1024]{1,0:T(8,128)(2,1)}, bf16[512,1024]{1,0:T(8,128)(2,1)}, bf16[4,256,1024]{2,1,0:T(8,128)(2,1)}, f32[2,8,256]{2,1,0:T(8,128)}) custom-call(s32[2]{0:T(128)S(1)} %copy-done.16, bf16[64,1024]{1,0:T(8,128)(2,1)S(1)} %copy-done.4, bf16[64,1024]{1,0:T(8,128)(2,1)S(1)} %copy-done.6, ...), custom_call_target="tpu_custom_call", output_to_operand_aliasing={{2}: (13, {})} | custom-call | flops 2147483648 | bytes 6291456 | tf_op jit(solution)/shard_map/pallas_call | solution.py:338
  125.7 3.1 %collective-permute-done.10.refs_5_ = bf16[64,1024]{1,0:T(8,128)(2,1)S(1)} collective-permute-done((bf16[64,1024]{1,0:T(8,128)(2,1)S(1)}, bf16[64,1024]{1,0:T(8,128)(2,1)S(1)}, u32[]{:S(2)}, u32[]{:S(2)}) %collective-permute-start.10) | collective-permute-done | bytes 131104 | tf_op jit(solution)/shard_map/ppermute | solution.py:396
  128.8 4.6 %shard_map.171 = (bf16[256,1024]{1,0:T(8,128)(2,1)}, bf16[256,1024]{1,0:T(8,128)(2,1)}, bf16[256,1024]{1,0:T(8,128)(2,1)}, bf16[256,1024]{1,0:T(8,128)(2,1)}, bf...) custom-call(s32[2]{0:T(128)S(1)} %copy-done.16, ...), custom_call_target="tpu_custom_call", output_to_operand_aliasing={{4}: (11, {})} | custom-call | flops 1610612736 | bytes 6291456 | tf_op jit(solution)/shard_map/pallas_call | solution.py:338
  133.4 6.1 %all-to-all-start.2 = ((bf16[32,32,1024]{2,1,0:T(8,128)(2,1)}), bf16[32,32,1024]{2,1,0:T(8,128)(2,1)S(1)}, u32[]{:S(2)}, u32[]{:S(2)}) async-start(bf16[32,32,1024]{2,1,0:T(8,128)(2,1)} %bitcast.35), calls=%async_computation.2 | async-start | bytes 4194304 | tf_op jit(solution)/shard_map/all_to_all | solution.py:844
  139.6 2.3 %collective-permute-start.35 = (f32[8,256]{1,0:T(8,128)S(1)}, f32[8,256]{1,0:T(8,128)S(1)}, u32[]{:S(2)}, u32[]{:S(2)}) collective-permute-start(f32[8,256]{1,0:T(8,128)S(1)} %get-tuple-element.198), channel_id=1, source_target_pairs={{0,16},{8,24},{16,0},{24,8},{1,17},{9,25},{17,1},{25,9},{2,18},{10... | collective-permute-start | bytes 24584 | tf_op jit(solution)/shard_map/ppermute | solution.py:392
  143.2 6.3 %shard_map.172 = bf16[1024,1024]{1,0:T(8,128)(2,1)} custom-call(bf16[256,1024]{1,0:T(8,128)(2,1)} %get-tuple-element.148.refs_0_, bf16[256,1024]{1,0:T(8,128)(2,1)} %get-tuple-element.149.refs_1_, bf16[512,1024]{1,0:T(8,128)(2,1)} %get-tuple-element.132.refs_8_.refs_2_, bf16[512,1024]{1,0:T(8,128)(2,1)} %get-tuple-element.150.refs_3_, ...), custom_call_target="tpu_custom_call" | custom-call | flops 2147483648 | bytes 6291456 | tf_op jit(solution)/shard_map/pallas_call | solution.py:33
  149.5 6.3 %shard_map.173 = bf16[1024,1024]{1,0:T(8,128)(2,1)} custom-call(bf16[256,1024]{1,0:T(8,128)(2,1)} %get-tuple-element.153.refs_0_, bf16[256,1024]{1,0:T(8,128)(2,1)} %get-tuple-element.154.refs_1_, bf16[512,1024]{1,0:T(8,128)(2,1)} %get-tuple-element.155.refs_2_, bf16[512,1024]{1,0:T(8,128)(2,1)} %get-tuple-element.156.refs_3_, ...), custom_call_target="tpu_custom_call" | custom-call | flops 2147483648 | bytes 6291456 | tf_op jit(solution)/shard_map/pallas_call | solution.py:33
  155.8 32.3 %collective-permute-done.35.refs_2_ = f32[8,256]{1,0:T(8,128)S(1)} collective-permute-done((f32[8,256]{1,0:T(8,128)S(1)}, f32[8,256]{1,0:T(8,128)S(1)}, u32[]{:S(2)}, u32[]{:S(2)}) %collective-permute-start.35) | collective-permute-done | bytes 8224 | tf_op jit(solution)/shard_map/ppermute | solution.py:392
  188.1 3.4 %shard_map.174 = (bf16[256,1024]{1,0:T(8,128)(2,1)}, bf16[128,1024]{1,0:T(8,128)(2,1)}) custom-call(bf16[1024,1024]{1,0:T(8,128)(2,1)S(1)} %bitcast.23, s32[2,256]{1,0:T(2,128)} %get-tuple-element.162.targets_ref, bf16[256,1024]{1,0:T(8,128)(2,1)} %resid_ref.3, bf16[256,1024]{1,0:T(8,128)(2,1)} %out_grad_ref.1, bf16[256,128]{1,0:T(8,128)(2,1)} %reads_ref.5, ...), custom_call_target="tpu_custom_call" | custom-call | tf_op jit(solution)/shard_map/pallas_call | solution.py:33
  191.6 4.8 %all-to-all-start.3 = ((bf16[8,16,1024]{2,1,0:T(8,128)(2,1)}), bf16[8,16,1024]{2,1,0:T(8,128)(2,1)S(1)}, u32[]{:S(2)}, u32[]{:S(2)}) async-start(bf16[8,16,1024]{2,1,0:T(8,128)(2,1)} %bitcast.36), calls=%async_computation.3 | async-start | bytes 524288 | tf_op jit(solution)/shard_map/all_to_all | solution.py:844
  197.2 1.7 collective-permute-start.38
  199.3 1.4 collective-permute-start.40
  200.9 2.4 %collective-permute-start.42 = (f32[8,128]{1,0:T(8,128)S(1)}, f32[8,128]{1,0:T(8,128)S(1)}, u32[]{:S(2)}, u32[]{:S(2)}) collective-permute-start(f32[8,128]{1,0:T(8,128)S(1)} %get-tuple-element.194), channel_id=1, source_target_pairs={{0,6},{1,7},{2,4},{3,5},{4,2},{5,3},{6,0},{7,1},{8,14},{9,15},{10,... | collective-permute-start | bytes 12296 | tf_op jit(solution)/shard_map/ppermute | solution.py:396
  204.3 2.9 %collective-permute-done.43.refs_7_ = f32[8,128]{1,0:T(8,128)S(1)} collective-permute-done((f32[8,128]{1,0:T(8,128)S(1)}, f32[8,128]{1,0:T(8,128)S(1)}, u32[]{:S(2)}, u32[]{:S(2)}) %collective-permute-start.43) | collective-permute-done | bytes 4128 | tf_op jit(solution)/shard_map/ppermute | solution.py:396
  207.3 1.4 shard_map.180
  209.4 3.7 %all-to-all-start.4 = ((bf16[8,16,1024]{2,1,0:T(8,128)(2,1)}), bf16[8,16,1024]{2,1,0:T(8,128)(2,1)S(1)}, u32[]{:S(2)}, u32[]{:S(2)}) async-start(bf16[8,16,1024]{2,1,0:T(8,128)(2,1)} %shard_map.175), calls=%async_computation.4 | async-start | bytes 524288 | tf_op jit(solution)/shard_map/all_to_all | solution.py:844
  214.4 5.0 %shard_map.177 = (bf16[256,512]{1,0:T(8,128)(2,1)}, f32[256,128]{1,0:T(8,128)}, f32[256,128]{1,0:T(8,128)}, f32[256,16]{1,0:T(8,128)}, f32[8,1,256]{2,1,0:T(1,128)}) custom-call(bf16[256,1024]{1,0:T(8,128)(2,1)} %inputs_ref.5, bf16[256,1024]{1,0:T(8,128)(2,1)} %get-tuple-element.99.grads_ref, bf16[256,128]{1,0:T(8,128)(2,1)} %writes_ref.7, ...), custom_call_target="tpu_custom_call" | custom-call | flops 268435456 | bytes 1048576 | tf_op jit(solution)/shard_map/pallas_call | solution.py:33
  219.4 4.9 %shard_map.176 = (bf16[256,512]{1,0:T(8,128)(2,1)}, f32[256,128]{1,0:T(8,128)}, f32[256,128]{1,0:T(8,128)}, f32[256,16]{1,0:T(8,128)}, f32[8,1,256]{2,1,0:T(1,128)}) custom-call(bf16[256,1024]{1,0:T(8,128)(2,1)} %inputs_ref.5, bf16[256,1024]{1,0:T(8,128)(2,1)} %get-tuple-element.99.grads_ref, bf16[256,128]{1,0:T(8,128)(2,1)} %writes_ref.7, ...), custom_call_target="tpu_custom_call" | custom-call | flops 268435456 | bytes 1048576 | tf_op jit(solution)/shard_map/pallas_call | solution.py:33
  224.3 3.6 %shard_map.178 = (bf16[256,1024]{1,0:T(8,128)(2,1)}, f32[256,128]{1,0:T(8,128)}, f32[256,128]{1,0:T(8,128)}, f32[16,256]{1,0:T(8,128)}) custom-call(bf16[256,128]{1,0:T(8,128)(2,1)} %writes_ref.7, bf16[128,1024]{1,0:T(8,128)(2,1)} %bitcast.5.state_ref, bf16[128,1024]{1,0:T(8,128)(2,1)S(1)} %bitcast.31, f32[16,1,256]{2,1,0:T(1,128)} %get-tuple-element.165.cumt_ref, ...), custom_call_target="tpu_custom_call" | custom-call | tf_op jit(solution)/shard_map/pallas_call | solution.py:33
  (143 shorter events, 29.9 us)
Async XLA Ops:
  2.7 38.3 %collective-permute-start.1 = (bf16[264,1024]{1,0:T(8,128)(2,1)}, bf16[264,1024]{1,0:T(8,128)(2,1)}, u32[]{:S(2)}, u32[]{:S(2)}) collective-permute-start(bf16[264,1024]{1,0:T(8,128)(2,1)} %get-tuple-element.103.message_ref), channel_id=1, source_target_pairs={{0,16},{8,24},{16,0},{24,8},{1,17},{9,25},{17,1},{25,9},{2,18},{10... | collective-permute-start | bytes 1622024 | tf_op jit(solution)/shard_map/ppermute | solution.py:392
  5.8 46.4 %collective-permute-start.4 = (bf16[256,1024]{1,0:T(8,128)(2,1)}, bf16[256,1024]{1,0:T(8,128)(2,1)}, u32[]{:S(2)}, u32[]{:S(2)}) collective-permute-start(bf16[256,1024]{1,0:T(8,128)(2,1)} %out_grad_ref.1), channel_id=1, source_target_pairs={{0,16},{8,24},{16,0},{24,8},{1,17},{9,25},{17,1},{25,9},{2,18},{10... | collective-permute-start | bytes 1572872 | tf_op jit(solution)/shard_map/ppermute | solution.py:392
  5.9 50.6 %collective-permute-start = (bf16[264,1024]{1,0:T(8,128)(2,1)}, bf16[264,1024]{1,0:T(8,128)(2,1)S(1)}, u32[]{:S(2)}, u32[]{:S(2)}) collective-permute-start(bf16[264,1024]{1,0:T(8,128)(2,1)} %get-tuple-element.103.message_ref), channel_id=1, source_target_pairs={{0,8},{8,0},{16,24},{24,16},{1,9},{9,1},{17,25},{25,17},{2,10},{10... | collective-permute-start | bytes 1622024 | tf_op jit(solution)/shard_map/ppermute | solution.py:392
  9.8 2.7 %collective-permute-start.27 = (bf16[64,1024]{1,0:T(8,128)(2,1)}, bf16[64,1024]{1,0:T(8,128)(2,1)S(1)}, u32[]{:S(2)}, u32[]{:S(2)}) collective-permute-start(bf16[64,1024]{1,0:T(8,128)(2,1)} %get-tuple-element.135), channel_id=1, source_target_pairs={{0,1},{1,0},{2,3},{3,2},{4,5},{5,4},{6,7},{7,6},{8,9},{9,8},{10,11... | collective-permute-start | bytes 393224 | tf_op jit(solution)/shard_map/ppermute | solution.py:396
  11.3 44.0 %collective-permute-start.13 = (bf16[256,1024]{1,0:T(8,128)(2,1)}, bf16[256,1024]{1,0:T(8,128)(2,1)S(1)}, u32[]{:S(2)}, u32[]{:S(2)}) collective-permute-start(bf16[256,1024]{1,0:T(8,128)(2,1)} %out_grad_ref.1), channel_id=1, source_target_pairs={{0,8},{8,0},{16,24},{24,16},{1,9},{9,1},{17,25},{25,17},{2,10},{10... | collective-permute-start | bytes 1572872 | tf_op jit(solution)/shard_map/ppermute | solution.py:392
  12.5 5.0 %collective-permute-start.28 = (bf16[64,1024]{1,0:T(8,128)(2,1)}, bf16[64,1024]{1,0:T(8,128)(2,1)S(1)}, u32[]{:S(2)}, u32[]{:S(2)}) collective-permute-start(bf16[64,1024]{1,0:T(8,128)(2,1)} %get-tuple-element.136), channel_id=1, source_target_pairs={{0,2},{1,3},{2,0},{3,1},{4,6},{5,7},{6,4},{7,5},{8,10},{9,11},{10,... | collective-permute-start | bytes 393224 | tf_op jit(solution)/shard_map/ppermute | solution.py:396
  17.5 24.6 %collective-permute-start.29 = (bf16[64,1024]{1,0:T(8,128)(2,1)}, bf16[64,1024]{1,0:T(8,128)(2,1)S(1)}, u32[]{:S(2)}, u32[]{:S(2)}) collective-permute-start(bf16[64,1024]{1,0:T(8,128)(2,1)} %get-tuple-element.137), channel_id=1, source_target_pairs={{0,3},{1,2},{2,1},{3,0},{4,7},{5,6},{6,5},{7,4},{8,11},{9,10},{10,... | collective-permute-start | bytes 393224 | tf_op jit(solution)/shard_map/ppermute | solution.py:396
  41.0 47.5 %collective-permute-start.3 = (bf16[264,1024]{1,0:T(8,128)(2,1)}, bf16[264,1024]{1,0:T(8,128)(2,1)S(1)}, u32[]{:S(2)}, u32[]{:S(2)}) collective-permute-start(bf16[264,1024]{1,0:T(8,128)(2,1)} %collective-permute-done.1.refs_1_), channel_id=1, source_target_pairs={{0,8},{8,0},{16,24},{24,16},{1,9},{9,1},{17,25},{25,17},{2,10},{10... | collective-permute-start | bytes 1622024 | tf_op jit(solution)/shard_map/ppermute | solution.py:392
  42.2 11.2 %collective-permute-start.30 = (bf16[64,1024]{1,0:T(8,128)(2,1)}, bf16[64,1024]{1,0:T(8,128)(2,1)S(1)}, u32[]{:S(2)}, u32[]{:S(2)}) collective-permute-start(bf16[64,1024]{1,0:T(8,128)(2,1)} %get-tuple-element.138), channel_id=1, source_target_pairs={{0,4},{1,5},{2,6},{3,7},{4,0},{5,1},{6,2},{7,3},{8,12},{9,13},{10,... | collective-permute-start | bytes 393224 | tf_op jit(solution)/shard_map/ppermute | solution.py:396
  52.2 35.1 %collective-permute-start.5 = (bf16[256,1024]{1,0:T(8,128)(2,1)}, bf16[256,1024]{1,0:T(8,128)(2,1)S(1)}, u32[]{:S(2)}, u32[]{:S(2)}) collective-permute-start(bf16[256,1024]{1,0:T(8,128)(2,1)} %collective-permute-done.4.refs_1_), channel_id=1, source_target_pairs={{0,8},{8,0},{16,24},{24,16},{1,9},{9,1},{17,25},{25,17},{2,10},{10... | collective-permute-start | bytes 1572872 | tf_op jit(solution)/shard_map/ppermute | solution.py:392
  53.4 16.6 %collective-permute-start.31 = (bf16[64,1024]{1,0:T(8,128)(2,1)}, bf16[64,1024]{1,0:T(8,128)(2,1)}, u32[]{:S(2)}, u32[]{:S(2)}) collective-permute-start(bf16[64,1024]{1,0:T(8,128)(2,1)} %get-tuple-element.139), channel_id=1, source_target_pairs={{0,5},{1,4},{2,7},{3,6},{4,1},{5,0},{6,3},{7,2},{8,13},{9,12},{10,... | collective-permute-start | bytes 393224 | tf_op jit(solution)/shard_map/ppermute | solution.py:396
  55.3 14.9 %collective-permute-start.32 = (bf16[64,1024]{1,0:T(8,128)(2,1)}, bf16[64,1024]{1,0:T(8,128)(2,1)}, u32[]{:S(2)}, u32[]{:S(2)}) collective-permute-start(bf16[64,1024]{1,0:T(8,128)(2,1)} %get-tuple-element.140), channel_id=1, source_target_pairs={{0,6},{1,7},{2,4},{3,5},{4,2},{5,3},{6,0},{7,1},{8,14},{9,15},{10,... | collective-permute-start | bytes 393224 | tf_op jit(solution)/shard_map/ppermute | solution.py:396
  56.5 15.3 %collective-permute-start.33 = (bf16[64,1024]{1,0:T(8,128)(2,1)}, bf16[64,1024]{1,0:T(8,128)(2,1)}, u32[]{:S(2)}, u32[]{:S(2)}) collective-permute-start(bf16[64,1024]{1,0:T(8,128)(2,1)} %get-tuple-element.141), channel_id=1, source_target_pairs={{0,7},{1,6},{2,5},{3,4},{4,3},{5,2},{6,1},{7,0},{8,15},{9,14},{10,... | collective-permute-start | bytes 393224 | tf_op jit(solution)/shard_map/ppermute | solution.py:396
  60.9 28.1 %all-to-all-start = ((bf16[8,24,1024]{2,1,0:T(8,128)(2,1)}), bf16[8,24,1024]{2,1,0:T(8,128)(2,1)S(1)}, u32[]{:S(2)}, u32[]{:S(2)}) async-start(bf16[8,24,1024]{2,1,0:T(8,128)(2,1)} %get-tuple-element.105), calls=%async_computation | async-start | bytes 786432 | tf_op jit(solution)/shard_map/all_to_all | solution.py:844
  70.2 5.2 %collective-permute-start.15 = (bf16[64,1024]{1,0:T(8,128)(2,1)}, bf16[64,1024]{1,0:T(8,128)(2,1)S(1)}, u32[]{:S(2)}, u32[]{:S(2)}) collective-permute-start(bf16[64,1024]{1,0:T(8,128)(2,1)} %get-tuple-element.118), channel_id=1, source_target_pairs={{0,2},{1,3},{2,0},{3,1},{4,6},{5,7},{6,4},{7,5},{8,10},{9,11},{10,... | collective-permute-start | bytes 393224 | tf_op jit(solution)/shard_map/ppermute | solution.py:396
  71.8 6.8 %collective-permute-start.16 = (bf16[64,1024]{1,0:T(8,128)(2,1)}, bf16[64,1024]{1,0:T(8,128)(2,1)S(1)}, u32[]{:S(2)}, u32[]{:S(2)}) collective-permute-start(bf16[64,1024]{1,0:T(8,128)(2,1)} %get-tuple-element.119), channel_id=1, source_target_pairs={{0,3},{1,2},{2,1},{3,0},{4,7},{5,6},{6,5},{7,4},{8,11},{9,10},{10,... | collective-permute-start | bytes 393224 | tf_op jit(solution)/shard_map/ppermute | solution.py:396
  72.9 7.9 %collective-permute-start.17 = (bf16[64,1024]{1,0:T(8,128)(2,1)}, bf16[64,1024]{1,0:T(8,128)(2,1)S(1)}, u32[]{:S(2)}, u32[]{:S(2)}) collective-permute-start(bf16[64,1024]{1,0:T(8,128)(2,1)} %get-tuple-element.120), channel_id=1, source_target_pairs={{0,4},{1,5},{2,6},{3,7},{4,0},{5,1},{6,2},{7,3},{8,12},{9,13},{10,... | collective-permute-start | bytes 393224 | tf_op jit(solution)/shard_map/ppermute | solution.py:396
  76.1 5.6 %collective-permute-start.2 = (bf16[64,1024]{1,0:T(8,128)(2,1)}, bf16[64,1024]{1,0:T(8,128)(2,1)S(1)}, u32[]{:S(2)}, u32[]{:S(2)}) collective-permute-start(bf16[64,1024]{1,0:T(8,128)(2,1)} %get-tuple-element.104), channel_id=1, source_target_pairs={{0,1},{1,0},{2,3},{3,2},{4,5},{5,4},{6,7},{7,6},{8,9},{9,8},{10,11... | collective-permute-start | bytes 393224 | tf_op jit(solution)/shard_map/ppermute | solution.py:396
  79.3 5.2 %collective-permute-start.21 = (bf16[64,1024]{1,0:T(8,128)(2,1)}, bf16[64,1024]{1,0:T(8,128)(2,1)S(1)}, u32[]{:S(2)}, u32[]{:S(2)}) collective-permute-start(bf16[64,1024]{1,0:T(8,128)(2,1)} %get-tuple-element.126), channel_id=1, source_target_pairs={{0,2},{1,3},{2,0},{3,1},{4,6},{5,7},{6,4},{7,5},{8,10},{9,11},{10,... | collective-permute-start | bytes 393224 | tf_op jit(solution)/shard_map/ppermute | solution.py:396
  81.4 16.1 %collective-permute-start.22 = (bf16[64,1024]{1,0:T(8,128)(2,1)}, bf16[64,1024]{1,0:T(8,128)(2,1)}, u32[]{:S(2)}, u32[]{:S(2)}) collective-permute-start(bf16[64,1024]{1,0:T(8,128)(2,1)} %get-tuple-element.127), channel_id=1, source_target_pairs={{0,3},{1,2},{2,1},{3,0},{4,7},{5,6},{6,5},{7,4},{8,11},{9,10},{10,... | collective-permute-start | bytes 393224 | tf_op jit(solution)/shard_map/ppermute | solution.py:396
  81.6 17.5 %collective-permute-start.23 = (bf16[64,1024]{1,0:T(8,128)(2,1)}, bf16[64,1024]{1,0:T(8,128)(2,1)}, u32[]{:S(2)}, u32[]{:S(2)}) collective-permute-start(bf16[64,1024]{1,0:T(8,128)(2,1)} %get-tuple-element.128), channel_id=1, source_target_pairs={{0,4},{1,5},{2,6},{3,7},{4,0},{5,1},{6,2},{7,3},{8,12},{9,13},{10,... | collective-permute-start | bytes 393224 | tf_op jit(solution)/shard_map/ppermute | solution.py:396
  84.5 15.8 %collective-permute-start.24 = (bf16[64,1024]{1,0:T(8,128)(2,1)}, bf16[64,1024]{1,0:T(8,128)(2,1)}, u32[]{:S(2)}, u32[]{:S(2)}) collective-permute-start(bf16[64,1024]{1,0:T(8,128)(2,1)} %get-tuple-element.129), channel_id=1, source_target_pairs={{0,5},{1,4},{2,7},{3,6},{4,1},{5,0},{6,3},{7,2},{8,13},{9,12},{10,... | collective-permute-start | bytes 393224 | tf_op jit(solution)/shard_map/ppermute | solution.py:396
  87.3 14.4 %collective-permute-start.25 = (bf16[64,1024]{1,0:T(8,128)(2,1)}, bf16[64,1024]{1,0:T(8,128)(2,1)}, u32[]{:S(2)}, u32[]{:S(2)}) collective-permute-start(bf16[64,1024]{1,0:T(8,128)(2,1)} %get-tuple-element.130), channel_id=1, source_target_pairs={{0,6},{1,7},{2,4},{3,5},{4,2},{5,3},{6,0},{7,1},{8,14},{9,15},{10,... | collective-permute-start | bytes 393224 | tf_op jit(solution)/shard_map/ppermute | solution.py:396
  88.5 13.4 %collective-permute-start.26 = (bf16[64,1024]{1,0:T(8,128)(2,1)}, bf16[64,1024]{1,0:T(8,128)(2,1)}, u32[]{:S(2)}, u32[]{:S(2)}) collective-permute-start(bf16[64,1024]{1,0:T(8,128)(2,1)} %get-tuple-element.131), channel_id=1, source_target_pairs={{0,7},{1,6},{2,5},{3,4},{4,3},{5,2},{6,1},{7,0},{8,15},{9,14},{10,... | collective-permute-start | bytes 393224 | tf_op jit(solution)/shard_map/ppermute | solution.py:396
  89.7 19.9 %all-to-all-start.1 = ((bf16[8,16,1024]{2,1,0:T(8,128)(2,1)}), bf16[8,16,1024]{2,1,0:T(8,128)(2,1)}, u32[]{:S(2)}, u32[]{:S(2)}) async-start(bf16[8,16,1024]{2,1,0:T(8,128)(2,1)} %shard_map.164), calls=%async_computation.1 | async-start | bytes 524288 | tf_op jit(solution)/shard_map/all_to_all | solution.py:844
  97.5 16.8 %collective-permute-start.18 = (bf16[64,1024]{1,0:T(8,128)(2,1)}, bf16[64,1024]{1,0:T(8,128)(2,1)S(1)}, u32[]{:S(2)}, u32[]{:S(2)}) collective-permute-start(bf16[64,1024]{1,0:T(8,128)(2,1)} %get-tuple-element.121), channel_id=1, source_target_pairs={{0,5},{1,4},{2,7},{3,6},{4,1},{5,0},{6,3},{7,2},{8,13},{9,12},{10,... | collective-permute-start | bytes 393224 | tf_op jit(solution)/shard_map/ppermute | solution.py:396
  99.1 16.1 %collective-permute-start.19 = (bf16[64,1024]{1,0:T(8,128)(2,1)}, bf16[64,1024]{1,0:T(8,128)(2,1)S(1)}, u32[]{:S(2)}, u32[]{:S(2)}) collective-permute-start(bf16[64,1024]{1,0:T(8,128)(2,1)} %get-tuple-element.122), channel_id=1, source_target_pairs={{0,6},{1,7},{2,4},{3,5},{4,2},{5,3},{6,0},{7,1},{8,14},{9,15},{10,... | collective-permute-start | bytes 393224 | tf_op jit(solution)/shard_map/ppermute | solution.py:396
  100.3 15.0 %collective-permute-start.20 = (bf16[64,1024]{1,0:T(8,128)(2,1)}, bf16[64,1024]{1,0:T(8,128)(2,1)S(1)}, u32[]{:S(2)}, u32[]{:S(2)}) collective-permute-start(bf16[64,1024]{1,0:T(8,128)(2,1)} %get-tuple-element.123), channel_id=1, source_target_pairs={{0,7},{1,6},{2,5},{3,4},{4,3},{5,2},{6,1},{7,0},{8,15},{9,14},{10,... | collective-permute-start | bytes 393224 | tf_op jit(solution)/shard_map/ppermute | solution.py:396
  101.8 15.0 %collective-permute-start.6 = (bf16[64,1024]{1,0:T(8,128)(2,1)}, bf16[64,1024]{1,0:T(8,128)(2,1)}, u32[]{:S(2)}, u32[]{:S(2)}) collective-permute-start(bf16[64,1024]{1,0:T(8,128)(2,1)} %get-tuple-element.108), channel_id=1, source_target_pairs={{0,1},{1,0},{2,3},{3,2},{4,5},{5,4},{6,7},{7,6},{8,9},{9,8},{10,11... | collective-permute-start | bytes 393224 | tf_op jit(solution)/shard_map/ppermute | solution.py:396
  101.9 15.9 %collective-permute-start.7 = (bf16[64,1024]{1,0:T(8,128)(2,1)}, bf16[64,1024]{1,0:T(8,128)(2,1)}, u32[]{:S(2)}, u32[]{:S(2)}) collective-permute-start(bf16[64,1024]{1,0:T(8,128)(2,1)} %get-tuple-element.109), channel_id=1, source_target_pairs={{0,2},{1,3},{2,0},{3,1},{4,6},{5,7},{6,4},{7,5},{8,10},{9,11},{10,... | collective-permute-start | bytes 393224 | tf_op jit(solution)/shard_map/ppermute | solution.py:396
  114.2 11.4 %collective-permute-start.8 = (bf16[64,1024]{1,0:T(8,128)(2,1)S(1)}, bf16[64,1024]{1,0:T(8,128)(2,1)S(1)}, u32[]{:S(2)}, u32[]{:S(2)}) collective-permute-start(bf16[64,1024]{1,0:T(8,128)(2,1)S(1)} %copy-done.31), channel_id=1, source_target_pairs={{0,3},{1,2},{2,1},{3,0},{4,7},{5,6},{6,5},{7,4},{8,11},{9,10},{10,... | collective-permute-start | bytes 393224 | tf_op jit(solution)/shard_map/ppermute | solution.py:396
  115.2 10.5 %collective-permute-start.9 = (bf16[64,1024]{1,0:T(8,128)(2,1)S(1)}, bf16[64,1024]{1,0:T(8,128)(2,1)S(1)}, u32[]{:S(2)}, u32[]{:S(2)}) collective-permute-start(bf16[64,1024]{1,0:T(8,128)(2,1)S(1)} %copy-done.30), channel_id=1, source_target_pairs={{0,4},{1,5},{2,6},{3,7},{4,0},{5,1},{6,2},{7,3},{8,12},{9,13},{10,... | collective-permute-start | bytes 393224 | tf_op jit(solution)/shard_map/ppermute | solution.py:396
  115.3 13.6 %collective-permute-start.10 = (bf16[64,1024]{1,0:T(8,128)(2,1)S(1)}, bf16[64,1024]{1,0:T(8,128)(2,1)S(1)}, u32[]{:S(2)}, u32[]{:S(2)}) collective-permute-start(bf16[64,1024]{1,0:T(8,128)(2,1)S(1)} %copy-done.29), channel_id=1, source_target_pairs={{0,5},{1,4},{2,7},{3,6},{4,1},{5,0},{6,3},{7,2},{8,13},{9,12},{10,... | collective-permute-start | bytes 393224 | tf_op jit(solution)/shard_map/ppermute | solution.py:396
  116.7 12.1 %collective-permute-start.11 = (bf16[64,1024]{1,0:T(8,128)(2,1)S(1)}, bf16[64,1024]{1,0:T(8,128)(2,1)S(1)}, u32[]{:S(2)}, u32[]{:S(2)}) collective-permute-start(bf16[64,1024]{1,0:T(8,128)(2,1)S(1)} %copy-done.28), channel_id=1, source_target_pairs={{0,6},{1,7},{2,4},{3,5},{4,2},{5,3},{6,0},{7,1},{8,14},{9,15},{10,... | collective-permute-start | bytes 393224 | tf_op jit(solution)/shard_map/ppermute | solution.py:396
  117.8 11.0 %collective-permute-start.12 = (bf16[64,1024]{1,0:T(8,128)(2,1)S(1)}, bf16[64,1024]{1,0:T(8,128)(2,1)S(1)}, u32[]{:S(2)}, u32[]{:S(2)}) collective-permute-start(bf16[64,1024]{1,0:T(8,128)(2,1)S(1)} %copy-done.27), channel_id=1, source_target_pairs={{0,7},{1,6},{2,5},{3,4},{4,3},{5,2},{6,1},{7,0},{8,15},{9,14},{10,... | collective-permute-start | bytes 393224 | tf_op jit(solution)/shard_map/ppermute | solution.py:396
  133.4 54.7 %all-to-all-start.2 = ((bf16[32,32,1024]{2,1,0:T(8,128)(2,1)}), bf16[32,32,1024]{2,1,0:T(8,128)(2,1)S(1)}, u32[]{:S(2)}, u32[]{:S(2)}) async-start(bf16[32,32,1024]{2,1,0:T(8,128)(2,1)} %bitcast.35), calls=%async_computation.2 | async-start | bytes 4194304 | tf_op jit(solution)/shard_map/all_to_all | solution.py:844
  139.6 48.5 %collective-permute-start.35 = (f32[8,256]{1,0:T(8,128)S(1)}, f32[8,256]{1,0:T(8,128)S(1)}, u32[]{:S(2)}, u32[]{:S(2)}) collective-permute-start(f32[8,256]{1,0:T(8,128)S(1)} %get-tuple-element.198), channel_id=1, source_target_pairs={{0,16},{8,24},{16,0},{24,8},{1,17},{9,25},{17,1},{25,9},{2,18},{10... | collective-permute-start | bytes 24584 | tf_op jit(solution)/shard_map/ppermute | solution.py:392
  141.9 46.2 %collective-permute-start.34 = (f32[8,256]{1,0:T(8,128)S(1)}, f32[8,256]{1,0:T(8,128)S(1)}, u32[]{:S(2)}, u32[]{:S(2)}) collective-permute-start(f32[8,256]{1,0:T(8,128)S(1)} %get-tuple-element.199), channel_id=1, source_target_pairs={{0,8},{8,0},{16,24},{24,16},{1,9},{9,1},{17,25},{25,17},{2,10},{10... | collective-permute-start | bytes 24584 | tf_op jit(solution)/shard_map/ppermute | solution.py:392
  143.1 45.0 %collective-permute-start.36 = (f32[8,256]{1,0:T(8,128)S(1)}, f32[8,256]{1,0:T(8,128)S(1)}, u32[]{:S(2)}, u32[]{:S(2)}) collective-permute-start(f32[8,256]{1,0:T(8,128)S(1)} %bitcast.40), channel_id=1, source_target_pairs={{0,24},{8,16},{16,8},{24,0},{1,25},{9,17},{17,9},{25,1},{2,26},{10... | collective-permute-start | bytes 24584 | tf_op jit(solution)/shard_map/ppermute | solution.py:392
  191.6 17.1 %all-to-all-start.3 = ((bf16[8,16,1024]{2,1,0:T(8,128)(2,1)}), bf16[8,16,1024]{2,1,0:T(8,128)(2,1)S(1)}, u32[]{:S(2)}, u32[]{:S(2)}) async-start(bf16[8,16,1024]{2,1,0:T(8,128)(2,1)} %bitcast.36), calls=%async_computation.3 | async-start | bytes 524288 | tf_op jit(solution)/shard_map/all_to_all | solution.py:844
  197.1 3.8 %collective-permute-start.37 = (f32[8,128]{1,0:T(8,128)S(1)}, f32[8,128]{1,0:T(8,128)S(1)}, u32[]{:S(2)}, u32[]{:S(2)}) collective-permute-start(f32[8,128]{1,0:T(8,128)S(1)} %get-tuple-element.189), channel_id=1, source_target_pairs={{0,1},{1,0},{2,3},{3,2},{4,5},{5,4},{6,7},{7,6},{8,9},{9,8},{10,11... | collective-permute-start | bytes 12296 | tf_op jit(solution)/shard_map/ppermute | solution.py:396
  197.2 6.1 %collective-permute-start.38 = (f32[8,128]{1,0:T(8,128)S(1)}, f32[8,128]{1,0:T(8,128)S(1)}, u32[]{:S(2)}, u32[]{:S(2)}) collective-permute-start(f32[8,128]{1,0:T(8,128)S(1)} %get-tuple-element.190), channel_id=1, source_target_pairs={{0,2},{1,3},{2,0},{3,1},{4,6},{5,7},{6,4},{7,5},{8,10},{9,11},{10,... | collective-permute-start | bytes 12296 | tf_op jit(solution)/shard_map/ppermute | solution.py:396
  198.9 4.8 %collective-permute-start.39 = (f32[8,128]{1,0:T(8,128)S(1)}, f32[8,128]{1,0:T(8,128)S(1)}, u32[]{:S(2)}, u32[]{:S(2)}) collective-permute-start(f32[8,128]{1,0:T(8,128)S(1)} %get-tuple-element.191), channel_id=1, source_target_pairs={{0,3},{1,2},{2,1},{3,0},{4,7},{5,6},{6,5},{7,4},{8,11},{9,10},{10,... | collective-permute-start | bytes 12296 | tf_op jit(solution)/shard_map/ppermute | solution.py:396
  199.3 4.4 %collective-permute-start.40 = (f32[8,128]{1,0:T(8,128)S(1)}, f32[8,128]{1,0:T(8,128)S(1)}, u32[]{:S(2)}, u32[]{:S(2)}) collective-permute-start(f32[8,128]{1,0:T(8,128)S(1)} %get-tuple-element.192), channel_id=1, source_target_pairs={{0,4},{1,5},{2,6},{3,7},{4,0},{5,1},{6,2},{7,3},{8,12},{9,13},{10,... | collective-permute-start | bytes 12296 | tf_op jit(solution)/shard_map/ppermute | solution.py:396
  200.7 3.1 %collective-permute-start.41 = (f32[8,128]{1,0:T(8,128)S(1)}, f32[8,128]{1,0:T(8,128)S(1)}, u32[]{:S(2)}, u32[]{:S(2)}) collective-permute-start(f32[8,128]{1,0:T(8,128)S(1)} %get-tuple-element.193), channel_id=1, source_target_pairs={{0,5},{1,4},{2,7},{3,6},{4,1},{5,0},{6,3},{7,2},{8,13},{9,12},{10,... | collective-permute-start | bytes 12296 | tf_op jit(solution)/shard_map/ppermute | solution.py:396
  200.9 3.4 %collective-permute-start.42 = (f32[8,128]{1,0:T(8,128)S(1)}, f32[8,128]{1,0:T(8,128)S(1)}, u32[]{:S(2)}, u32[]{:S(2)}) collective-permute-start(f32[8,128]{1,0:T(8,128)S(1)} %get-tuple-element.194), channel_id=1, source_target_pairs={{0,6},{1,7},{2,4},{3,5},{4,2},{5,3},{6,0},{7,1},{8,14},{9,15},{10,... | collective-permute-start | bytes 12296 | tf_op jit(solution)/shard_map/ppermute | solution.py:396
  203.3 3.9 %collective-permute-start.43 = (f32[8,128]{1,0:T(8,128)S(1)}, f32[8,128]{1,0:T(8,128)S(1)}, u32[]{:S(2)}, u32[]{:S(2)}) collective-permute-start(f32[8,128]{1,0:T(8,128)S(1)} %get-tuple-element.195), channel_id=1, source_target_pairs={{0,7},{1,6},{2,5},{3,4},{4,3},{5,2},{6,1},{7,0},{8,15},{9,14},{10,... | collective-permute-start | bytes 12296 | tf_op jit(solution)/shard_map/ppermute | solution.py:396
  209.4 14.9 %all-to-all-start.4 = ((bf16[8,16,1024]{2,1,0:T(8,128)(2,1)}), bf16[8,16,1024]{2,1,0:T(8,128)(2,1)S(1)}, u32[]{:S(2)}, u32[]{:S(2)}) async-start(bf16[8,16,1024]{2,1,0:T(8,128)(2,1)} %shard_map.175), calls=%async_computation.4 | async-start | bytes 524288 | tf_op jit(solution)/shard_map/all_to_all | solution.py:844
  (36 other events, 412.8 us)

commit v5 on v4

--- a/solution.py
+++ b/solution.py
@@ -273,10 +273,7 @@
     pre_ref[...] = pre
     row_ref[0] = dot(pre, up_ref[...], 1, 1).astype(BF16)
     prod = act_grad * act.astype(F32)
-    high = prod.astype(BF16)
-    low = (prod - high.astype(F32)).astype(BF16)
-    ones = jnp.ones((8, prod.shape[1]), BF16)
-    term_ref[0] = dot(ones, high, 1, 1) + dot(ones, low, 1, 1)
+    term_ref[0] = dot(jnp.ones((8, prod.shape[1]), BF16), prod.astype(BF16), 1, 1)
 
 
 def routed_kernel(count, me_ref, *refs):

time: 230 us -> 229 us (level)
  no operation moved by 1% of the time
where the time goes in v5:
time: 229 us; the launch traced here: 228 us
  waiting for transfers between devices  78 us (34%)
  starting transfers between devices  74.8 us (33%)
  Pallas kernels  66.4 us (29%)
  local copies, waits for them, and re-layouts  6.21 us (3%)
    ppermute x9, waiting for transfers between devices, across(): return lax.ppermute(x, 'grp', [(i, i ^ bit) for i in range(planes)])  62.4 us
    pallas_call x16, Pallas kernels, call(): pl.pallas_call(kernel, out_shape=outs, in_specs=in_specs if in_specs is n...  48.4 us
    ppermute x35, starting transfers between devices, spread_out(): lax.ppermute(part, 'seq', [(i, i ^ x) for i in range(shard_count)])  40.8 us
    all_to_all x5, starting transfers between devices, swap(): return lax.all_to_all(x, axes, split_axis=0, concat_axis=0, tiled=True)  23.5 us
    pallas_call x4, Pallas kernels, grouped(): pl.pallas_call(functools.partial(kernel, len(parts)), out_shape=outs, gri...  18 us
    ppermute x35, waiting for transfers between devices, spread_out(): lax.ppermute(part, 'seq', [(i, i ^ x) for i in range(shard_count)])  15.5 us
    ppermute x9, starting transfers between devices, across(): return lax.ppermute(x, 'grp', [(i, i ^ bit) for i in range(planes)])  10.5 us
    unnamed x70, local copies, waits for them, and re-layouts  6.2 us
  transfers between devices with their start and end apart: 49, of which 11 were waited for; matrix products, arithmetic and copies ran while one was open for 1% of the time, Pallas kernels for 23%

profile of v5, /device:TPU:1, one launch (start us, length us, event | category | flops | bytes accessed | tf_op | source)
XLA Modules:
  0.0 227.7 jit_solution(3195425382888592236)
XLA Ops:
  0.6 2.1 shard_map.161
  2.7 3.1 %collective-permute-start.1 = (bf16[264,1024]{1,0:T(8,128)(2,1)}, bf16[264,1024]{1,0:T(8,128)(2,1)}, u32[]{:S(2)}, u32[]{:S(2)}) collective-permute-start(bf16[264,1024]{1,0:T(8,128)(2,1)} %get-tuple-element.103.message_ref), channel_id=1, source_target_pairs={{0,16},{8,24},{16,0},{24,8},{1,17},{9,25},{17,1},{25,9},{2,18},{10... | collective-permute-start | bytes 1622024 | tf_op jit(solution)/shard_map/ppermute | solution.py:389
  5.9 1.3 collective-permute-start
  7.3 2.6 %shard_map.168 = (bf16[64,1024]{1,0:T(8,128)(2,1)}, bf16[64,1024]{1,0:T(8,128)(2,1)}, bf16[64,1024]{1,0:T(8,128)(2,1)}, bf16[64,1024]{1,0:T(8,128)(2,1)}, bf16[6...) custom-call(s32[2]{0:T(128)S(1)} %pad_add_fusion.me_ref, ...), custom_call_target="tpu_custom_call" | custom-call | tf_op jit(solution)/shard_map/pallas_call | solution.py:33
  9.8 1.5 collective-permute-start.27
  13.8 3.8 %collective-permute-done.28.refs_2_ = bf16[64,1024]{1,0:T(8,128)(2,1)S(1)} collective-permute-done((bf16[64,1024]{1,0:T(8,128)(2,1)}, bf16[64,1024]{1,0:T(8,128)(2,1)S(1)}, u32[]{:S(2)}, u32[]{:S(2)}) %collective-permute-start.28) | collective-permute-done | bytes 131104 | tf_op jit(solution)/shard_map/ppermute | solution.py:393
  17.5 2.2 collective-permute-start.29
  19.8 21.2 %collective-permute-done.1.refs_1_ = bf16[264,1024]{1,0:T(8,128)(2,1)} collective-permute-done((bf16[264,1024]{1,0:T(8,128)(2,1)}, bf16[264,1024]{1,0:T(8,128)(2,1)}, u32[]{:S(2)}, u32[]{:S(2)}) %collective-permute-start.1) | collective-permute-done | bytes 540704 | tf_op jit(solution)/shard_map/ppermute | solution.py:389
  43.4 8.8 %collective-permute-done.4.refs_1_ = bf16[256,1024]{1,0:T(8,128)(2,1)} collective-permute-done((bf16[256,1024]{1,0:T(8,128)(2,1)}, bf16[256,1024]{1,0:T(8,128)(2,1)}, u32[]{:S(2)}, u32[]{:S(2)}) %collective-permute-start.4) | collective-permute-done | bytes 524320 | tf_op jit(solution)/shard_map/ppermute | solution.py:389
  53.4 1.9 collective-permute-start.31
  57.7 3.2 %shard_map.163 = (f32[256,16]{1,0:T(8,128)}, f32[16,1,256]{2,1,0:T(1,128)}, bf16[256,1024]{1,0:T(8,128)(2,1)}, bf16[256,1024]{1,0:T(8,128)(2,1)}, bf16[256,1024]...) custom-call(bf16[256,1024]{1,0:T(8,128)(2,1)} %inputs_ref.5, bf16[256,128]{1,0:T(8,128)(2,1)} %writes_ref.7, f32[16,256]{1,0:T(8,128)} %bitcast.37), custom_call_target="tpu_custom_call" | custom-call | tf_op jit(solution)/shard_map/pallas_call | solution.py:33
  60.9 3.9 %all-to-all-start = ((bf16[8,24,1024]{2,1,0:T(8,128)(2,1)}), bf16[8,24,1024]{2,1,0:T(8,128)(2,1)S(1)}, u32[]{:S(2)}, u32[]{:S(2)}) async-start(bf16[8,24,1024]{2,1,0:T(8,128)(2,1)} %get-tuple-element.105), calls=%async_computation | async-start | bytes 786432 | tf_op jit(solution)/shard_map/all_to_all | solution.py:841
  64.8 2.6 %shard_map.162 = (bf16[64,1024]{1,0:T(8,128)(2,1)}, bf16[64,1024]{1,0:T(8,128)(2,1)}, bf16[64,1024]{1,0:T(8,128)(2,1)}, bf16[64,1024]{1,0:T(8,128)(2,1)}, bf16[6...) custom-call(s32[2]{0:T(128)S(1)} %pad_add_fusion.me_ref, ...), custom_call_target="tpu_custom_call" | custom-call | tf_op jit(solution)/shard_map/pallas_call | solution.py:33
  67.3 2.7 %shard_map.166 = (bf16[64,1024]{1,0:T(8,128)(2,1)}, bf16[64,1024]{1,0:T(8,128)(2,1)}, bf16[64,1024]{1,0:T(8,128)(2,1)}, bf16[64,1024]{1,0:T(8,128)(2,1)}, bf16[6...) custom-call(f32[2,8,256]{2,1,0:T(8,128)} %get-tuple-element.115.keys_ref, ...), custom_call_target="tpu_custom_call" | custom-call | tf_op jit(solution)/shard_map/pallas_call | solution.py:33
  70.2 1.6 collective-permute-start.15
  72.9 1.4 collective-permute-start.17
  76.1 1.8 collective-permute-start.2
  79.3 1.5 collective-permute-start.21
  81.6 1.5 collective-permute-start.23
  84.5 2.8 %collective-permute-start.24 = (bf16[64,1024]{1,0:T(8,128)(2,1)}, bf16[64,1024]{1,0:T(8,128)(2,1)}, u32[]{:S(2)}, u32[]{:S(2)}) collective-permute-start(bf16[64,1024]{1,0:T(8,128)(2,1)} %get-tuple-element.129), channel_id=1, source_target_pairs={{0,5},{1,4},{2,7},{3,6},{4,1},{5,0},{6,3},{7,2},{8,13},{9,12},{10,... | collective-permute-start | bytes 393224 | tf_op jit(solution)/shard_map/ppermute | solution.py:393
  89.7 5.2 %all-to-all-start.1 = ((bf16[8,16,1024]{2,1,0:T(8,128)(2,1)}), bf16[8,16,1024]{2,1,0:T(8,128)(2,1)}, u32[]{:S(2)}, u32[]{:S(2)}) async-start(bf16[8,16,1024]{2,1,0:T(8,128)(2,1)} %shard_map.164), calls=%async_computation.1 | async-start | bytes 524288 | tf_op jit(solution)/shard_map/all_to_all | solution.py:841
  95.5 1.9 shard_map.165
  97.5 1.7 collective-permute-start.18
  100.3 1.5 collective-permute-start.20
  103.1 1.6 copy-done.1
  104.7 4.8 %shard_map.169 = (bf16[256,1024]{1,0:T(8,128)(2,1)}, bf16[256,1024]{1,0:T(8,128)(2,1)}, bf16[256,1024]{1,0:T(8,128)(2,1)}, bf16[256,1024]{1,0:T(8,128)(2,1)}, bf...) custom-call(s32[2]{0:T(128)S(1)} %copy-done.15, bf16[64,1024]{1,0:T(8,128)(2,1)} %get-tuple-element.134.refs_0_, ...), custom_call_target="tpu_custom_call" | custom-call | flops 1610612736 | bytes 6291456 | tf_op jit(solution)/shard_map/pallas_call | solution.py:335
  109.6 4.5 %shard_map.167 = (bf16[512,1024]{1,0:T(8,128)(2,1)}, bf16[512,1024]{1,0:T(8,128)(2,1)}, f32[512,1024]{1,0:T(8,128)S(1)}) custom-call(s32[2]{0:T(128)S(1)} %copy-done.16, bf16[64,1024]{1,0:T(8,128)(2,1)} %get-tuple-element.124.refs_0_, bf16[64,1024]{1,0:T(8,128)(2,1)} %copy-done.32, bf16[64,1024]{1,0:T(8,128)(2,1)} %copy-done.33, ...), custom_call_target="tpu_custom_call" | custom-call | flops 1073741824 | bytes 6291456 | tf_op jit(solution)/shard_map/pallas_call | solution.py:335
  115.1 1.5 collective-permute-start.10
  117.7 1.8 collective-permute-start.12
  120.7 4.3 %shard_map.170 = (bf16[512,1024]{1,0:T(8,128)(2,1)}, bf16[512,1024]{1,0:T(8,128)(2,1)}, bf16[4,256,1024]{2,1,0:T(8,128)(2,1)}, f32[2,8,256]{2,1,0:T(8,128)}) custom-call(s32[2]{0:T(128)S(1)} %copy-done.16, bf16[64,1024]{1,0:T(8,128)(2,1)S(1)} %copy-done.4, bf16[64,1024]{1,0:T(8,128)(2,1)S(1)} %copy-done.6, ...), custom_call_target="tpu_custom_call", output_to_operand_aliasing={{2}: (13, {})} | custom-call | flops 2147483648 | bytes 6291456 | tf_op jit(solution)/shard_map/pallas_call | solution.py:335
  125.0 3.7 %collective-permute-done.10.refs_5_ = bf16[64,1024]{1,0:T(8,128)(2,1)S(1)} collective-permute-done((bf16[64,1024]{1,0:T(8,128)(2,1)S(1)}, bf16[64,1024]{1,0:T(8,128)(2,1)S(1)}, u32[]{:S(2)}, u32[]{:S(2)}) %collective-permute-start.10) | collective-permute-done | bytes 131104 | tf_op jit(solution)/shard_map/ppermute | solution.py:393
  128.7 4.5 %shard_map.171 = (bf16[256,1024]{1,0:T(8,128)(2,1)}, bf16[256,1024]{1,0:T(8,128)(2,1)}, bf16[256,1024]{1,0:T(8,128)(2,1)}, bf16[256,1024]{1,0:T(8,128)(2,1)}, bf...) custom-call(s32[2]{0:T(128)S(1)} %copy-done.16, ...), custom_call_target="tpu_custom_call", output_to_operand_aliasing={{4}: (11, {})} | custom-call | flops 1610612736 | bytes 6291456 | tf_op jit(solution)/shard_map/pallas_call | solution.py:335
  133.1 6.1 %all-to-all-start.2 = ((bf16[32,32,1024]{2,1,0:T(8,128)(2,1)}), bf16[32,32,1024]{2,1,0:T(8,128)(2,1)S(1)}, u32[]{:S(2)}, u32[]{:S(2)}) async-start(bf16[32,32,1024]{2,1,0:T(8,128)(2,1)} %bitcast.35), calls=%async_computation.2 | async-start | bytes 4194304 | tf_op jit(solution)/shard_map/all_to_all | solution.py:841
  139.3 2.3 %collective-permute-start.35 = (f32[8,256]{1,0:T(8,128)S(1)}, f32[8,256]{1,0:T(8,128)S(1)}, u32[]{:S(2)}, u32[]{:S(2)}) collective-permute-start(f32[8,256]{1,0:T(8,128)S(1)} %get-tuple-element.198), channel_id=1, source_target_pairs={{0,16},{8,24},{16,0},{24,8},{1,17},{9,25},{17,1},{25,9},{2,18},{10... | collective-permute-start | bytes 24584 | tf_op jit(solution)/shard_map/ppermute | solution.py:389
  142.9 6.3 %shard_map.172 = bf16[1024,1024]{1,0:T(8,128)(2,1)} custom-call(bf16[256,1024]{1,0:T(8,128)(2,1)} %get-tuple-element.148.refs_0_, bf16[256,1024]{1,0:T(8,128)(2,1)} %get-tuple-element.149.refs_1_, bf16[512,1024]{1,0:T(8,128)(2,1)} %get-tuple-element.132.refs_8_.refs_2_, bf16[512,1024]{1,0:T(8,128)(2,1)} %get-tuple-element.150.refs_3_, ...), custom_call_target="tpu_custom_call" | custom-call | flops 2147483648 | bytes 6291456 | tf_op jit(solution)/shard_map/pallas_call | solution.py:33
  149.2 6.3 %shard_map.173 = bf16[1024,1024]{1,0:T(8,128)(2,1)} custom-call(bf16[256,1024]{1,0:T(8,128)(2,1)} %get-tuple-element.153.refs_0_, bf16[256,1024]{1,0:T(8,128)(2,1)} %get-tuple-element.154.refs_1_, bf16[512,1024]{1,0:T(8,128)(2,1)} %get-tuple-element.155.refs_2_, bf16[512,1024]{1,0:T(8,128)(2,1)} %get-tuple-element.156.refs_3_, ...), custom_call_target="tpu_custom_call" | custom-call | flops 2147483648 | bytes 6291456 | tf_op jit(solution)/shard_map/pallas_call | solution.py:33
  155.6 32.4 %collective-permute-done.35.refs_2_ = f32[8,256]{1,0:T(8,128)S(1)} collective-permute-done((f32[8,256]{1,0:T(8,128)S(1)}, f32[8,256]{1,0:T(8,128)S(1)}, u32[]{:S(2)}, u32[]{:S(2)}) %collective-permute-start.35) | collective-permute-done | bytes 8224 | tf_op jit(solution)/shard_map/ppermute | solution.py:389
  188.0 3.4 %shard_map.174 = (bf16[256,1024]{1,0:T(8,128)(2,1)}, bf16[128,1024]{1,0:T(8,128)(2,1)}) custom-call(bf16[1024,1024]{1,0:T(8,128)(2,1)S(1)} %bitcast.23, s32[2,256]{1,0:T(2,128)} %get-tuple-element.162.targets_ref, bf16[256,1024]{1,0:T(8,128)(2,1)} %resid_ref.3, bf16[256,1024]{1,0:T(8,128)(2,1)} %out_grad_ref.1, bf16[256,128]{1,0:T(8,128)(2,1)} %reads_ref.5, ...), custom_call_target="tpu_custom_call" | custom-call | tf_op jit(solution)/shard_map/pallas_call | solution.py:33
  191.4 4.6 %all-to-all-start.3 = ((bf16[8,16,1024]{2,1,0:T(8,128)(2,1)}), bf16[8,16,1024]{2,1,0:T(8,128)(2,1)S(1)}, u32[]{:S(2)}, u32[]{:S(2)}) async-start(bf16[8,16,1024]{2,1,0:T(8,128)(2,1)} %bitcast.36), calls=%async_computation.3 | async-start | bytes 524288 | tf_op jit(solution)/shard_map/all_to_all | solution.py:841
  196.9 1.7 collective-permute-start.38
  199.1 1.4 collective-permute-start.40
  200.7 2.4 %collective-permute-start.42 = (f32[8,128]{1,0:T(8,128)S(1)}, f32[8,128]{1,0:T(8,128)S(1)}, u32[]{:S(2)}, u32[]{:S(2)}) collective-permute-start(f32[8,128]{1,0:T(8,128)S(1)} %get-tuple-element.194), channel_id=1, source_target_pairs={{0,6},{1,7},{2,4},{3,5},{4,2},{5,3},{6,0},{7,1},{8,14},{9,15},{10,... | collective-permute-start | bytes 12296 | tf_op jit(solution)/shard_map/ppermute | solution.py:393
  204.1 2.9 %collective-permute-done.43.refs_7_ = f32[8,128]{1,0:T(8,128)S(1)} collective-permute-done((f32[8,128]{1,0:T(8,128)S(1)}, f32[8,128]{1,0:T(8,128)S(1)}, u32[]{:S(2)}, u32[]{:S(2)}) %collective-permute-start.43) | collective-permute-done | bytes 4128 | tf_op jit(solution)/shard_map/ppermute | solution.py:393
  207.0 1.4 shard_map.180
  209.2 3.7 %all-to-all-start.4 = ((bf16[8,16,1024]{2,1,0:T(8,128)(2,1)}), bf16[8,16,1024]{2,1,0:T(8,128)(2,1)S(1)}, u32[]{:S(2)}, u32[]{:S(2)}) async-start(bf16[8,16,1024]{2,1,0:T(8,128)(2,1)} %shard_map.175), calls=%async_computation.4 | async-start | bytes 524288 | tf_op jit(solution)/shard_map/all_to_all | solution.py:841
  214.1 5.0 %shard_map.177 = (bf16[256,512]{1,0:T(8,128)(2,1)}, f32[256,128]{1,0:T(8,128)}, f32[256,128]{1,0:T(8,128)}, f32[256,16]{1,0:T(8,128)}, f32[8,1,256]{2,1,0:T(1,128)}) custom-call(bf16[256,1024]{1,0:T(8,128)(2,1)} %inputs_ref.5, bf16[256,1024]{1,0:T(8,128)(2,1)} %get-tuple-element.99.grads_ref, bf16[256,128]{1,0:T(8,128)(2,1)} %writes_ref.7, ...), custom_call_target="tpu_custom_call" | custom-call | flops 268435456 | bytes 1048576 | tf_op jit(solution)/shard_map/pallas_call | solution.py:33
  219.1 4.9 %shard_map.176 = (bf16[256,512]{1,0:T(8,128)(2,1)}, f32[256,128]{1,0:T(8,128)}, f32[256,128]{1,0:T(8,128)}, f32[256,16]{1,0:T(8,128)}, f32[8,1,256]{2,1,0:T(1,128)}) custom-call(bf16[256,1024]{1,0:T(8,128)(2,1)} %inputs_ref.5, bf16[256,1024]{1,0:T(8,128)(2,1)} %get-tuple-element.99.grads_ref, bf16[256,128]{1,0:T(8,128)(2,1)} %writes_ref.7, ...), custom_call_target="tpu_custom_call" | custom-call | flops 268435456 | bytes 1048576 | tf_op jit(solution)/shard_map/pallas_call | solution.py:33
  224.1 3.6 %shard_map.178 = (bf16[256,1024]{1,0:T(8,128)(2,1)}, f32[256,128]{1,0:T(8,128)}, f32[256,128]{1,0:T(8,128)}, f32[16,256]{1,0:T(8,128)}) custom-call(bf16[256,128]{1,0:T(8,128)(2,1)} %writes_ref.7, bf16[128,1024]{1,0:T(8,128)(2,1)} %bitcast.5.state_ref, bf16[128,1024]{1,0:T(8,128)(2,1)S(1)} %bitcast.31, f32[16,1,256]{2,1,0:T(1,128)} %get-tuple-element.165.cumt_ref, ...), custom_call_target="tpu_custom_call" | custom-call | tf_op jit(solution)/shard_map/pallas_call | solution.py:33
  (143 shorter events, 29.9 us)
Async XLA Ops:
  2.7 38.3 %collective-permute-start.1 = (bf16[264,1024]{1,0:T(8,128)(2,1)}, bf16[264,1024]{1,0:T(8,128)(2,1)}, u32[]{:S(2)}, u32[]{:S(2)}) collective-permute-start(bf16[264,1024]{1,0:T(8,128)(2,1)} %get-tuple-element.103.message_ref), channel_id=1, source_target_pairs={{0,16},{8,24},{16,0},{24,8},{1,17},{9,25},{17,1},{25,9},{2,18},{10... | collective-permute-start | bytes 1622024 | tf_op jit(solution)/shard_map/ppermute | solution.py:389
  5.8 46.4 %collective-permute-start.4 = (bf16[256,1024]{1,0:T(8,128)(2,1)}, bf16[256,1024]{1,0:T(8,128)(2,1)}, u32[]{:S(2)}, u32[]{:S(2)}) collective-permute-start(bf16[256,1024]{1,0:T(8,128)(2,1)} %out_grad_ref.1), channel_id=1, source_target_pairs={{0,16},{8,24},{16,0},{24,8},{1,17},{9,25},{17,1},{25,9},{2,18},{10... | collective-permute-start | bytes 1572872 | tf_op jit(solution)/shard_map/ppermute | solution.py:389
  5.9 50.6 %collective-permute-start = (bf16[264,1024]{1,0:T(8,128)(2,1)}, bf16[264,1024]{1,0:T(8,128)(2,1)S(1)}, u32[]{:S(2)}, u32[]{:S(2)}) collective-permute-start(bf16[264,1024]{1,0:T(8,128)(2,1)} %get-tuple-element.103.message_ref), channel_id=1, source_target_pairs={{0,8},{8,0},{16,24},{24,16},{1,9},{9,1},{17,25},{25,17},{2,10},{10... | collective-permute-start | bytes 1622024 | tf_op jit(solution)/shard_map/ppermute | solution.py:389
  9.8 2.7 %collective-permute-start.27 = (bf16[64,1024]{1,0:T(8,128)(2,1)}, bf16[64,1024]{1,0:T(8,128)(2,1)S(1)}, u32[]{:S(2)}, u32[]{:S(2)}) collective-permute-start(bf16[64,1024]{1,0:T(8,128)(2,1)} %get-tuple-element.135), channel_id=1, source_target_pairs={{0,1},{1,0},{2,3},{3,2},{4,5},{5,4},{6,7},{7,6},{8,9},{9,8},{10,11... | collective-permute-start | bytes 393224 | tf_op jit(solution)/shard_map/ppermute | solution.py:393
  11.3 44.0 %collective-permute-start.13 = (bf16[256,1024]{1,0:T(8,128)(2,1)}, bf16[256,1024]{1,0:T(8,128)(2,1)S(1)}, u32[]{:S(2)}, u32[]{:S(2)}) collective-permute-start(bf16[256,1024]{1,0:T(8,128)(2,1)} %out_grad_ref.1), channel_id=1, source_target_pairs={{0,8},{8,0},{16,24},{24,16},{1,9},{9,1},{17,25},{25,17},{2,10},{10... | collective-permute-start | bytes 1572872 | tf_op jit(solution)/shard_map/ppermute | solution.py:389
  12.5 5.0 %collective-permute-start.28 = (bf16[64,1024]{1,0:T(8,128)(2,1)}, bf16[64,1024]{1,0:T(8,128)(2,1)S(1)}, u32[]{:S(2)}, u32[]{:S(2)}) collective-permute-start(bf16[64,1024]{1,0:T(8,128)(2,1)} %get-tuple-element.136), channel_id=1, source_target_pairs={{0,2},{1,3},{2,0},{3,1},{4,6},{5,7},{6,4},{7,5},{8,10},{9,11},{10,... | collective-permute-start | bytes 393224 | tf_op jit(solution)/shard_map/ppermute | solution.py:393
  17.5 24.6 %collective-permute-start.29 = (bf16[64,1024]{1,0:T(8,128)(2,1)}, bf16[64,1024]{1,0:T(8,128)(2,1)S(1)}, u32[]{:S(2)}, u32[]{:S(2)}) collective-permute-start(bf16[64,1024]{1,0:T(8,128)(2,1)} %get-tuple-element.137), channel_id=1, source_target_pairs={{0,3},{1,2},{2,1},{3,0},{4,7},{5,6},{6,5},{7,4},{8,11},{9,10},{10,... | collective-permute-start | bytes 393224 | tf_op jit(solution)/shard_map/ppermute | solution.py:393
  41.0 47.5 %collective-permute-start.3 = (bf16[264,1024]{1,0:T(8,128)(2,1)}, bf16[264,1024]{1,0:T(8,128)(2,1)S(1)}, u32[]{:S(2)}, u32[]{:S(2)}) collective-permute-start(bf16[264,1024]{1,0:T(8,128)(2,1)} %collective-permute-done.1.refs_1_), channel_id=1, source_target_pairs={{0,8},{8,0},{16,24},{24,16},{1,9},{9,1},{17,25},{25,17},{2,10},{10... | collective-permute-start | bytes 1622024 | tf_op jit(solution)/shard_map/ppermute | solution.py:389
  42.2 11.2 %collective-permute-start.30 = (bf16[64,1024]{1,0:T(8,128)(2,1)}, bf16[64,1024]{1,0:T(8,128)(2,1)S(1)}, u32[]{:S(2)}, u32[]{:S(2)}) collective-permute-start(bf16[64,1024]{1,0:T(8,128)(2,1)} %get-tuple-element.138), channel_id=1, source_target_pairs={{0,4},{1,5},{2,6},{3,7},{4,0},{5,1},{6,2},{7,3},{8,12},{9,13},{10,... | collective-permute-start | bytes 393224 | tf_op jit(solution)/shard_map/ppermute | solution.py:393
  52.2 35.1 %collective-permute-start.5 = (bf16[256,1024]{1,0:T(8,128)(2,1)}, bf16[256,1024]{1,0:T(8,128)(2,1)S(1)}, u32[]{:S(2)}, u32[]{:S(2)}) collective-permute-start(bf16[256,1024]{1,0:T(8,128)(2,1)} %collective-permute-done.4.refs_1_), channel_id=1, source_target_pairs={{0,8},{8,0},{16,24},{24,16},{1,9},{9,1},{17,25},{25,17},{2,10},{10... | collective-permute-start | bytes 1572872 | tf_op jit(solution)/shard_map/ppermute | solution.py:389
  53.4 16.6 %collective-permute-start.31 = (bf16[64,1024]{1,0:T(8,128)(2,1)}, bf16[64,1024]{1,0:T(8,128)(2,1)}, u32[]{:S(2)}, u32[]{:S(2)}) collective-permute-start(bf16[64,1024]{1,0:T(8,128)(2,1)} %get-tuple-element.139), channel_id=1, source_target_pairs={{0,5},{1,4},{2,7},{3,6},{4,1},{5,0},{6,3},{7,2},{8,13},{9,12},{10,... | collective-permute-start | bytes 393224 | tf_op jit(solution)/shard_map/ppermute | solution.py:393
  55.3 14.9 %collective-permute-start.32 = (bf16[64,1024]{1,0:T(8,128)(2,1)}, bf16[64,1024]{1,0:T(8,128)(2,1)}, u32[]{:S(2)}, u32[]{:S(2)}) collective-permute-start(bf16[64,1024]{1,0:T(8,128)(2,1)} %get-tuple-element.140), channel_id=1, source_target_pairs={{0,6},{1,7},{2,4},{3,5},{4,2},{5,3},{6,0},{7,1},{8,14},{9,15},{10,... | collective-permute-start | bytes 393224 | tf_op jit(solution)/shard_map/ppermute | solution.py:393
  56.5 15.3 %collective-permute-start.33 = (bf16[64,1024]{1,0:T(8,128)(2,1)}, bf16[64,1024]{1,0:T(8,128)(2,1)}, u32[]{:S(2)}, u32[]{:S(2)}) collective-permute-start(bf16[64,1024]{1,0:T(8,128)(2,1)} %get-tuple-element.141), channel_id=1, source_target_pairs={{0,7},{1,6},{2,5},{3,4},{4,3},{5,2},{6,1},{7,0},{8,15},{9,14},{10,... | collective-permute-start | bytes 393224 | tf_op jit(solution)/shard_map/ppermute | solution.py:393
  60.9 28.1 %all-to-all-start = ((bf16[8,24,1024]{2,1,0:T(8,128)(2,1)}), bf16[8,24,1024]{2,1,0:T(8,128)(2,1)S(1)}, u32[]{:S(2)}, u32[]{:S(2)}) async-start(bf16[8,24,1024]{2,1,0:T(8,128)(2,1)} %get-tuple-element.105), calls=%async_computation | async-start | bytes 786432 | tf_op jit(solution)/shard_map/all_to_all | solution.py:841
  70.2 5.2 %collective-permute-start.15 = (bf16[64,1024]{1,0:T(8,128)(2,1)}, bf16[64,1024]{1,0:T(8,128)(2,1)S(1)}, u32[]{:S(2)}, u32[]{:S(2)}) collective-permute-start(bf16[64,1024]{1,0:T(8,128)(2,1)} %get-tuple-element.118), channel_id=1, source_target_pairs={{0,2},{1,3},{2,0},{3,1},{4,6},{5,7},{6,4},{7,5},{8,10},{9,11},{10,... | collective-permute-start | bytes 393224 | tf_op jit(solution)/shard_map/ppermute | solution.py:393
  71.8 6.8 %collective-permute-start.16 = (bf16[64,1024]{1,0:T(8,128)(2,1)}, bf16[64,1024]{1,0:T(8,128)(2,1)S(1)}, u32[]{:S(2)}, u32[]{:S(2)}) collective-permute-start(bf16[64,1024]{1,0:T(8,128)(2,1)} %get-tuple-element.119), channel_id=1, source_target_pairs={{0,3},{1,2},{2,1},{3,0},{4,7},{5,6},{6,5},{7,4},{8,11},{9,10},{10,... | collective-permute-start | bytes 393224 | tf_op jit(solution)/shard_map/ppermute | solution.py:393
  72.9 7.9 %collective-permute-start.17 = (bf16[64,1024]{1,0:T(8,128)(2,1)}, bf16[64,1024]{1,0:T(8,128)(2,1)S(1)}, u32[]{:S(2)}, u32[]{:S(2)}) collective-permute-start(bf16[64,1024]{1,0:T(8,128)(2,1)} %get-tuple-element.120), channel_id=1, source_target_pairs={{0,4},{1,5},{2,6},{3,7},{4,0},{5,1},{6,2},{7,3},{8,12},{9,13},{10,... | collective-permute-start | bytes 393224 | tf_op jit(solution)/shard_map/ppermute | solution.py:393
  76.1 5.6 %collective-permute-start.2 = (bf16[64,1024]{1,0:T(8,128)(2,1)}, bf16[64,1024]{1,0:T(8,128)(2,1)S(1)}, u32[]{:S(2)}, u32[]{:S(2)}) collective-permute-start(bf16[64,1024]{1,0:T(8,128)(2,1)} %get-tuple-element.104), channel_id=1, source_target_pairs={{0,1},{1,0},{2,3},{3,2},{4,5},{5,4},{6,7},{7,6},{8,9},{9,8},{10,11... | collective-permute-start | bytes 393224 | tf_op jit(solution)/shard_map/ppermute | solution.py:393
  79.3 5.2 %collective-permute-start.21 = (bf16[64,1024]{1,0:T(8,128)(2,1)}, bf16[64,1024]{1,0:T(8,128)(2,1)S(1)}, u32[]{:S(2)}, u32[]{:S(2)}) collective-permute-start(bf16[64,1024]{1,0:T(8,128)(2,1)} %get-tuple-element.126), channel_id=1, source_target_pairs={{0,2},{1,3},{2,0},{3,1},{4,6},{5,7},{6,4},{7,5},{8,10},{9,11},{10,... | collective-permute-start | bytes 393224 | tf_op jit(solution)/shard_map/ppermute | solution.py:393
  81.4 16.1 %collective-permute-start.22 = (bf16[64,1024]{1,0:T(8,128)(2,1)}, bf16[64,1024]{1,0:T(8,128)(2,1)}, u32[]{:S(2)}, u32[]{:S(2)}) collective-permute-start(bf16[64,1024]{1,0:T(8,128)(2,1)} %get-tuple-element.127), channel_id=1, source_target_pairs={{0,3},{1,2},{2,1},{3,0},{4,7},{5,6},{6,5},{7,4},{8,11},{9,10},{10,... | collective-permute-start | bytes 393224 | tf_op jit(solution)/shard_map/ppermute | solution.py:393
  81.6 17.5 %collective-permute-start.23 = (bf16[64,1024]{1,0:T(8,128)(2,1)}, bf16[64,1024]{1,0:T(8,128)(2,1)}, u32[]{:S(2)}, u32[]{:S(2)}) collective-permute-start(bf16[64,1024]{1,0:T(8,128)(2,1)} %get-tuple-element.128), channel_id=1, source_target_pairs={{0,4},{1,5},{2,6},{3,7},{4,0},{5,1},{6,2},{7,3},{8,12},{9,13},{10,... | collective-permute-start | bytes 393224 | tf_op jit(solution)/shard_map/ppermute | solution.py:393
  84.5 15.8 %collective-permute-start.24 = (bf16[64,1024]{1,0:T(8,128)(2,1)}, bf16[64,1024]{1,0:T(8,128)(2,1)}, u32[]{:S(2)}, u32[]{:S(2)}) collective-permute-start(bf16[64,1024]{1,0:T(8,128)(2,1)} %get-tuple-element.129), channel_id=1, source_target_pairs={{0,5},{1,4},{2,7},{3,6},{4,1},{5,0},{6,3},{7,2},{8,13},{9,12},{10,... | collective-permute-start | bytes 393224 | tf_op jit(solution)/shard_map/ppermute | solution.py:393
  87.3 14.4 %collective-permute-start.25 = (bf16[64,1024]{1,0:T(8,128)(2,1)}, bf16[64,1024]{1,0:T(8,128)(2,1)}, u32[]{:S(2)}, u32[]{:S(2)}) collective-permute-start(bf16[64,1024]{1,0:T(8,128)(2,1)} %get-tuple-element.130), channel_id=1, source_target_pairs={{0,6},{1,7},{2,4},{3,5},{4,2},{5,3},{6,0},{7,1},{8,14},{9,15},{10,... | collective-permute-start | bytes 393224 | tf_op jit(solution)/shard_map/ppermute | solution.py:393
  88.5 13.4 %collective-permute-start.26 = (bf16[64,1024]{1,0:T(8,128)(2,1)}, bf16[64,1024]{1,0:T(8,128)(2,1)}, u32[]{:S(2)}, u32[]{:S(2)}) collective-permute-start(bf16[64,1024]{1,0:T(8,128)(2,1)} %get-tuple-element.131), channel_id=1, source_target_pairs={{0,7},{1,6},{2,5},{3,4},{4,3},{5,2},{6,1},{7,0},{8,15},{9,14},{10,... | collective-permute-start | bytes 393224 | tf_op jit(solution)/shard_map/ppermute | solution.py:393
  89.7 19.8 %all-to-all-start.1 = ((bf16[8,16,1024]{2,1,0:T(8,128)(2,1)}), bf16[8,16,1024]{2,1,0:T(8,128)(2,1)}, u32[]{:S(2)}, u32[]{:S(2)}) async-start(bf16[8,16,1024]{2,1,0:T(8,128)(2,1)} %shard_map.164), calls=%async_computation.1 | async-start | bytes 524288 | tf_op jit(solution)/shard_map/all_to_all | solution.py:841
  97.5 16.6 %collective-permute-start.18 = (bf16[64,1024]{1,0:T(8,128)(2,1)}, bf16[64,1024]{1,0:T(8,128)(2,1)S(1)}, u32[]{:S(2)}, u32[]{:S(2)}) collective-permute-start(bf16[64,1024]{1,0:T(8,128)(2,1)} %get-tuple-element.121), channel_id=1, source_target_pairs={{0,5},{1,4},{2,7},{3,6},{4,1},{5,0},{6,3},{7,2},{8,13},{9,12},{10,... | collective-permute-start | bytes 393224 | tf_op jit(solution)/shard_map/ppermute | solution.py:393
  99.1 15.9 %collective-permute-start.19 = (bf16[64,1024]{1,0:T(8,128)(2,1)}, bf16[64,1024]{1,0:T(8,128)(2,1)S(1)}, u32[]{:S(2)}, u32[]{:S(2)}) collective-permute-start(bf16[64,1024]{1,0:T(8,128)(2,1)} %get-tuple-element.122), channel_id=1, source_target_pairs={{0,6},{1,7},{2,4},{3,5},{4,2},{5,3},{6,0},{7,1},{8,14},{9,15},{10,... | collective-permute-start | bytes 393224 | tf_op jit(solution)/shard_map/ppermute | solution.py:393
  100.3 14.9 %collective-permute-start.20 = (bf16[64,1024]{1,0:T(8,128)(2,1)}, bf16[64,1024]{1,0:T(8,128)(2,1)S(1)}, u32[]{:S(2)}, u32[]{:S(2)}) collective-permute-start(bf16[64,1024]{1,0:T(8,128)(2,1)} %get-tuple-element.123), channel_id=1, source_target_pairs={{0,7},{1,6},{2,5},{3,4},{4,3},{5,2},{6,1},{7,0},{8,15},{9,14},{10,... | collective-permute-start | bytes 393224 | tf_op jit(solution)/shard_map/ppermute | solution.py:393
  101.8 14.9 %collective-permute-start.6 = (bf16[64,1024]{1,0:T(8,128)(2,1)}, bf16[64,1024]{1,0:T(8,128)(2,1)}, u32[]{:S(2)}, u32[]{:S(2)}) collective-permute-start(bf16[64,1024]{1,0:T(8,128)(2,1)} %get-tuple-element.108), channel_id=1, source_target_pairs={{0,1},{1,0},{2,3},{3,2},{4,5},{5,4},{6,7},{7,6},{8,9},{9,8},{10,11... | collective-permute-start | bytes 393224 | tf_op jit(solution)/shard_map/ppermute | solution.py:393
  101.9 15.8 %collective-permute-start.7 = (bf16[64,1024]{1,0:T(8,128)(2,1)}, bf16[64,1024]{1,0:T(8,128)(2,1)}, u32[]{:S(2)}, u32[]{:S(2)}) collective-permute-start(bf16[64,1024]{1,0:T(8,128)(2,1)} %get-tuple-element.109), channel_id=1, source_target_pairs={{0,2},{1,3},{2,0},{3,1},{4,6},{5,7},{6,4},{7,5},{8,10},{9,11},{10,... | collective-permute-start | bytes 393224 | tf_op jit(solution)/shard_map/ppermute | solution.py:393
  114.1 10.8 %collective-permute-start.8 = (bf16[64,1024]{1,0:T(8,128)(2,1)S(1)}, bf16[64,1024]{1,0:T(8,128)(2,1)S(1)}, u32[]{:S(2)}, u32[]{:S(2)}) collective-permute-start(bf16[64,1024]{1,0:T(8,128)(2,1)S(1)} %copy-done.31), channel_id=1, source_target_pairs={{0,3},{1,2},{2,1},{3,0},{4,7},{5,6},{6,5},{7,4},{8,11},{9,10},{10,... | collective-permute-start | bytes 393224 | tf_op jit(solution)/shard_map/ppermute | solution.py:393
  115.0 10.0 %collective-permute-start.9 = (bf16[64,1024]{1,0:T(8,128)(2,1)S(1)}, bf16[64,1024]{1,0:T(8,128)(2,1)S(1)}, u32[]{:S(2)}, u32[]{:S(2)}) collective-permute-start(bf16[64,1024]{1,0:T(8,128)(2,1)S(1)} %copy-done.30), channel_id=1, source_target_pairs={{0,4},{1,5},{2,6},{3,7},{4,0},{5,1},{6,2},{7,3},{8,12},{9,13},{10,... | collective-permute-start | bytes 393224 | tf_op jit(solution)/shard_map/ppermute | solution.py:393
  115.1 13.5 %collective-permute-start.10 = (bf16[64,1024]{1,0:T(8,128)(2,1)S(1)}, bf16[64,1024]{1,0:T(8,128)(2,1)S(1)}, u32[]{:S(2)}, u32[]{:S(2)}) collective-permute-start(bf16[64,1024]{1,0:T(8,128)(2,1)S(1)} %copy-done.29), channel_id=1, source_target_pairs={{0,5},{1,4},{2,7},{3,6},{4,1},{5,0},{6,3},{7,2},{8,13},{9,12},{10,... | collective-permute-start | bytes 393224 | tf_op jit(solution)/shard_map/ppermute | solution.py:393
  116.6 12.1 %collective-permute-start.11 = (bf16[64,1024]{1,0:T(8,128)(2,1)S(1)}, bf16[64,1024]{1,0:T(8,128)(2,1)S(1)}, u32[]{:S(2)}, u32[]{:S(2)}) collective-permute-start(bf16[64,1024]{1,0:T(8,128)(2,1)S(1)} %copy-done.28), channel_id=1, source_target_pairs={{0,6},{1,7},{2,4},{3,5},{4,2},{5,3},{6,0},{7,1},{8,14},{9,15},{10,... | collective-permute-start | bytes 393224 | tf_op jit(solution)/shard_map/ppermute | solution.py:393
  117.7 11.0 %collective-permute-start.12 = (bf16[64,1024]{1,0:T(8,128)(2,1)S(1)}, bf16[64,1024]{1,0:T(8,128)(2,1)S(1)}, u32[]{:S(2)}, u32[]{:S(2)}) collective-permute-start(bf16[64,1024]{1,0:T(8,128)(2,1)S(1)} %copy-done.27), channel_id=1, source_target_pairs={{0,7},{1,6},{2,5},{3,4},{4,3},{5,2},{6,1},{7,0},{8,15},{9,14},{10,... | collective-permute-start | bytes 393224 | tf_op jit(solution)/shard_map/ppermute | solution.py:393
  133.1 54.8 %all-to-all-start.2 = ((bf16[32,32,1024]{2,1,0:T(8,128)(2,1)}), bf16[32,32,1024]{2,1,0:T(8,128)(2,1)S(1)}, u32[]{:S(2)}, u32[]{:S(2)}) async-start(bf16[32,32,1024]{2,1,0:T(8,128)(2,1)} %bitcast.35), calls=%async_computation.2 | async-start | bytes 4194304 | tf_op jit(solution)/shard_map/all_to_all | solution.py:841
  139.3 48.6 %collective-permute-start.35 = (f32[8,256]{1,0:T(8,128)S(1)}, f32[8,256]{1,0:T(8,128)S(1)}, u32[]{:S(2)}, u32[]{:S(2)}) collective-permute-start(f32[8,256]{1,0:T(8,128)S(1)} %get-tuple-element.198), channel_id=1, source_target_pairs={{0,16},{8,24},{16,0},{24,8},{1,17},{9,25},{17,1},{25,9},{2,18},{10... | collective-permute-start | bytes 24584 | tf_op jit(solution)/shard_map/ppermute | solution.py:389
  141.6 46.3 %collective-permute-start.34 = (f32[8,256]{1,0:T(8,128)S(1)}, f32[8,256]{1,0:T(8,128)S(1)}, u32[]{:S(2)}, u32[]{:S(2)}) collective-permute-start(f32[8,256]{1,0:T(8,128)S(1)} %get-tuple-element.199), channel_id=1, source_target_pairs={{0,8},{8,0},{16,24},{24,16},{1,9},{9,1},{17,25},{25,17},{2,10},{10... | collective-permute-start | bytes 24584 | tf_op jit(solution)/shard_map/ppermute | solution.py:389
  142.9 45.1 %collective-permute-start.36 = (f32[8,256]{1,0:T(8,128)S(1)}, f32[8,256]{1,0:T(8,128)S(1)}, u32[]{:S(2)}, u32[]{:S(2)}) collective-permute-start(f32[8,256]{1,0:T(8,128)S(1)} %bitcast.40), channel_id=1, source_target_pairs={{0,24},{8,16},{16,8},{24,0},{1,25},{9,17},{17,9},{25,1},{2,26},{10... | collective-permute-start | bytes 24584 | tf_op jit(solution)/shard_map/ppermute | solution.py:389
  191.4 17.0 %all-to-all-start.3 = ((bf16[8,16,1024]{2,1,0:T(8,128)(2,1)}), bf16[8,16,1024]{2,1,0:T(8,128)(2,1)S(1)}, u32[]{:S(2)}, u32[]{:S(2)}) async-start(bf16[8,16,1024]{2,1,0:T(8,128)(2,1)} %bitcast.36), calls=%async_computation.3 | async-start | bytes 524288 | tf_op jit(solution)/shard_map/all_to_all | solution.py:841
  196.9 3.8 %collective-permute-start.37 = (f32[8,128]{1,0:T(8,128)S(1)}, f32[8,128]{1,0:T(8,128)S(1)}, u32[]{:S(2)}, u32[]{:S(2)}) collective-permute-start(f32[8,128]{1,0:T(8,128)S(1)} %get-tuple-element.189), channel_id=1, source_target_pairs={{0,1},{1,0},{2,3},{3,2},{4,5},{5,4},{6,7},{7,6},{8,9},{9,8},{10,11... | collective-permute-start | bytes 12296 | tf_op jit(solution)/shard_map/ppermute | solution.py:393
  196.9 6.1 %collective-permute-start.38 = (f32[8,128]{1,0:T(8,128)S(1)}, f32[8,128]{1,0:T(8,128)S(1)}, u32[]{:S(2)}, u32[]{:S(2)}) collective-permute-start(f32[8,128]{1,0:T(8,128)S(1)} %get-tuple-element.190), channel_id=1, source_target_pairs={{0,2},{1,3},{2,0},{3,1},{4,6},{5,7},{6,4},{7,5},{8,10},{9,11},{10,... | collective-permute-start | bytes 12296 | tf_op jit(solution)/shard_map/ppermute | solution.py:393
  198.7 4.8 %collective-permute-start.39 = (f32[8,128]{1,0:T(8,128)S(1)}, f32[8,128]{1,0:T(8,128)S(1)}, u32[]{:S(2)}, u32[]{:S(2)}) collective-permute-start(f32[8,128]{1,0:T(8,128)S(1)} %get-tuple-element.191), channel_id=1, source_target_pairs={{0,3},{1,2},{2,1},{3,0},{4,7},{5,6},{6,5},{7,4},{8,11},{9,10},{10,... | collective-permute-start | bytes 12296 | tf_op jit(solution)/shard_map/ppermute | solution.py:393
  199.1 4.4 %collective-permute-start.40 = (f32[8,128]{1,0:T(8,128)S(1)}, f32[8,128]{1,0:T(8,128)S(1)}, u32[]{:S(2)}, u32[]{:S(2)}) collective-permute-start(f32[8,128]{1,0:T(8,128)S(1)} %get-tuple-element.192), channel_id=1, source_target_pairs={{0,4},{1,5},{2,6},{3,7},{4,0},{5,1},{6,2},{7,3},{8,12},{9,13},{10,... | collective-permute-start | bytes 12296 | tf_op jit(solution)/shard_map/ppermute | solution.py:393
  200.4 3.1 %collective-permute-start.41 = (f32[8,128]{1,0:T(8,128)S(1)}, f32[8,128]{1,0:T(8,128)S(1)}, u32[]{:S(2)}, u32[]{:S(2)}) collective-permute-start(f32[8,128]{1,0:T(8,128)S(1)} %get-tuple-element.193), channel_id=1, source_target_pairs={{0,5},{1,4},{2,7},{3,6},{4,1},{5,0},{6,3},{7,2},{8,13},{9,12},{10,... | collective-permute-start | bytes 12296 | tf_op jit(solution)/shard_map/ppermute | solution.py:393
  200.7 3.4 %collective-permute-start.42 = (f32[8,128]{1,0:T(8,128)S(1)}, f32[8,128]{1,0:T(8,128)S(1)}, u32[]{:S(2)}, u32[]{:S(2)}) collective-permute-start(f32[8,128]{1,0:T(8,128)S(1)} %get-tuple-element.194), channel_id=1, source_target_pairs={{0,6},{1,7},{2,4},{3,5},{4,2},{5,3},{6,0},{7,1},{8,14},{9,15},{10,... | collective-permute-start | bytes 12296 | tf_op jit(solution)/shard_map/ppermute | solution.py:393
  203.1 3.9 %collective-permute-start.43 = (f32[8,128]{1,0:T(8,128)S(1)}, f32[8,128]{1,0:T(8,128)S(1)}, u32[]{:S(2)}, u32[]{:S(2)}) collective-permute-start(f32[8,128]{1,0:T(8,128)S(1)} %get-tuple-element.195), channel_id=1, source_target_pairs={{0,7},{1,6},{2,5},{3,4},{4,3},{5,2},{6,1},{7,0},{8,15},{9,14},{10,... | collective-permute-start | bytes 12296 | tf_op jit(solution)/shard_map/ppermute | solution.py:393
  209.2 14.9 %all-to-all-start.4 = ((bf16[8,16,1024]{2,1,0:T(8,128)(2,1)}), bf16[8,16,1024]{2,1,0:T(8,128)(2,1)S(1)}, u32[]{:S(2)}, u32[]{:S(2)}) async-start(bf16[8,16,1024]{2,1,0:T(8,128)(2,1)} %shard_map.175), calls=%async_computation.4 | async-start | bytes 524288 | tf_op jit(solution)/shard_map/all_to_all | solution.py:841
  (36 other events, 412.2 us)
